TPU v7x, 256 devices: a whole 4x4x8 slice. The times are simulated.
256 devices in a mesh: order: 8 (over z_hi, core), blk: 32 (over y, x, z_lo).
Axes of the slice: x: 4, y: 4, z: 8 (z_hi: 4, z_lo: 2; z = z_hi * 2 + z_lo), core: 2. Of those that a mesh axis runs over, the one named last changes fastest.
Arguments:
- emode_coeffs: bfloat16 [4096, 32, 128], P('blk', 'order'), may hold values from -6 to 6
- lensing_coeffs: bfloat16 [4096, 32, 128], P('blk', 'order'), may hold values from -6 to 6
- order_values: int32 [32], replicated, may hold values from 0 to 4095, as said below
- circle_indices: int32 [4096], replicated, may hold values from 0 to 4095, each once
- circle_weights: float32 [4096], replicated, may hold values from 0.25 to 1
Outputs:
- gradient_part: bfloat16 [4096, 32, 128], P('blk', 'order')
- curl_part: bfloat16 [4096, 32, 128], P('blk', 'order')
Inputs may be any that keep to these rules, and one draw needn't show every extreme that they name: `order_values`: distinct; exactly one value lies in each band from b * 128 to (b + 1) * 128 - 1. `circle_indices`: each circle of the sky exactly once.
All inputs are finite; a program needn't handle non-finite values.
Results may differ from a plain program's by a relative error of at most 0.012.
The roundings to bfloat16 on the way count: a program that leaves them out, or rounds other values in their place, can miss the bound.
Values may be sent and summed in bfloat16 or wider, within the bound.
No kernel may reach another device: no remote copies, remote signals or barrier semaphores. Data moves between devices by JAX's collectives and lax.ppermute only.
A program may use at most 128 MiB of HBM per device.

v0:
```python
import math

import jax
import jax.numpy as jnp
from jax import lax
from jax.sharding import Mesh
from jax.sharding import PartitionSpec as P

LMAX = 4096
ORD_DEV = 4
CIRCLE_DEV = 128
SIMS = 64
LONGS = 256
BLK = ("blk_0", "blk_1", "blk_2")


def sent_together(arrays, axis, dim, along):
    widths = [a.shape[along] for a in arrays]
    both = jnp.concatenate(arrays, axis=along)
    out = lax.all_gather(both, axis, axis=dim, tiled=True)
    return tuple(jnp.split(out, [sum(widths[:k]) for k in range(1, len(widths))], axis=along))


def in_order(pieces, dim):
    pieces = jnp.moveaxis(pieces, 0, dim)
    lengths = pieces.shape
    return pieces.reshape(*lengths[:dim], lengths[dim] * lengths[dim + 1], *lengths[dim + 2 :])


def all_blocks(shard, axes, turns):
    pieces = shard
    for k in turns:
        pieces = lax.all_gather(pieces, axes[k])
    done = turns[::-1]
    back = [done.index(k) for k in range(len(axes))]
    pieces = pieces.transpose(*back, *range(len(axes), pieces.ndim))
    return pieces.reshape(-1, *shard.shape)


def gathered_by_axis(shard, axes, turns, dim):
    return in_order(all_blocks(shard, axes, turns), dim)


def spin_tables(degrees, circle_list, order_list, spin_shift, circle_total):
    frequency = 2 * degrees + 1 + spin_shift
    colatitude = 2 * circle_list + 1
    phases = (
        colatitude[None, :, None] * frequency[None, None, :]
        - 2 * circle_total * order_list[:, None, None]
    )
    phases = jnp.mod(phases, 8 * circle_total)
    angles = phases.astype(jnp.float32) * (math.pi / (4 * circle_total))
    amplitude = math.sqrt(2.0 / LMAX)
    inside = degrees[None, None, :] >= order_list[:, None, None]
    cosine = jnp.where(inside, amplitude * jnp.cos(angles), 0.0)
    weight_deg = (frequency.astype(jnp.float32) / (2.0 * LMAX))[None, None, :]
    slopes = jnp.where(inside, -weight_deg * amplitude * jnp.sin(angles), 0.0)
    return (cosine.astype(jnp.bfloat16), slopes.astype(jnp.bfloat16))


def longitude_table(circle_list, order_list):
    full_circle = 2 * LMAX
    longitude = jnp.arange(LONGS, dtype=jnp.int32)
    parity = jnp.mod(circle_list, 2)
    phase_steps = order_list[None, :, None] * (2 * longitude[None, None, :] + parity[:, None, None])
    phase_steps = jnp.mod(phase_steps, 2 * full_circle)
    angles = phase_steps.astype(jnp.float32) * (math.pi / full_circle)
    scaling = 1.0 / math.sqrt(order_list.shape[0])
    fourier = jnp.concatenate([jnp.cos(angles) * scaling, -jnp.sin(angles) * scaling], axis=1)
    return fourier.astype(jnp.bfloat16)


def rotate(block, factor):
    return jnp.concatenate([-block[..., SIMS:], block[..., :SIMS]], axis=-1) * factor


def block_rows(total_rows, row_limit):
    for candidate in range(min(total_rows, row_limit), 0, -1):
        if total_rows % candidate == 0:
            return candidate
    return 1


def adjoint_terms(plus_table, minus_table, circle_values, csims):
    plus = jnp.einsum("orl,roc->loc", plus_table, circle_values, preferred_element_type=jnp.float32)
    minus = jnp.einsum(
        "orl,roc->loc", minus_table, circle_values, preferred_element_type=jnp.float32
    )
    return jnp.concatenate(
        [plus[..., :csims] + minus[..., csims:], plus[..., csims:] - minus[..., :csims]], axis=-1
    )


def body(emode_coeffs, lensing_coeffs, order_values, circle_indices, circle_weights):
    csims = 2 * SIMS
    circle_total = circle_indices.shape[0]
    order_total = order_values.shape[0]
    degree_local = emode_coeffs.shape[0]
    order_pos = lax.axis_index("order")
    block_pos = lax.axis_index(BLK)
    my_orders = lax.dynamic_slice_in_dim(order_values, order_pos * ORD_DEV, ORD_DEV)
    my_circles = lax.dynamic_slice_in_dim(circle_indices, block_pos * CIRCLE_DEV, CIRCLE_DEV)
    all_degrees = jnp.arange(LMAX, dtype=jnp.int32)
    cos_plus, der_plus = spin_tables(all_degrees, my_circles, my_orders, 2, circle_total)
    cos_minus, der_minus = spin_tables(all_degrees, my_circles, my_orders, -2, circle_total)
    cos_zero, der_zero = spin_tables(all_degrees, my_circles, my_orders, 0, circle_total)
    emode_tabs = jnp.stack([der_plus, der_minus, cos_plus, cos_minus])
    lens_tabs = jnp.stack([der_zero, cos_zero])
    emode_piece, lens_piece = sent_together((emode_coeffs, lensing_coeffs), BLK, 0, 1)
    emode_out = jnp.einsum(
        "torl,loc->rotc", emode_tabs, emode_piece, preferred_element_type=jnp.float32
    )
    lens_out = jnp.einsum(
        "torl,loc->rotc", lens_tabs, lens_piece, preferred_element_type=jnp.float32
    )
    emode_out = emode_out.reshape(CIRCLE_DEV, ORD_DEV, 4 * csims)
    lens_out = lens_out.reshape(CIRCLE_DEV, ORD_DEV, 2 * csims)
    synthesized = jnp.concatenate([emode_out, lens_out], axis=-1)
    factor = (my_orders.astype(jnp.float32) / LMAX)[None, :, None]
    modes = jnp.concatenate(
        [
            synthesized[..., 0:csims],
            synthesized[..., csims : 2 * csims],
            rotate(synthesized[..., 2 * csims : 3 * csims], factor),
            rotate(synthesized[..., 3 * csims : 4 * csims], factor),
            synthesized[..., 4 * csims : 5 * csims],
            rotate(synthesized[..., 5 * csims : 6 * csims], factor),
        ],
        axis=-1,
    ).astype(jnp.bfloat16)
    spread = lax.all_to_all(modes, "order", split_axis=0, concat_axis=1, tiled=True)
    circle_part = spread.shape[0]
    sub_begin = block_pos * CIRCLE_DEV + order_pos * circle_part
    part_circles = lax.dynamic_slice_in_dim(circle_indices, sub_begin, circle_part)
    part_weights = lax.dynamic_slice_in_dim(circle_weights, sub_begin, circle_part)
    fourier = longitude_table(part_circles, order_values)
    arranged = spread.reshape(circle_part, order_total, 6, 2, SIMS).transpose(0, 3, 1, 2, 4)
    arranged = arranged.reshape(circle_part, 2 * order_total, 6 * SIMS)
    pixels = jnp.einsum("knj,knc->kjc", fourier, arranged, preferred_element_type=jnp.float32)
    pixels = pixels.reshape(circle_part, LONGS, 6, SIMS)
    delta_q = pixels[:, :, 4] * pixels[:, :, 0] + pixels[:, :, 5] * pixels[:, :, 2]
    delta_u = pixels[:, :, 4] * pixels[:, :, 1] + pixels[:, :, 5] * pixels[:, :, 3]
    deflected = jnp.concatenate([delta_q, delta_u], axis=-1).astype(jnp.bfloat16)
    analysed = jnp.einsum("knj,kjc->knc", fourier, deflected, preferred_element_type=jnp.float32)
    weighted = (analysed * part_weights[:, None, None]).astype(jnp.bfloat16)
    weighted = weighted.reshape(circle_part, 2, order_total, 2, SIMS).transpose(0, 2, 3, 1, 4)
    weighted = weighted.reshape(circle_part, order_total, 4 * SIMS)
    circle_values = lax.all_to_all(weighted, "order", split_axis=1, concat_axis=0, tiled=True)
    own_degrees = block_pos * degree_local + jnp.arange(degree_local, dtype=jnp.int32)
    initial_sum = jnp.zeros((degree_local, ORD_DEV, 4 * SIMS), jnp.float32)
    running_sum = initial_sum
    circle_piece = gathered_by_axis(circle_values, BLK, (2, 0, 1), 0)
    first_circle = jnp.int32(0)
    piece_rows = circle_piece.shape[0]
    step_rows = block_rows(piece_rows, 512)

    def one_block(partial_sum, block_id):
        begin = block_id * step_rows
        circle_list = lax.dynamic_slice_in_dim(circle_indices, first_circle + begin, step_rows)
        map_rows = lax.dynamic_slice_in_dim(circle_piece, begin, step_rows, 0)
        plus_table, unused_plus = spin_tables(own_degrees, circle_list, my_orders, 2, circle_total)
        minus_table, unused_minus = spin_tables(
            own_degrees, circle_list, my_orders, -2, circle_total
        )
        return (partial_sum + adjoint_terms(plus_table, minus_table, map_rows, csims), None)

    running_sum, unused = lax.scan(
        one_block, running_sum, jnp.arange(piece_rows // step_rows, dtype=jnp.int32)
    )
    return (
        running_sum[..., :csims].astype(jnp.bfloat16),
        running_sum[..., csims:].astype(jnp.bfloat16),
    )


def solution(mesh):
    split = Mesh(
        mesh.devices.reshape(mesh.shape["order"], 4, 4, 2), ("order", "blk_0", "blk_1", "blk_2")
    )
    placed = (P(BLK, "order", None), P(BLK, "order", None), P(), P(), P())
    return jax.shard_map(
        body,
        mesh=split,
        in_specs=placed,
        out_specs=(P(BLK, "order", None), P(BLK, "order", None)),
        check_vma=False,
    )
```

profile of v0, /device:TPU:1, one launch (start us, length us, event | category | flops | bytes accessed | tf_op | source)
XLA Modules:
  0.0 579.1 jit_solution(5243992694850781579)
XLA Ops:
  7.2 1.0 copy.87
  8.2 1.0 copy.88
  12.5 107.8 %select_convert_fusion.1 = (bf16[1,4,128,4096]{3,2,0,1:T(8,128)(2,1)}, bf16[1,4,128,4096]{3,2,0,1:T(8,128)(2,1)}, bf16[1,4,128,4096]{3,2,0,1:T(8,128)(2,1)}, bf1...) fusion(f32[4096]{0:T(1024)S(1)} %get-tuple-element.198, ...), kind=kLoop, calls=%fused_computation.107 | loop fusion | flops 125829120 | bytes 31522832 | tf_op jit(solution)/shard_map/convert_element_type | solution.py:58
  120.3 89.8 %all-gather.6.cloned.1.call-done = bf16[4096,8,128]{0,2,1:T(8,128)(2,1)} async-done(((bf16[128,8,128]{0,2,1:T(8,128)(2,1)}), bf16[4096,8,128]{0,2,1:T(8,128)(2,1)}) %all-gather.6.cloned.1.call-update) | async-done | bytes 8388624 | tf_op jit(solution)/shard_map/all_gather | solution.py:20
  210.1 11.2 %fusion.50 = f32[4,128,4,128]{3,1,2,0:T(8,128)S(1)} fusion(bf16[1,4,128,4096]{3,2,0,1:T(8,128)(2,1)} %get-tuple-element.189, bf16[1,4,128,4096]{3,2,0,1:T(8,128)(2,1)} %get-tuple-element.191, bf16[1,4,128,4096]{3,2,0,1:T(8,128)(2,1)} %get-tuple-element.190, bf16[1,4,128,4096]{3,2,0,1:T(8,128)(2,1)} %get-tuple-element.192, ...), kind=kOutput, calls=%fused_computation.70 | convolution fusion | flops 2214592512 | bytes 22020096 | tf_op jit(solution)/shard_map/torl,loc->rotc/dot_general | solution.py:110
  221.4 4.7 fusion.67
  226.5 0.9 convert_dynamic-update-slice_fusion
  228.5 0.9 fusion.86
  229.4 0.9 fusion.85
  231.0 0.9 fusion.84
  232.0 21.4 %all-to-all-start = ((bf16[128,4,768]{2,1,0:T(4,128)(2,1)}), bf16[128,4,768]{2,1,0:T(4,128)(2,1)S(1)}, u32[]{:S(2)}, u32[]{:S(2)}) async-start(bf16[128,4,768]{2,1,0:T(4,128)(2,1)} %fusion.84), calls=%async_computation | async-start | bytes 1572864 | tf_op jit(solution)/shard_map/all_to_all | solution.py:131
  254.9 2.3 multiply_convert_fusion.1
  257.2 16.6 %all-to-all-done = bf16[128,4,768]{2,1,0:T(4,128)(2,1)S(1)} async-done(((bf16[128,4,768]{2,1,0:T(4,128)(2,1)}), bf16[128,4,768]{2,1,0:T(4,128)(2,1)S(1)}, u32[]{:S(2)}, u32[]{:S(2)}) %all-to-all-start) | async-done | bytes 786464 | tf_op jit(solution)/shard_map/all_to_all | solution.py:131
  274.0 1.8 reshape.519
  275.9 1.9 copy.99
  277.8 1.2 reshape.520
  279.0 1.0 fusion.80
  280.0 2.4 fusion.95
  282.5 1.8 copy.117
  284.3 3.2 copy.118
  287.5 3.1 copy.119
  290.6 3.2 copy.120
  293.8 3.2 copy.121
  297.1 2.0 copy.122
  299.0 5.3 fusion.72
  305.4 0.8 copy.132
  306.7 14.6 %all_to_all.30 = bf16[16,32,256]{2,0,1:T(8,128)(2,1)S(1)} all-to-all(bf16[16,32,256]{2,0,1:T(8,128)(2,1)S(1)} %copy.108), channel_id=1, replica_groups=mesh['order'=8,'blk_0'=4,'blk_1'=4,'blk_2'=2] {'order'}, dimensions={1} | all-to-all | bytes 524288 | tf_op jit(solution)/shard_map/all_to_all | solution.py:148
  321.4 6.6 %all_gather.23 = bf16[2,128,4,256]{3,1,2,0:T(8,128)(2,1)} all-gather(bf16[1,128,4,256]{3,1,2,0:T(8,128)(2,1)S(1)} %bitcast.60), channel_id=1, replica_groups=mesh['order'=8,'blk_0'=4,'blk_1'=4,'blk_2'=2] {'blk_2'}, dimensions={0}, use_global_device_ids=true | all-gather | bytes 786432 | tf_op jit(solution)/shard_map/all_gather | solution.py:33
  328.2 33.4 %all-gather.8.cloned.1.call-done = bf16[8,128,4,256]{3,1,2,0:T(8,128)(2,1)} async-done(((bf16[2,128,4,256]{3,1,2,0:T(8,128)(2,1)}), bf16[8,128,4,256]{3,1,2,0:T(8,128)(2,1)}) %all-gather.8.cloned.1.call-update) | async-done | bytes 2097168 | tf_op jit(solution)/shard_map/all_gather | solution.py:33
  361.7 87.5 %all-gather.10.cloned.1.call-done = bf16[16,2,128,4,256]{4,2,3,1,0:T(8,128)(2,1)} async-done(((bf16[4,2,128,4,256]{4,2,3,1,0:T(8,128)(2,1)}), bf16[16,2,128,4,256]{4,2,3,1,0:T(8,128)(2,1)}) %all-gather.10.cloned.1.call-update) | async-done | bytes 8388624 | tf_op jit(solution)/shard_map/all_gather | solution.py:33
  449.2 7.8 %copy.110 = bf16[4,4,2,128,4,256]{5,3,2,1,0,4:T(8,128)(2,1)} copy(bf16[4,4,2,128,4,256]{5,3,4,2,0,1:T(8,128)(2,1)} %bitcast.55) | data formatting | bytes 16777216 | tf_op jit(solution)/shard_map/transpose | solution.py:36
  457.0 114.5 %while.13 = (s32[]{:T(128)}, f32[128,4,256]{0,2,1:T(8,128)S(1)}, s32[8]{0:T(128)S(1)}, bf16[4096,4,256]{2,0,1:T(8,128)(2,1)}, s32[4]{0:T(128)S(1)}, /*index=5*/s...) while((s32[]{:T(128)}, f32[128,4,256]{0,2,1:T(8,128)S(1)}, ...), condition=%wide.region_1.2_spmd.clone, body=%wide.region_0.1_spmd.clone.sunk | while | flops 278006016 | bytes 7351061 | solution.py:167
  459.1 6.0 %convolution_bitcast_fusion.5 = f32[128,4,256]{0,2,1:T(8,128)S(1)} fusion(bf16[4096,4,256]{2,0,1:T(8,128)(2,1)} %get-tuple-element.280, s32[]{:T(128)S(6)} %select_n.276, s32[4]{0:T(128)S(1)} %broadcast_multiply_fusion.10, s32[512,128]{1,0:T(8,128)S(1)} %get-tuple-element.252, pred[4,128]{1,0:T(4,128)(4,1)S(1)} %broadcast_compare_fusion.2), kind=kOutput, calls=%fused_computation.12.clone.1 | convolution fusion | flops 138674176 | bytes 1835540 | tf_op jit(solution)/shard_map/while/body/eval_jaxpr/orl,roc->loc/dot_general | solution.py:85
  465.1 6.0 %convolution_bitcast_fusion.4 = f32[128,4,256]{0,2,1:T(8,128)S(1)} fusion(bf16[4096,4,256]{2,0,1:T(8,128)(2,1)} %get-tuple-element.280, s32[]{:T(128)S(6)} %select_n.276, s32[512,128]{1,0:T(8,128)S(1)} %get-tuple-element.250, s32[4]{0:T(128)S(1)} %broadcast_multiply_fusion.10, pred[4,128]{1,0:T(4,128)(4,1)S(1)} %broadcast_compare_fusion.2), kind=kOutput, calls=%fused_computation.11.clone.1 | convolution fusion | flops 138674176 | bytes 1835540 | tf_op jit(solution)/shard_map/while/body/eval_jaxpr/orl,roc->loc/dot_general | solution.py:86
  473.4 6.0 %convolution_bitcast_fusion.5 = f32[128,4,256]{0,2,1:T(8,128)S(1)} fusion(bf16[4096,4,256]{2,0,1:T(8,128)(2,1)} %get-tuple-element.280, s32[]{:T(128)S(6)} %select_n.276, s32[4]{0:T(128)S(1)} %broadcast_multiply_fusion.10, s32[512,128]{1,0:T(8,128)S(1)} %get-tuple-element.252, pred[4,128]{1,0:T(4,128)(4,1)S(1)} %broadcast_compare_fusion.2), kind=kOutput, calls=%fused_computation.12.clone.1 | convolution fusion | flops 138674176 | bytes 1835540 | tf_op jit(solution)/shard_map/while/body/eval_jaxpr/orl,roc->loc/dot_general | solution.py:85
  479.4 6.0 %convolution_bitcast_fusion.4 = f32[128,4,256]{0,2,1:T(8,128)S(1)} fusion(bf16[4096,4,256]{2,0,1:T(8,128)(2,1)} %get-tuple-element.280, s32[]{:T(128)S(6)} %select_n.276, s32[512,128]{1,0:T(8,128)S(1)} %get-tuple-element.250, s32[4]{0:T(128)S(1)} %broadcast_multiply_fusion.10, pred[4,128]{1,0:T(4,128)(4,1)S(1)} %broadcast_compare_fusion.2), kind=kOutput, calls=%fused_computation.11.clone.1 | convolution fusion | flops 138674176 | bytes 1835540 | tf_op jit(solution)/shard_map/while/body/eval_jaxpr/orl,roc->loc/dot_general | solution.py:86
  487.7 6.0 %convolution_bitcast_fusion.5 = f32[128,4,256]{0,2,1:T(8,128)S(1)} fusion(bf16[4096,4,256]{2,0,1:T(8,128)(2,1)} %get-tuple-element.280, s32[]{:T(128)S(6)} %select_n.276, s32[4]{0:T(128)S(1)} %broadcast_multiply_fusion.10, s32[512,128]{1,0:T(8,128)S(1)} %get-tuple-element.252, pred[4,128]{1,0:T(4,128)(4,1)S(1)} %broadcast_compare_fusion.2), kind=kOutput, calls=%fused_computation.12.clone.1 | convolution fusion | flops 138674176 | bytes 1835540 | tf_op jit(solution)/shard_map/while/body/eval_jaxpr/orl,roc->loc/dot_general | solution.py:85
  493.7 6.0 %convolution_bitcast_fusion.4 = f32[128,4,256]{0,2,1:T(8,128)S(1)} fusion(bf16[4096,4,256]{2,0,1:T(8,128)(2,1)} %get-tuple-element.280, s32[]{:T(128)S(6)} %select_n.276, s32[512,128]{1,0:T(8,128)S(1)} %get-tuple-element.250, s32[4]{0:T(128)S(1)} %broadcast_multiply_fusion.10, pred[4,128]{1,0:T(4,128)(4,1)S(1)} %broadcast_compare_fusion.2), kind=kOutput, calls=%fused_computation.11.clone.1 | convolution fusion | flops 138674176 | bytes 1835540 | tf_op jit(solution)/shard_map/while/body/eval_jaxpr/orl,roc->loc/dot_general | solution.py:86
  502.0 6.0 %convolution_bitcast_fusion.5 = f32[128,4,256]{0,2,1:T(8,128)S(1)} fusion(bf16[4096,4,256]{2,0,1:T(8,128)(2,1)} %get-tuple-element.280, s32[]{:T(128)S(6)} %select_n.276, s32[4]{0:T(128)S(1)} %broadcast_multiply_fusion.10, s32[512,128]{1,0:T(8,128)S(1)} %get-tuple-element.252, pred[4,128]{1,0:T(4,128)(4,1)S(1)} %broadcast_compare_fusion.2), kind=kOutput, calls=%fused_computation.12.clone.1 | convolution fusion | flops 138674176 | bytes 1835540 | tf_op jit(solution)/shard_map/while/body/eval_jaxpr/orl,roc->loc/dot_general | solution.py:85
  508.0 6.0 %convolution_bitcast_fusion.4 = f32[128,4,256]{0,2,1:T(8,128)S(1)} fusion(bf16[4096,4,256]{2,0,1:T(8,128)(2,1)} %get-tuple-element.280, s32[]{:T(128)S(6)} %select_n.276, s32[512,128]{1,0:T(8,128)S(1)} %get-tuple-element.250, s32[4]{0:T(128)S(1)} %broadcast_multiply_fusion.10, pred[4,128]{1,0:T(4,128)(4,1)S(1)} %broadcast_compare_fusion.2), kind=kOutput, calls=%fused_computation.11.clone.1 | convolution fusion | flops 138674176 | bytes 1835540 | tf_op jit(solution)/shard_map/while/body/eval_jaxpr/orl,roc->loc/dot_general | solution.py:86
  516.4 6.0 %convolution_bitcast_fusion.5 = f32[128,4,256]{0,2,1:T(8,128)S(1)} fusion(bf16[4096,4,256]{2,0,1:T(8,128)(2,1)} %get-tuple-element.280, s32[]{:T(128)S(6)} %select_n.276, s32[4]{0:T(128)S(1)} %broadcast_multiply_fusion.10, s32[512,128]{1,0:T(8,128)S(1)} %get-tuple-element.252, pred[4,128]{1,0:T(4,128)(4,1)S(1)} %broadcast_compare_fusion.2), kind=kOutput, calls=%fused_computation.12.clone.1 | convolution fusion | flops 138674176 | bytes 1835540 | tf_op jit(solution)/shard_map/while/body/eval_jaxpr/orl,roc->loc/dot_general | solution.py:85
  522.3 6.0 %convolution_bitcast_fusion.4 = f32[128,4,256]{0,2,1:T(8,128)S(1)} fusion(bf16[4096,4,256]{2,0,1:T(8,128)(2,1)} %get-tuple-element.280, s32[]{:T(128)S(6)} %select_n.276, s32[512,128]{1,0:T(8,128)S(1)} %get-tuple-element.250, s32[4]{0:T(128)S(1)} %broadcast_multiply_fusion.10, pred[4,128]{1,0:T(4,128)(4,1)S(1)} %broadcast_compare_fusion.2), kind=kOutput, calls=%fused_computation.11.clone.1 | convolution fusion | flops 138674176 | bytes 1835540 | tf_op jit(solution)/shard_map/while/body/eval_jaxpr/orl,roc->loc/dot_general | solution.py:86
  530.7 6.0 %convolution_bitcast_fusion.5 = f32[128,4,256]{0,2,1:T(8,128)S(1)} fusion(bf16[4096,4,256]{2,0,1:T(8,128)(2,1)} %get-tuple-element.280, s32[]{:T(128)S(6)} %select_n.276, s32[4]{0:T(128)S(1)} %broadcast_multiply_fusion.10, s32[512,128]{1,0:T(8,128)S(1)} %get-tuple-element.252, pred[4,128]{1,0:T(4,128)(4,1)S(1)} %broadcast_compare_fusion.2), kind=kOutput, calls=%fused_computation.12.clone.1 | convolution fusion | flops 138674176 | bytes 1835540 | tf_op jit(solution)/shard_map/while/body/eval_jaxpr/orl,roc->loc/dot_general | solution.py:85
  536.7 6.0 %convolution_bitcast_fusion.4 = f32[128,4,256]{0,2,1:T(8,128)S(1)} fusion(bf16[4096,4,256]{2,0,1:T(8,128)(2,1)} %get-tuple-element.280, s32[]{:T(128)S(6)} %select_n.276, s32[512,128]{1,0:T(8,128)S(1)} %get-tuple-element.250, s32[4]{0:T(128)S(1)} %broadcast_multiply_fusion.10, pred[4,128]{1,0:T(4,128)(4,1)S(1)} %broadcast_compare_fusion.2), kind=kOutput, calls=%fused_computation.11.clone.1 | convolution fusion | flops 138674176 | bytes 1835540 | tf_op jit(solution)/shard_map/while/body/eval_jaxpr/orl,roc->loc/dot_general | solution.py:86
  545.0 6.0 %convolution_bitcast_fusion.5 = f32[128,4,256]{0,2,1:T(8,128)S(1)} fusion(bf16[4096,4,256]{2,0,1:T(8,128)(2,1)} %get-tuple-element.280, s32[]{:T(128)S(6)} %select_n.276, s32[4]{0:T(128)S(1)} %broadcast_multiply_fusion.10, s32[512,128]{1,0:T(8,128)S(1)} %get-tuple-element.252, pred[4,128]{1,0:T(4,128)(4,1)S(1)} %broadcast_compare_fusion.2), kind=kOutput, calls=%fused_computation.12.clone.1 | convolution fusion | flops 138674176 | bytes 1835540 | tf_op jit(solution)/shard_map/while/body/eval_jaxpr/orl,roc->loc/dot_general | solution.py:85
  551.0 6.0 %convolution_bitcast_fusion.4 = f32[128,4,256]{0,2,1:T(8,128)S(1)} fusion(bf16[4096,4,256]{2,0,1:T(8,128)(2,1)} %get-tuple-element.280, s32[]{:T(128)S(6)} %select_n.276, s32[512,128]{1,0:T(8,128)S(1)} %get-tuple-element.250, s32[4]{0:T(128)S(1)} %broadcast_multiply_fusion.10, pred[4,128]{1,0:T(4,128)(4,1)S(1)} %broadcast_compare_fusion.2), kind=kOutput, calls=%fused_computation.11.clone.1 | convolution fusion | flops 138674176 | bytes 1835540 | tf_op jit(solution)/shard_map/while/body/eval_jaxpr/orl,roc->loc/dot_general | solution.py:86
  559.3 6.0 %convolution_bitcast_fusion.5 = f32[128,4,256]{0,2,1:T(8,128)S(1)} fusion(bf16[4096,4,256]{2,0,1:T(8,128)(2,1)} %get-tuple-element.280, s32[]{:T(128)S(6)} %select_n.276, s32[4]{0:T(128)S(1)} %broadcast_multiply_fusion.10, s32[512,128]{1,0:T(8,128)S(1)} %get-tuple-element.252, pred[4,128]{1,0:T(4,128)(4,1)S(1)} %broadcast_compare_fusion.2), kind=kOutput, calls=%fused_computation.12.clone.1 | convolution fusion | flops 138674176 | bytes 1835540 | tf_op jit(solution)/shard_map/while/body/eval_jaxpr/orl,roc->loc/dot_general | solution.py:85
  565.3 6.0 %convolution_bitcast_fusion.4 = f32[128,4,256]{0,2,1:T(8,128)S(1)} fusion(bf16[4096,4,256]{2,0,1:T(8,128)(2,1)} %get-tuple-element.280, s32[]{:T(128)S(6)} %select_n.276, s32[512,128]{1,0:T(8,128)S(1)} %get-tuple-element.250, s32[4]{0:T(128)S(1)} %broadcast_multiply_fusion.10, pred[4,128]{1,0:T(4,128)(4,1)S(1)} %broadcast_compare_fusion.2), kind=kOutput, calls=%fused_computation.11.clone.1 | convolution fusion | flops 138674176 | bytes 1835540 | tf_op jit(solution)/shard_map/while/body/eval_jaxpr/orl,roc->loc/dot_general | solution.py:86
  (129 shorter events, 24.1 us)
Async XLA Ops:
  7.2 202.9 %all-gather.6.cloned.1.call-start = ((), (), s32[]{:S(2)}) async-start(), calls=%async_computation.2 | async-start | bytes 8650752 | tf_op jit(solution)/shard_map/all_gather | solution.py:20
  210.1 11.3 %copy-start = (bf16[1,4,128,4096]{3,2,0,1:T(8,128)(2,1)S(1)}, bf16[1,4,128,4096]{3,2,0,1:T(8,128)(2,1)}, u32[]{:S(2)}) copy-start(bf16[1,4,128,4096]{3,2,0,1:T(8,128)(2,1)} %get-tuple-element.173) | copy-start | bytes 12582916
  210.1 11.3 %copy-start.1 = (bf16[1,4,128,4096]{3,2,0,1:T(8,128)(2,1)S(1)}, bf16[1,4,128,4096]{3,2,0,1:T(8,128)(2,1)}, u32[]{:S(2)}) copy-start(bf16[1,4,128,4096]{3,2,0,1:T(8,128)(2,1)} %get-tuple-element.174) | copy-start | bytes 12582916
  226.1 28.8 %copy-start.4 = (s32[32]{0:T(128)S(1)}, s32[32]{0:T(128)}, u32[]{:S(2)}) copy-start(s32[32]{0:T(128)} %param.9) | copy-start | bytes 388
  232.0 41.9 %all-to-all-start = ((bf16[128,4,768]{2,1,0:T(4,128)(2,1)}), bf16[128,4,768]{2,1,0:T(4,128)(2,1)S(1)}, u32[]{:S(2)}, u32[]{:S(2)}) async-start(bf16[128,4,768]{2,1,0:T(4,128)(2,1)} %fusion.84), calls=%async_computation | async-start | bytes 1572864 | tf_op jit(solution)/shard_map/all_to_all | solution.py:131
  253.3 108.4 %all-gather.8.cloned.1.call-start = ((), (), s32[]{:S(2)}) async-start(), calls=%async_computation.3 | async-start | bytes 2621440 | tf_op jit(solution)/shard_map/all_gather | solution.py:33
  257.2 22.8 %copy-start.2 = (bf16[16,32,256]{2,1,0:T(8,128)(2,1)}, bf16[16,32,256]{2,1,0:T(8,128)(2,1)S(1)}, u32[]{:S(2)}) copy-start(bf16[16,32,256]{2,1,0:T(8,128)(2,1)S(1)} %get-tuple-element.188) | copy-start | bytes 786436
  299.0 5.3 copy-start.3
  328.0 121.3 %all-gather.10.cloned.1.call-start = ((), (), s32[]{:S(2)}) async-start(), calls=%async_computation.4 | async-start | bytes 10485760 | tf_op jit(solution)/shard_map/all_gather | solution.py:33
Sparse Core Ops, SparseCore 0:
  10.2 199.8 all-gather.5
  328.1 33.5 all-gather.7
  363.5 85.6 all-gather.9
where the time goes:
time: 580 us; the launch traced here: 579 us
  waiting for transfers between devices  227 us (39%)
  other arithmetic  132 us (23%)
  matrix products  113 us (19%)
  local copies, waits for them, and re-layouts  44.7 us (8%)
  starting transfers between devices  21.7 us (4%)
  blocking collectives  21.2 us (4%)
  between operations  14.1 us (2%)
    all_gather x2, waiting for transfers between devices, all_blocks(): pieces = lax.all_gather(pieces, axes[k])  121 us
    convert_element_type x1, other arithmetic, spin_tables(): return (cosine.astype(jnp.bfloat16), slopes.astype(jnp.bfloat16))  108 us
    all_gather x1, waiting for transfers between devices, sent_together(): out = lax.all_gather(both, axis, axis=dim, tiled=True)  89.8 us
    dot_general x8, matrix products, adjoint_terms(): jnp.einsum('orl,roc->loc', minus_table, circle_values, preferred_element_...  47.9 us
    dot_general x8, matrix products, adjoint_terms(): jnp.einsum('orl,roc->loc', plus_table, circle_values, preferred_element_t...  47.7 us
    unnamed x28, local copies, waits for them, and re-layouts  21.4 us
    all_to_all x1, starting transfers between devices, body(): lax.all_to_all(modes, 'order', split_axis=0, concat_axis=1, tiled=True)  21.4 us
    all_to_all x1, waiting for transfers between devices, body(): lax.all_to_all(modes, 'order', split_axis=0, concat_axis=1, tiled=True)  16.6 us
  transfers between devices with their start and end apart: 4, of which 4 were waited for; matrix products, arithmetic and copies ran while one was open for 20% of the time, Pallas kernels for 0%

commit v1 on v0

v1 whole, which is shorter than its diff:
```python
import math

import jax
import jax.numpy as jnp
import numpy as np
from jax import lax
from jax.experimental import pallas as pl
from jax.experimental.pallas import tpu as pltpu

LMAX = 4096
ORD_DEV = 4
SIMS = 64
LONGS = 256
SPINS = (2, -2, 0)
F32 = jnp.float32
BF16 = jnp.bfloat16


def split_hi_lo(values):
    values = values.astype(np.float32)
    hi = values.astype(jnp.bfloat16)
    lo = (values - hi.astype(np.float32)).astype(jnp.bfloat16)
    return hi, lo


def make_constants():
    a = np.arange(32)
    b = np.arange(128)
    c = np.arange(64)
    e = np.arange(32)
    amp = math.sqrt(2.0 / LMAX)
    first = np.pi * np.outer(2 * e + 1, a) / 64.0
    plain = np.concatenate([np.cos(first), np.sin(first)], axis=0)
    both = np.concatenate([plain, plain * (a / 32.0)[None, :]], axis=0)
    hi, lo = split_hi_lo(both)
    w1 = np.concatenate([hi, lo], axis=1)
    twiddle, w2, wadj = [], [], []
    for s in SPINS:
        f = 2 * b + 1 + s
        t = np.pi * np.outer(2 * e + 1, f) / 16384.0
        twiddle += [amp * np.cos(t), amp * np.sin(t)]
        at_c = np.pi * np.outer(f, c) / 128.0
        at_n = np.pi * np.outer(f, c + 1) / 128.0
        full = np.concatenate(
            [
                np.concatenate([np.cos(at_c), np.cos(at_n)], axis=1),
                np.concatenate([-np.sin(at_c), np.sin(at_n)], axis=1),
            ],
            axis=0,
        )
        w2.append(np.stack(split_hi_lo(full)))
        if s:
            back = np.concatenate([full[:128].T, -full[128:].T], axis=1)
            wadj.append(np.concatenate(split_hi_lo(back), axis=0))
    last = np.concatenate([np.cos(first).T, -np.sin(first).T], axis=1)
    hi, lo = split_hi_lo(last)
    w3 = np.concatenate([hi, hi, lo], axis=1)
    return {
        "w1": w1,
        "tw": np.stack(twiddle).astype(np.float32),
        "w2": np.stack(w2),
        "wadj": np.concatenate(wadj, axis=1),
        "w3": w3,
    }


CONST = make_constants()


def order_phase(m):
    q = jnp.bitwise_and(m, 3)
    pc = jnp.where(q == 0, 1.0, jnp.where(q == 2, -1.0, 0.0)).astype(F32)
    ps = jnp.where(q == 1, 1.0, jnp.where(q == 3, -1.0, 0.0)).astype(F32)
    sign = jnp.where(jnp.bitwise_and(m, 1) == 0, 1.0, -1.0).astype(F32)
    return pc, ps, sign


def half_sign(width, value):
    lane = lax.broadcasted_iota(jnp.int32, (1, width), 1)
    return jnp.where(jnp.bitwise_and(lane, 127) < 64, jnp.float32(1.0), value)


def degree_index():
    return lax.broadcasted_iota(jnp.int32, (32, 128), 0) * 128 + lax.broadcasted_iota(
        jnp.int32, (32, 128), 1
    )


def pack_kernel(e_ref, x_ref, out_ref, src, dst):
    for field, ref in enumerate((e_ref, x_ref)):
        src[...] = ref[...].astype(F32)
        for o in range(ORD_DEV):
            t = src[pl.ds(o, 128, stride=ORD_DEV), :].T
            for ri in range(2):
                for s in range(2):
                    j = o * 8 + field * 4 + ri * 2 + s
                    at = ri * 64 + s * 32
                    dst[pl.ds(j, 32, stride=32), :] = t[at : at + 32, :]
    out_ref[...] = dst[...].astype(BF16)


def unpack_kernel(in_ref, g_ref, c_ref, src, dst):
    src[...] = in_ref[...].astype(F32)
    for part, ref in enumerate((g_ref, c_ref)):
        for o in range(ORD_DEV):
            rows = []
            for ri in range(2):
                for s in range(2):
                    j = o * 8 + part * 4 + ri * 2 + s
                    rows.append(src[pl.ds(j, 32, stride=32), :])
            dst[pl.ds(o, 128, stride=ORD_DEV), :] = jnp.concatenate(rows, axis=0).T
        ref[...] = dst[...].astype(BF16)


def synth_kernel(m_ref, x_ref, w1_ref, tw_ref, w2_ref, out_ref, xs, os):
    xs[...] = x_ref[...].astype(F32)
    degree = degree_index()
    lane = lax.broadcasted_iota(jnp.int32, (1, 128), 1)
    for o in range(ORD_DEV):
        m = m_ref[o]
        inside = degree >= m
        pc, ps, sign = order_phase(m)
        factor = m.astype(F32) * (1.0 / LMAX)
        for field in range(2):
            tiles = []
            for t in range(4):
                j = o * 8 + field * 4 + t
                tile = xs[pl.ds(j, 32, stride=32), :]
                tiles.append(jnp.where(inside, tile, 0.0).astype(BF16))
            rhs = jnp.concatenate(tiles, axis=1)
            rhs = jnp.concatenate([rhs, rhs], axis=0)
            first = jnp.dot(w1_ref[...], rhs, preferred_element_type=F32)
            for k in (0, 1) if field == 0 else (2,):
                ar, ai = tw_ref[2 * k], tw_ref[2 * k + 1]
                tr = ar * pc + ai * ps
                ti = ai * pc - ar * ps
                slope = (2 * lane + 1 + SPINS[k]).astype(F32) * (1.0 / (2 * LMAX))
                rows_c, rows_d = [], []
                for t in range(4):
                    part = first[:, t * 128 : (t + 1) * 128]
                    sr, si = part[0:32], part[32:64]
                    vr = part[64:96] + slope * sr
                    vi = part[96:128] + slope * si
                    rows_c.append(jnp.concatenate([sr * tr - si * ti, sr * ti + si * tr], axis=1))
                    rows_d.append(
                        jnp.concatenate([-(vr * ti + vi * tr), vr * tr - vi * ti], axis=1)
                    )
                lhs = jnp.concatenate(rows_c + rows_d, axis=0)
                hi = lhs.astype(BF16)
                lo = (lhs - hi.astype(F32)).astype(BF16)
                y = (
                    jnp.dot(hi, w2_ref[k, 0], preferred_element_type=F32)
                    + jnp.dot(lo, w2_ref[k, 0], preferred_element_type=F32)
                    + jnp.dot(hi, w2_ref[k, 1], preferred_element_type=F32)
                )
                cos_sum = y[:128] * half_sign(128, sign)
                der_sum = y[128:] * half_sign(128, -sign)
                der_map, cos_map = ((0, 2), (1, 3), (4, 5))[k]
                for ri in range(2):
                    scale = -factor if ri == 0 else factor
                    for s in range(2):
                        t = ri * 2 + s
                        u = (1 - ri) * 2 + s
                        rows = pl.ds(o * 2 + ri, 32, stride=8)
                        os[der_map * 2 + s, rows, :] = der_sum[t * 32 : (t + 1) * 32]
                        os[cos_map * 2 + s, rows, :] = cos_sum[u * 32 : (u + 1) * 32] * scale
    for k in range(12):
        out_ref[:, k * 128 : (k + 1) * 128] = os[k].astype(BF16)


def pixel_kernel(x_ref, ft_ref, f_ref, w_ref, out_ref):
    lane_in = lax.broadcasted_iota(jnp.int32, (1, 12 * 128), 1)
    low_in = jnp.bitwise_and(lane_in, 127) < 64
    lane_out = lax.broadcasted_iota(jnp.int32, (1, 4 * 128), 1)
    low_out = jnp.bitwise_and(lane_out, 127) < 64

    def rows_of(i):
        chunks = [x_ref[g * 32 + i * 8 : g * 32 + i * 8 + 8, :].astype(F32) for g in range(8)]
        return jnp.concatenate(chunks, axis=0)

    for pair in range(2):
        i0, i1 = 2 * pair, 2 * pair + 1
        x0, x1 = rows_of(i0), rows_of(i1)
        results = []
        for parity in range(2):
            if parity == 0:
                x = jnp.where(low_in, x0, x1)
            else:
                x = jnp.where(low_in, x1, x0)
            px = jnp.dot(ft_ref[parity], x.astype(BF16), preferred_element_type=F32)
            qt, ut, qp, up, dt, dp = (px[:, k * 256 : (k + 1) * 256] for k in range(6))
            deflected = jnp.concatenate([dt * qt + dp * qp, dt * ut + dp * up], axis=1)
            results.append(
                jnp.dot(f_ref[parity], deflected.astype(BF16), preferred_element_type=F32)
            )
        even, odd = results
        for i, g in ((i0, jnp.where(low_out, even, odd)), (i1, jnp.where(low_out, odd, even))):
            w = w_ref[i : i + 1, :]
            g = (g * jnp.concatenate([w, w, w, w], axis=1)).astype(BF16)
            for k in range(8):
                out_ref[k * 32 + i * 8 : k * 32 + i * 8 + 8, :] = g[k * 8 : k * 8 + 8]


def adjoint_kernel(m_ref, g_ref, tw_ref, wadj_ref, w3_ref, out_ref, gs, os):
    for t in range(4):
        gs[t] = g_ref[:, t * 128 : (t + 1) * 128].astype(F32)
    degree = degree_index()
    for o in range(ORD_DEV):
        m = m_ref[o]
        inside = degree >= m
        pc, ps, sign = order_phase(m)
        signs = half_sign(128, sign)
        turned = []
        for k in range(2):
            ar, ai = tw_ref[2 * k], tw_ref[2 * k + 1]
            turned.append((ar * pc + ai * ps, ai * pc - ar * ps))
        (pr, pi), (mr, mi) = turned
        rows = []
        for ri in range(2):
            rows += [gs[t, pl.ds(o * 2 + ri, 32, stride=8), :] * signs for t in range(4)]
        lhs = jnp.concatenate(rows, axis=0).astype(BF16)
        lhs = jnp.concatenate([lhs, lhs], axis=1)
        y = jnp.dot(lhs, wadj_ref[...], preferred_element_type=F32)
        for ri in range(2):
            for s in range(2):
                yq = y[(ri * 4 + s) * 32 : (ri * 4 + s) * 32 + 32]
                yu = y[(ri * 4 + 2 + s) * 32 : (ri * 4 + 2 + s) * 32 + 32]
                qr, qi, nr, ni = (yq[:, t * 128 : (t + 1) * 128] for t in range(4))
                ur, ui, vr, vi = (yu[:, t * 128 : (t + 1) * 128] for t in range(4))
                grad_re = pr * qr - pi * qi + mr * vr - mi * vi
                grad_im = pr * qi + pi * qr + mr * vi + mi * vr
                curl_re = pr * ur - pi * ui - mr * nr + mi * ni
                curl_im = pr * ui + pi * ur - mr * ni - mi * nr
                p = jnp.concatenate(
                    [
                        jnp.concatenate([grad_re, curl_re], axis=1),
                        jnp.concatenate([grad_im, curl_im], axis=1),
                    ],
                    axis=0,
                )
                hi = p.astype(BF16)
                lo = (p - hi.astype(F32)).astype(BF16)
                rhs = jnp.concatenate([hi, lo, hi], axis=0)
                r = jnp.dot(w3_ref[...], rhs, preferred_element_type=F32)
                for part in range(2):
                    j = o * 8 + part * 4 + ri * 2 + s
                    value = jnp.where(inside, r[:, part * 128 : part * 128 + 128], 0.0)
                    os[pl.ds(j, 32, stride=32), :] = value
    out_ref[...] = os[...].astype(BF16)


VMEM = pl.BlockSpec(memory_space=pltpu.VMEM)
SMEM = pl.BlockSpec(memory_space=pltpu.SMEM)


def call(kernel, name, inputs, out_shapes, scratch):
    specs = [SMEM if x.ndim == 1 else VMEM for x in inputs]
    single = len(out_shapes) == 1
    out = pl.pallas_call(
        kernel,
        name=name,
        out_shape=[jax.ShapeDtypeStruct(s, BF16) for s in out_shapes],
        in_specs=specs,
        out_specs=[VMEM for s in out_shapes],
        scratch_shapes=[pltpu.VMEM(s, F32) for s in scratch],
        compiler_params=pltpu.CompilerParams(vmem_limit_bytes=48 << 20),
    )(*inputs)
    return out[0] if single else out


def fourier_tables(order_values):
    longitude = jnp.arange(LONGS, dtype=jnp.int32)
    full_circle = 2 * LMAX
    parity = jnp.arange(2, dtype=jnp.int32)
    steps = order_values[None, :, None] * (2 * longitude[None, None, :] + parity[:, None, None])
    steps = jnp.mod(steps, 2 * full_circle)
    angles = steps.astype(F32) * (math.pi / full_circle)
    scaling = 1.0 / math.sqrt(order_values.shape[0])
    f = jnp.stack([jnp.cos(angles) * scaling, -jnp.sin(angles) * scaling], axis=2)
    f = f.astype(BF16).reshape(2, 2 * order_values.shape[0], LONGS)
    return f, f.transpose(0, 2, 1)


def weights_by_circle(circle_indices, circle_weights, order_pos):
    e = order_pos * 4 + jnp.arange(4, dtype=jnp.int32)
    ds = jnp.concatenate([e, 63 - e])
    low = jnp.bitwise_and(circle_indices, 63)
    high = jnp.right_shift(circle_indices, 6)
    picked = jnp.where(low[None, :] == ds[:, None], circle_weights[None, :], 0.0)
    chosen = (high[:, None] == jnp.arange(64, dtype=jnp.int32)[None, :]).astype(F32)
    w = jnp.dot(picked, chosen, precision=lax.Precision.HIGHEST)
    return jnp.concatenate([w[:4], w[4:]], axis=1)


def body(emode_coeffs, lensing_coeffs, order_values, circle_indices, circle_weights):
    order_pos = lax.axis_index("order")
    my_orders = lax.dynamic_slice_in_dim(order_values, order_pos * ORD_DEV, ORD_DEV)
    const = {k: jnp.asarray(v) for k, v in CONST.items()}
    fourier, fourier_t = fourier_tables(order_values)
    weights = weights_by_circle(circle_indices, circle_weights, order_pos)
    sent = call(
        pack_kernel,
        "pack",
        [emode_coeffs.reshape(512, 128), lensing_coeffs.reshape(512, 128)],
        [(1024, 128)],
        [(512, 128), (1024, 128)],
    )
    got = lax.all_to_all(sent.reshape(32, 32, 128), "blk", 0, 0, tiled=True)
    modes = call(
        synth_kernel,
        "synth",
        [my_orders, got.reshape(1024, 128), const["w1"], const["tw"], const["w2"]],
        [(256, 1536)],
        [(1024, 128), (12, 256, 128)],
    )
    spread = lax.all_to_all(modes.reshape(8, 32, 1536), "order", 0, 0, tiled=True)
    weighted = call(
        pixel_kernel,
        "pixel",
        [spread.reshape(256, 1536), fourier_t, fourier, weights],
        [(256, 512)],
        [],
    )
    back = lax.all_to_all(weighted.reshape(8, 32, 512), "order", 0, 0, tiled=True)
    sums = call(
        adjoint_kernel,
        "adjoint",
        [my_orders, back.reshape(256, 512), const["tw"], const["wadj"], const["w3"]],
        [(1024, 128)],
        [(4, 256, 128), (1024, 128)],
    )
    home = lax.all_to_all(sums.reshape(32, 32, 128), "blk", 0, 0, tiled=True)
    grad, curl = call(
        unpack_kernel,
        "unpack",
        [home.reshape(1024, 128)],
        [(512, 128), (512, 128)],
        [(1024, 128), (512, 128)],
    )
    return grad.reshape(128, ORD_DEV, 128), curl.reshape(128, ORD_DEV, 128)


def solution(mesh):
    from jax.sharding import PartitionSpec as P

    placed = (P("blk", "order", None), P("blk", "order", None), P(), P(), P())
    return jax.shard_map(
        body,
        mesh=mesh,
        in_specs=placed,
        out_specs=(P("blk", "order", None), P("blk", "order", None)),
        check_vma=False,
    )
```

time: 580 us -> 89.2 us (0.15)
  waiting for transfers between devices: 227 us -> 27.8 us
  other arithmetic: 132 us -> 0.53 us
  matrix products: 113 us -> 0.98 us
  local copies, waits for them, and re-layouts: 44.7 us -> 2.2 us
  between operations: 14.1 us -> 0.75 us
  Pallas kernels: 0 us -> 10 us
    all_gather x3 -> x0, waiting for transfers between devices: 211 us -> none  [the longest x2 121 us: all_blocks(): pieces = lax.all_gather(pieces, axes[k])]
    dot_general x20 -> x1, matrix products: 113 us -> 0.98 us  [weights_by_circle(): w = jnp.dot(picked, chosen, precision=lax.Precision.HIGHEST)]
    convert_element_type x1 -> x0, other arithmetic: 108 us -> none  [spin_tables(): return (cosine.astype(jnp.bfloat16), slopes.astype(jnp.bfloat16))]
    unnamed x28 -> x20, local copies, waits for them, and re-layouts: 21.4 us -> 1.89 us
    add x45 -> x2, other arithmetic: 14.1 us -> 0.01 us  [the longest x1 0.01 us: weights_by_circle(): e = order_pos * 4 + jnp.arange(4, dtype=jnp.int32)]
    all_to_all x1 -> x2, blocking collectives: 14.6 us -> 26.7 us  [the longest x1 14.2 us: body(): lax.all_to_all(weighted.reshape(8, 32, 512), 'order', 0, 0, tiled=True)]
    all_to_all x1 -> x2, waiting for transfers between devices: 16.6 us -> 27.8 us  [the longest x1 19.3 us: body(): lax.all_to_all(modes.reshape(8, 32, 1536), 'order', 0, 0, tiled=True)]
    pallas_call x0 -> x5, Pallas kernels: none -> 10 us  [call(): pl.pallas_call(kernel, name=name, out_shape=[jax.ShapeDtypeStruct(s, BF16...]
  transfers between devices with their start and end apart: 4 -> 2, of which waited for: 4 -> 2; matrix products, arithmetic and copies ran while one was open for 20% -> 2% of each run, Pallas kernels for 0% -> 0%
where the time goes in v1:
time: 89.2 us; the launch traced here: 87.7 us
  waiting for transfers between devices  27.8 us (31%)
  blocking collectives  26.7 us (30%)
  starting transfers between devices  18.7 us (21%)
  Pallas kernels  10 us (11%)
  local copies, waits for them, and re-layouts  2.2 us (2%)
  matrix products  0.98 us (1%)
    all_to_all x1, waiting for transfers between devices, body(): lax.all_to_all(modes.reshape(8, 32, 1536), 'order', 0, 0, tiled=True)  19.3 us
    all_to_all x1, blocking collectives, body(): lax.all_to_all(weighted.reshape(8, 32, 512), 'order', 0, 0, tiled=True)  14.2 us
    all_to_all x1, blocking collectives, body(): home = lax.all_to_all(sums.reshape(32, 32, 128), 'blk', 0, 0, tiled=True)  12.5 us
    pallas_call x5, Pallas kernels, call(): pl.pallas_call(kernel, name=name, out_shape=[jax.ShapeDtypeStruct(s, BF16...  10 us
    all_to_all x1, starting transfers between devices, body(): lax.all_to_all(modes.reshape(8, 32, 1536), 'order', 0, 0, tiled=True)  9.51 us
    all_to_all x1, starting transfers between devices, body(): got = lax.all_to_all(sent.reshape(32, 32, 128), 'blk', 0, 0, tiled=True)  9.22 us
    all_to_all x1, waiting for transfers between devices, body(): got = lax.all_to_all(sent.reshape(32, 32, 128), 'blk', 0, 0, tiled=True)  8.47 us
    unnamed x20, local copies, waits for them, and re-layouts  1.89 us
  transfers between devices with their start and end apart: 2, of which 2 were waited for; matrix products, arithmetic and copies ran while one was open for 2% of the time, Pallas kernels for 0%

profile of v1, /device:TPU:1, one launch (start us, length us, event | category | flops | bytes accessed | tf_op | source)
XLA Modules:
  0.0 87.7 jit_solution(14104222552173087921)
XLA Ops:
  0.6 0.0 copy-start
  0.6 0.0 copy-start.1
  0.7 0.0 copy-start.3
  0.7 0.9 %copy-done.3 = bf16[128,4,128]{2,1,0:T(4,128)(2,1)S(1)} copy-done((bf16[128,4,128]{2,1,0:T(4,128)(2,1)S(1)}, bf16[128,4,128]{2,1,0:T(4,128)(2,1)}, u32[]{:S(2)}) %copy-start.3) | copy-done | bytes 131096
  1.6 0.0 copy-start.4
  1.6 0.9 %copy-done.4 = bf16[128,4,128]{2,1,0:T(4,128)(2,1)S(1)} copy-done((bf16[128,4,128]{2,1,0:T(4,128)(2,1)S(1)}, bf16[128,4,128]{2,1,0:T(4,128)(2,1)}, u32[]{:S(2)}) %copy-start.4) | copy-done | bytes 131096
  2.5 0.0 copy-start.8
  2.5 0.0 copy-start.5
  2.5 1.1 %pack.1 = bf16[1024,128]{1,0:T(8,128)(2,1)} custom-call(bf16[512,128]{1,0:T(8,128)(2,1)S(1)} %bitcast.20, bf16[512,128]{1,0:T(8,128)(2,1)S(1)} %bitcast.21), custom_call_target="tpu_custom_call" | custom-call | tf_op jit(solution)/shard_map/pack/pallas_call | solution.py:259
  3.6 9.2 %all-to-all-start = ((bf16[32,32,128]{2,1,0:T(8,128)(2,1)}), bf16[32,32,128]{2,1,0:T(8,128)(2,1)S(1)}, u32[]{:S(2)}, u32[]{:S(2)}) async-start(bf16[32,32,128]{2,1,0:T(8,128)(2,1)} %bitcast.2), calls=%async_computation | async-start | bytes 524288 | tf_op jit(solution)/shard_map/all_to_all | solution.py:308
  12.9 0.0 copy-done.8
  12.9 0.1 dynamic_slice.3.m_ref
  12.9 8.5 %all-to-all-done = bf16[32,32,128]{2,1,0:T(8,128)(2,1)S(1)} async-done(((bf16[32,32,128]{2,1,0:T(8,128)(2,1)}), bf16[32,32,128]{2,1,0:T(8,128)(2,1)S(1)}, u32[]{:S(2)}, u32[]{:S(2)}) %all-to-all-start) | async-done | bytes 262176 | tf_op jit(solution)/shard_map/all_to_all | solution.py:308
  21.4 0.0 copy-done
  21.4 0.0 copy-done.1
  21.4 0.0 copy-done.5
  21.4 4.4 %synth.1 = bf16[256,1536]{1,0:T(8,128)(2,1)} custom-call(s32[4]{0:T(128)S(1)} %dynamic_slice.3.m_ref, bf16[1024,128]{1,0:T(8,128)(2,1)S(1)} %bitcast.18, bf16[128,64]{1,0:T(8,128)(2,1)S(1)} %copy-done.5, f32[6,32,128]{2,1,0:T(8,128)S(1)} %copy-done, bf16[3,2,256,128]{3,2,1,0:T(8,128)(2,1)S(1)} %copy-done.1), custom_call_target="tpu_custom_call" | custom-call | tf_op jit(solution)/shard_map/synth/pallas_call | solution.py:259
  25.8 0.0 copy-start.7
  25.9 0.0 copy-start.9
  25.9 9.5 %all-to-all-start.1 = ((bf16[8,32,1536]{2,1,0:T(8,128)(2,1)}), bf16[8,32,1536]{2,1,0:T(8,128)(2,1)S(1)}, u32[]{:S(2)}, u32[]{:S(2)}) async-start(bf16[8,32,1536]{2,1,0:T(8,128)(2,1)} %bitcast.4), calls=%async_computation.1 | async-start | bytes 1572864 | tf_op jit(solution)/shard_map/all_to_all | solution.py:316
  35.4 0.3 multiply_convert_fusion.1
  35.7 0.1 copy.13
  35.8 0.1 copy.14.ft_ref
  36.0 0.1 pad_add_fusion
  36.1 0.0 copy-done.7
  36.1 0.0 copy-done.9
  36.1 1.0 %fusion = f32[8,64]{1,0:T(8,128)S(1)} fusion(s32[4096]{0:T(1024)S(1)} %get-tuple-element.7, f32[4096]{0:T(1024)S(1)} %copy-done.9, s32[4096]{0:T(1024)S(1)} %get-tuple-element.6, s32[8]{0:T(128)S(1)} %pad_add_fusion), kind=kOutput, calls=%fused_computation.1 | convolution fusion | flops 25493504 | bytes 51232 | tf_op jit(solution)/shard_map/dot_general | solution.py:291
  37.1 0.1 pad_maximum_fusion.1.w_ref
  37.1 19.3 %all-to-all-done.1 = bf16[8,32,1536]{2,1,0:T(8,128)(2,1)S(1)} async-done(((bf16[8,32,1536]{2,1,0:T(8,128)(2,1)}), bf16[8,32,1536]{2,1,0:T(8,128)(2,1)S(1)}, u32[]{:S(2)}, u32[]{:S(2)}) %all-to-all-start.1) | async-done | bytes 786464 | tf_op jit(solution)/shard_map/all_to_all | solution.py:316
  56.5 0.0 copy-start.2
  56.5 0.0 copy-start.6
  56.5 1.6 %pixel.1 = bf16[256,512]{1,0:T(8,128)(2,1)S(1)} custom-call(bf16[256,1536]{1,0:T(8,128)(2,1)S(1)} %bitcast.13, bf16[2,256,64]{2,1,0:T(8,128)(2,1)S(1)} %copy.14.ft_ref, bf16[2,64,256]{2,1,0:T(8,128)(2,1)S(1)} %convert_element_type.21.f_ref, f32[4,128]{1,0:T(4,128)S(1)} %pad_maximum_fusion.1.w_ref), custom_call_target="tpu_custom_call" | custom-call | tf_op jit(solution)/shard_map/pixel/pallas_call | solution.py:259
  58.1 14.2 %all_to_all.20 = bf16[8,32,512]{2,1,0:T(8,128)(2,1)S(1)} all-to-all(bf16[8,32,512]{2,1,0:T(8,128)(2,1)S(1)} %bitcast.16), channel_id=1, replica_groups=mesh['order'=8,'blk'=32] {'order'}, dimensions={0} | all-to-all | bytes 524288 | tf_op jit(solution)/shard_map/all_to_all | solution.py:324
  72.3 0.0 copy-done.2
  72.3 0.0 copy-done.6
  72.3 1.9 %adjoint.1 = bf16[1024,128]{1,0:T(8,128)(2,1)S(1)} custom-call(s32[4]{0:T(128)S(1)} %dynamic_slice.3.m_ref, bf16[256,512]{1,0:T(8,128)(2,1)S(1)} %bitcast.14, f32[6,32,128]{2,1,0:T(8,128)S(1)} %copy-done, bf16[256,512]{1,0:T(8,128)(2,1)S(1)} %copy-done.2, bf16[32,192]{1,0:T(8,128)(2,1)S(1)} %copy-done.6), custom_call_target="tpu_custom_call" | custom-call | tf_op jit(solution)/shard_map/adjoint/pallas_call | solution.py:259
  74.2 12.5 %all_to_all.21 = bf16[32,32,128]{2,1,0:T(8,128)(2,1)S(1)} all-to-all(bf16[32,32,128]{2,1,0:T(8,128)(2,1)S(1)} %bitcast.15), channel_id=1, replica_groups=mesh['order'=8,'blk'=32] {'blk'}, dimensions={0} | all-to-all | bytes 524288 | tf_op jit(solution)/shard_map/all_to_all | solution.py:332
  86.7 1.1 %unpack.1 = (bf16[512,128]{1,0:T(8,128)(2,1)}, bf16[512,128]{1,0:T(8,128)(2,1)}) custom-call(bf16[1024,128]{1,0:T(8,128)(2,1)S(1)} %bitcast.17), custom_call_target="tpu_custom_call" | custom-call | tf_op jit(solution)/shard_map/unpack/pallas_call | solution.py:259
  (7 shorter events, 0.1 us)
Async XLA Ops:
  0.6 20.8 %copy-start = (f32[6,32,128]{2,1,0:T(8,128)S(1)}, f32[6,32,128]{2,1,0:T(8,128)}, u32[]{:S(2)}) copy-start(f32[6,32,128]{2,1,0:T(8,128)} %constant.50.clone.tw_ref) | copy-start | bytes 294916
  0.6 20.8 %copy-start.1 = (bf16[3,2,256,128]{3,2,1,0:T(8,128)(2,1)S(1)}, bf16[3,2,256,128]{3,2,1,0:T(8,128)(2,1)}, u32[]{:S(2)}) copy-start(bf16[3,2,256,128]{3,2,1,0:T(8,128)(2,1)} %constant.51.clone.w2_ref) | copy-start | bytes 1179652
  0.7 1.0 %copy-start.3 = (bf16[128,4,128]{2,1,0:T(4,128)(2,1)S(1)}, bf16[128,4,128]{2,1,0:T(4,128)(2,1)}, u32[]{:S(2)}) copy-start(bf16[128,4,128]{2,1,0:T(4,128)(2,1)} %param.10) | copy-start | bytes 393220
  1.6 0.9 %copy-start.4 = (bf16[128,4,128]{2,1,0:T(4,128)(2,1)S(1)}, bf16[128,4,128]{2,1,0:T(4,128)(2,1)}, u32[]{:S(2)}) copy-start(bf16[128,4,128]{2,1,0:T(4,128)(2,1)} %param.11) | copy-start | bytes 393220
  2.5 10.3 %copy-start.8 = (s32[32]{0:T(128)S(1)}, s32[32]{0:T(128)}, u32[]{:S(2)}) copy-start(s32[32]{0:T(128)} %param.12) | copy-start | bytes 388
  2.5 18.9 %copy-start.5 = (bf16[128,64]{1,0:T(8,128)(2,1)S(1)}, bf16[128,64]{1,0:T(8,128)(2,1)}, u32[]{:S(2)}) copy-start(bf16[128,64]{1,0:T(8,128)(2,1)} %constant.49.clone.w1_ref) | copy-start | bytes 49156
  3.6 17.8 %all-to-all-start = ((bf16[32,32,128]{2,1,0:T(8,128)(2,1)}), bf16[32,32,128]{2,1,0:T(8,128)(2,1)S(1)}, u32[]{:S(2)}, u32[]{:S(2)}) async-start(bf16[32,32,128]{2,1,0:T(8,128)(2,1)} %bitcast.2), calls=%async_computation | async-start | bytes 524288 | tf_op jit(solution)/shard_map/all_to_all | solution.py:308
  25.8 10.2 %copy-start.7 = (s32[4096]{0:T(1024)S(1)}, s32[4096]{0:T(1024)}, u32[]{:S(2)}) copy-start(s32[4096]{0:T(1024)} %param.13) | copy-start | bytes 49156
  25.9 10.2 %copy-start.9 = (f32[4096]{0:T(1024)S(1)}, f32[4096]{0:T(1024)}, u32[]{:S(2)}) copy-start(f32[4096]{0:T(1024)} %param.14) | copy-start | bytes 49156
  25.9 30.6 %all-to-all-start.1 = ((bf16[8,32,1536]{2,1,0:T(8,128)(2,1)}), bf16[8,32,1536]{2,1,0:T(8,128)(2,1)S(1)}, u32[]{:S(2)}, u32[]{:S(2)}) async-start(bf16[8,32,1536]{2,1,0:T(8,128)(2,1)} %bitcast.4), calls=%async_computation.1 | async-start | bytes 1572864 | tf_op jit(solution)/shard_map/all_to_all | solution.py:316
  56.5 15.8 %copy-start.2 = (bf16[256,512]{1,0:T(8,128)(2,1)S(1)}, bf16[256,512]{1,0:T(8,128)(2,1)}, u32[]{:S(2)}) copy-start(bf16[256,512]{1,0:T(8,128)(2,1)} %constant.52.clone.wadj_ref) | copy-start | bytes 786436
  56.5 15.8 %copy-start.6 = (bf16[32,192]{1,0:T(8,128)(2,1)S(1)}, bf16[32,192]{1,0:T(8,128)(2,1)}, u32[]{:S(2)}) copy-start(bf16[32,192]{1,0:T(8,128)(2,1)} %constant.53.clone.w3_ref) | copy-start | bytes 36868

commit v2 on v1

v2 whole, which is shorter than its diff:
```python
import math

import jax
import jax.numpy as jnp
import numpy as np
from jax import lax
from jax.experimental import pallas as pl
from jax.experimental.pallas import tpu as pltpu
from jax.sharding import Mesh
from jax.sharding import PartitionSpec as P

LMAX = 4096
ORD_DEV = 4
ORD_ROW = 8
SIMS = 64
LONGS = 256
SPINS = (2, -2, 0)
ALL = ("row", "core", "y", "x", "z")


def quad_position():
    return jnp.where(lax.axis_index("core") == 0, lax.axis_index("y"), lax.axis_index("x"))


def quad_shift(shift):
    pairs = []
    for row, core, y, x, z in np.ndindex(4, 2, 4, 4, 2):
        to = (row, core, (y + shift) % 4, x, z) if core == 0 else (row, core, y, (x + shift) % 4, z)
        dims = (4, 2, 4, 4, 2)
        pairs.append(
            (int(np.ravel_multi_index((row, core, y, x, z), dims)), int(np.ravel_multi_index(to, dims)))
        )
    return pairs


def exchange(blocks, direction):
    return [blocks[0]] + [
        lax.ppermute(blocks[k], ALL, quad_shift(direction * k)) for k in (1, 2, 3)
    ]


def realization_rows(o):
    out = []
    for row in range(4):
        out.append(((row * 64 + o * 8) * 4, 8, 4, row * 16))
        for z in range(2):
            out.append(((row * 64 + 32 + o * 2 + z) * 4, 4, 32, row * 16 + 8 + z * 4))
    return out
F32 = jnp.float32
BF16 = jnp.bfloat16


def split_hi_lo(values):
    values = values.astype(np.float32)
    hi = values.astype(jnp.bfloat16)
    lo = (values - hi.astype(np.float32)).astype(jnp.bfloat16)
    return hi, lo


def make_constants():
    a = np.arange(32)
    b = np.arange(128)
    c = np.arange(64)
    e = np.arange(32)
    amp = math.sqrt(2.0 / LMAX)
    first = np.pi * np.outer(2 * e + 1, a) / 64.0
    plain = np.concatenate([np.cos(first), np.sin(first)], axis=0)
    both = np.concatenate([plain, plain * (a / 32.0)[None, :]], axis=0)
    hi, lo = split_hi_lo(both)
    w1 = np.concatenate([hi, lo], axis=1)
    twiddle, w2, wadj = [], [], []
    for s in SPINS:
        f = 2 * b + 1 + s
        t = np.pi * np.outer(2 * e + 1, f) / 16384.0
        twiddle += [amp * np.cos(t), amp * np.sin(t)]
        at_c = np.pi * np.outer(f, c) / 128.0
        at_n = np.pi * np.outer(f, c + 1) / 128.0
        full = np.concatenate(
            [
                np.concatenate([np.cos(at_c), np.cos(at_n)], axis=1),
                np.concatenate([-np.sin(at_c), np.sin(at_n)], axis=1),
            ],
            axis=0,
        )
        w2.append(np.concatenate(split_hi_lo(full), axis=1))
        if s:
            back = np.concatenate([full[:128].T, -full[128:].T], axis=1)
            wadj.append(np.concatenate(split_hi_lo(back), axis=0))
    last = np.concatenate([np.cos(first).T, -np.sin(first).T], axis=1)
    hi, lo = split_hi_lo(last)
    w3 = np.concatenate([hi, hi, lo], axis=1)
    return {
        "w1": w1,
        "tw": np.stack(twiddle).astype(np.float32),
        "w2": np.stack(w2),
        "wadj": np.concatenate(wadj, axis=1),
        "w3": w3,
    }


CONST = make_constants()


def order_phase(m):
    q = jnp.bitwise_and(m, 3)
    pc = jnp.where(q == 0, 1.0, jnp.where(q == 2, -1.0, 0.0)).astype(F32)
    ps = jnp.where(q == 1, 1.0, jnp.where(q == 3, -1.0, 0.0)).astype(F32)
    sign = jnp.where(jnp.bitwise_and(m, 1) == 0, 1.0, -1.0).astype(F32)
    return pc, ps, sign


def half_sign(width, value):
    lane = lax.broadcasted_iota(jnp.int32, (1, width), 1)
    return jnp.where(jnp.bitwise_and(lane, 127) < 64, jnp.float32(1.0), value)


def degree_index():
    return lax.broadcasted_iota(jnp.int32, (32, 128), 0) * 128 + lax.broadcasted_iota(
        jnp.int32, (32, 128), 1
    )


def fourier_tables(m_ref, t, f_ref):
    row = lax.broadcasted_iota(jnp.int32, (64, LONGS), 0)
    longitude = lax.broadcasted_iota(jnp.int32, (64, LONGS), 1)
    slot = jnp.right_shift(row, 1)
    m = jnp.zeros((64, LONGS), jnp.int32)
    for k in range(32):
        value = m_ref[4 * (k % 8) + jnp.bitwise_and(t - k // 8, 3)]
        m = jnp.where(slot == k, value, m)
    quarter = jnp.bitwise_and(row, 1) * LMAX
    for parity in range(2):
        steps = jnp.bitwise_and(m * (2 * longitude + parity) + quarter, 4 * LMAX - 1)
        angles = steps.astype(F32) * (math.pi / (2 * LMAX))
        f_ref[parity] = (jnp.cos(angles) * (1.0 / math.sqrt(32))).astype(BF16)


def weight_rows(row_pos, ci_ref, cw_ref, w_ref):
    e = lax.broadcasted_iota(jnp.int32, (16, 128), 0)
    ds = jnp.where(e < 8, row_pos * 8 + e, 71 - row_pos * 8 - e)
    cs = lax.broadcasted_iota(jnp.int32, (64, 128), 0)
    picked, chosen = [], []
    for k in range(32):
        circle = ci_ref[k : k + 1, :]
        low = jnp.bitwise_and(circle, 63)
        high = jnp.right_shift(circle, 6)
        chosen.append(jnp.where(high == cs, 1.0, 0.0).astype(BF16))
        w = jnp.where(low == ds, cw_ref[k : k + 1, :], 0.0)
        w_hi = w.astype(BF16)
        rest = w - w_hi.astype(F32)
        w_mid = rest.astype(BF16)
        w_lo = (rest - w_mid.astype(F32)).astype(BF16)
        picked.append(jnp.concatenate([w_hi, w_mid, w_lo], axis=0))
    w = lax.dot_general(
        jnp.concatenate(picked, axis=1),
        jnp.concatenate(chosen, axis=1),
        (((1,), (1,)), ((), ())),
        preferred_element_type=F32,
    )
    w = (w[32:] + w[16:32]) + w[:16]
    w_ref[...] = jnp.concatenate([w[:8], w[8:]], axis=1)


def pack_kernel(e_hbm, x_hbm, ci_hbm, cw_hbm, m_hbm, *refs):
    out_ref, f_ref, w_ref, ex, ci_ref, cw_ref, m_ref, src, dst, sems = refs
    copies = [
        pltpu.make_async_copy(e_hbm, ex.at[0], sems.at[0]),
        pltpu.make_async_copy(x_hbm, ex.at[1], sems.at[1]),
        pltpu.make_async_copy(ci_hbm, ci_ref, sems.at[2]),
        pltpu.make_async_copy(cw_hbm, cw_ref, sems.at[3]),
        pltpu.make_async_copy(m_hbm, m_ref, sems.at[4]),
    ]
    for copy in copies:
        copy.start()
    t = quad_position()
    copies[4].wait()
    fourier_tables(m_ref, t, f_ref)
    copies[2].wait()
    copies[3].wait()
    weight_rows(t, ci_ref, cw_ref, w_ref)
    for field in range(2):
        copies[field].wait()
        src[field] = ex[field].astype(F32)
        for o in range(ORD_DEV):
            tile = src[field, pl.ds(o, 128, stride=ORD_DEV), :].T
            for ri in range(2):
                j = field * 2 + ri
                for at, rows, stride, sim in realization_rows(o):
                    sim += ri * 64
                    dst[pl.ds(at + j, rows, stride=stride), :] = tile[sim : sim + rows, :]
    out_ref[...] = dst[...].astype(BF16)


def unpack_kernel(in_ref, g_ref, c_ref, src, dst):
    src[...] = in_ref[...].astype(F32)
    for part, ref in enumerate((g_ref, c_ref)):
        for o in range(ORD_DEV):
            rows = []
            for ri in range(2):
                j = part * 2 + ri
                for at, n, stride, sim in realization_rows(o):
                    rows.append(src[pl.ds(at + j, n, stride=stride), :])
            dst[part, pl.ds(o, 128, stride=ORD_DEV), :] = jnp.concatenate(rows, axis=0).T
        ref[...] = dst[part].astype(BF16)


def synth_kernel(m_ref, x_ref, w1_ref, tw_ref, w2_ref, *refs):
    out_refs, (xs, lhs_ref, os) = refs[:4], refs[4:]
    t = quad_position()
    xs[...] = x_ref[...].astype(F32)
    degree = degree_index()
    lane = lax.broadcasted_iota(jnp.int32, (1, 128), 1)
    for o in range(ORD_ROW):
        m = m_ref[4 * o + t]
        inside = degree >= m
        pc, ps, sign = order_phase(m)
        for field in range(2):
            tiles = []
            for ri in range(2):
                j = o * 128 + field * 2 + ri
                tile = xs[pl.ds(j, 32, stride=4), :]
                tiles.append(jnp.where(inside, tile, 0.0).astype(BF16))
            rhs = jnp.concatenate(tiles, axis=1)
            rhs = jnp.concatenate([rhs, rhs], axis=0)
            first = jnp.dot(w1_ref[...], rhs, preferred_element_type=F32)
            for k in (0, 1) if field == 0 else (2,):
                ar, ai = tw_ref[2 * k], tw_ref[2 * k + 1]
                tr = ar * pc + ai * ps
                ti = ai * pc - ar * ps
                slope = (2 * lane + 1 + SPINS[k]).astype(F32) * (1.0 / (2 * LMAX))
                for ri in range(2):
                    part = first[:, ri * 128 : (ri + 1) * 128]
                    sr, si = part[0:32], part[32:64]
                    vr = part[64:96] + slope * sr
                    vi = part[96:128] + slope * si
                    rows = (
                        (sr * tr - si * ti, sr * ti + si * tr),
                        (-(vr * ti + vi * tr), vr * tr - vi * ti),
                    )
                    for kind in range(2):
                        row = jnp.concatenate(rows[kind], axis=1)
                        hi = row.astype(BF16)
                        lo = (row - hi.astype(F32)).astype(BF16)
                        at = ((kind * ORD_ROW + o) * 2 + ri) * 32
                        lhs_ref[k, at : at + 32, :] = hi
                        lhs_ref[k, 1024 + at : 1024 + at + 32, :] = lo
    for k in range(3):
        y = jnp.dot(lhs_ref[k], w2_ref[k], preferred_element_type=F32)
        y = (y[1024:, :128] + y[:1024, 128:]) + y[:1024, :128]
        der_map, cos_map = ((0, 2), (1, 3), (4, 5))[k]
        for o in range(ORD_ROW):
            m = m_ref[4 * o + t]
            pc, ps, sign = order_phase(m)
            factor = m.astype(F32) * (1.0 / LMAX)
            for ri in range(2):
                rows = pl.ds(o * 2 + ri, 32, stride=16)
                scale = -factor if ri == 0 else factor
                at = (o * 2 + 1 - ri) * 32
                os[cos_map, rows, :] = y[at : at + 32] * (half_sign(128, sign) * scale)
                at = ((ORD_ROW + o) * 2 + ri) * 32
                os[der_map, rows, :] = y[at : at + 32] * half_sign(128, -sign)
    for shift in range(4):
        rows = pl.ds(jnp.bitwise_and(t + shift, 3) * 128, 128)
        for k in range(6):
            out_refs[shift][:, k * 128 : (k + 1) * 128] = os[k, rows, :].astype(BF16)


def pixel_kernel(*refs):
    x_refs, (f_ref, w_ref), out_refs = refs[:4], refs[4:6], refs[6:]
    low_in = lax.bitwise_and(lax.broadcasted_iota(jnp.int32, (1, 6 * 128), 1), 127) < 64
    low_out = lax.bitwise_and(lax.broadcasted_iota(jnp.int32, (1, 2 * 128), 1), 127) < 64

    def rows_of(i):
        chunks = [x_ref[i * 16 : i * 16 + 16, :] for x_ref in x_refs]
        return jnp.concatenate(chunks, axis=0).astype(F32)

    for pair in range(4):
        i0, i1 = 2 * pair, 2 * pair + 1
        x0, x1 = rows_of(i0), rows_of(i1)
        results = []
        for parity in range(2):
            if parity == 0:
                x = jnp.where(low_in, x0, x1)
            else:
                x = jnp.where(low_in, x1, x0)
            px = lax.dot_general(
                f_ref[parity],
                x.astype(BF16),
                (((0,), (0,)), ((), ())),
                preferred_element_type=F32,
            )
            qt, ut, qp, up, dt, dp = (px[:, k * 128 : (k + 1) * 128] for k in range(6))
            deflected = jnp.concatenate([dt * qt + dp * qp, dt * ut + dp * up], axis=1)
            results.append(
                jnp.dot(f_ref[parity], deflected.astype(BF16), preferred_element_type=F32)
            )
        even, odd = results
        for i, g in ((i0, jnp.where(low_out, even, odd)), (i1, jnp.where(low_out, odd, even))):
            w = w_ref[i : i + 1, :]
            g = (g * jnp.concatenate([w, w], axis=1)).astype(BF16)
            for k in range(4):
                out_refs[k][i * 16 : i * 16 + 16, :] = g[k * 16 : k * 16 + 16]


def adjoint_kernel(m_ref, *refs):
    g_refs, (tw_ref, wadj_ref, w3_ref, out_ref, gs, os) = refs[:4], refs[4:]
    t = quad_position()
    for shift in range(4):
        at = pl.ds(jnp.bitwise_and(t + shift, 3) * 128, 128)
        for k in range(2):
            gs[k, at, :] = g_refs[shift][:, k * 128 : (k + 1) * 128].astype(F32)
    degree = degree_index()
    rows = []
    for o in range(ORD_ROW):
        pc, ps, sign = order_phase(m_ref[4 * o + t])
        signs = half_sign(128, sign)
        for ri in range(2):
            rows += [gs[k, pl.ds(o * 2 + ri, 32, stride=16), :] * signs for k in range(2)]
    lhs = jnp.concatenate(rows, axis=0).astype(BF16)
    lhs = jnp.concatenate([lhs, lhs], axis=1)
    y = jnp.dot(lhs, wadj_ref[...], preferred_element_type=F32)
    for o in range(ORD_ROW):
        m = m_ref[4 * o + t]
        inside = degree >= m
        pc, ps, sign = order_phase(m)
        turned = []
        for k in range(2):
            ar, ai = tw_ref[2 * k], tw_ref[2 * k + 1]
            turned.append((ar * pc + ai * ps, ai * pc - ar * ps))
        (pr, pi), (mr, mi) = turned
        for ri in range(2):
            at = (o * 2 + ri) * 64
            yq, yu = y[at : at + 32], y[at + 32 : at + 64]
            qr, qi, nr, ni = (yq[:, k * 128 : (k + 1) * 128] for k in range(4))
            ur, ui, vr, vi = (yu[:, k * 128 : (k + 1) * 128] for k in range(4))
            grad_re = pr * qr - pi * qi + mr * vr - mi * vi
            grad_im = pr * qi + pi * qr + mr * vi + mi * vr
            curl_re = pr * ur - pi * ui - mr * nr + mi * ni
            curl_im = pr * ui + pi * ur - mr * ni - mi * nr
            p = jnp.concatenate(
                [
                    jnp.concatenate([grad_re, curl_re], axis=1),
                    jnp.concatenate([grad_im, curl_im], axis=1),
                ],
                axis=0,
            )
            hi = p.astype(BF16)
            lo = (p - hi.astype(F32)).astype(BF16)
            rhs = jnp.concatenate([hi, lo, hi], axis=0)
            r = jnp.dot(w3_ref[...], rhs, preferred_element_type=F32)
            for part in range(2):
                value = jnp.where(inside, r[:, part * 128 : part * 128 + 128], 0.0)
                os[pl.ds(o * 128 + part * 2 + ri, 32, stride=4), :] = value
    out_ref[...] = os[...].astype(BF16)


VMEM = pl.BlockSpec(memory_space=pltpu.VMEM)
SMEM = pl.BlockSpec(memory_space=pltpu.SMEM)
HBM = pl.BlockSpec(memory_space=pltpu.HBM)


def call(kernel, name, inputs, outs, scratch, spaces=None):
    specs = spaces or [SMEM if x.ndim == 1 else VMEM for x in inputs]
    single = len(outs) == 1
    out = pl.pallas_call(
        kernel,
        name=name,
        out_shape=[jax.ShapeDtypeStruct(s, d) for s, d in outs],
        in_specs=specs,
        out_specs=[VMEM for o in outs],
        scratch_shapes=scratch,
        compiler_params=pltpu.CompilerParams(vmem_limit_bytes=48 << 20),
    )(*inputs)
    return out[0] if single else out


def in_hbm(x):
    return pltpu.with_memory_space_constraint(x, pltpu.HBM)


def scratch(shape, dtype=F32):
    return pltpu.VMEM(shape, dtype)


def body(emode_coeffs, lensing_coeffs, order_values, circle_indices, circle_weights):
    const = {k: jnp.asarray(v) for k, v in CONST.items()}
    sent, fourier, weights = call(
        pack_kernel,
        "pack",
        [
            in_hbm(emode_coeffs.reshape(512, 128)),
            in_hbm(lensing_coeffs.reshape(512, 128)),
            in_hbm(circle_indices.reshape(32, 128)),
            in_hbm(circle_weights.reshape(32, 128)),
            in_hbm(order_values),
        ],
        [((1024, 128), BF16), ((2, 64, LONGS), BF16), ((8, 128), F32)],
        [
            scratch((2, 512, 128), BF16),
            scratch((32, 128), jnp.int32),
            scratch((32, 128), F32),
            pltpu.SMEM((32,), jnp.int32),
            scratch((2, 512, 128)),
            scratch((1024, 128)),
            pltpu.SemaphoreType.DMA((5,)),
        ],
        [HBM] * 5,
    )
    got = lax.all_to_all(sent.reshape(256, 4, 128), ALL, 0, 0, tiled=True)
    modes = call(
        synth_kernel,
        "synth",
        [order_values, got.reshape(1024, 128), const["w1"], const["tw"], const["w2"]],
        [((128, 768), BF16)] * 4,
        [scratch((1024, 128)), scratch((3, 2048, 256), BF16), scratch((6, 512, 128))],
    )
    weighted = call(
        pixel_kernel,
        "pixel",
        [*exchange(modes, 1), fourier, weights],
        [((128, 256), BF16)] * 4,
        [],
    )
    sums = call(
        adjoint_kernel,
        "adjoint",
        [order_values, *exchange(weighted, -1), const["tw"], const["wadj"], const["w3"]],
        [((1024, 128), BF16)],
        [scratch((2, 512, 128)), scratch((1024, 128))],
    )
    home = lax.all_to_all(sums.reshape(256, 4, 128), ALL, 0, 0, tiled=True)
    grad, curl = call(
        unpack_kernel,
        "unpack",
        [home.reshape(1024, 128)],
        [((512, 128), BF16), ((512, 128), BF16)],
        [scratch((1024, 128)), scratch((2, 512, 128))],
    )
    return grad.reshape(128, ORD_DEV, 128), curl.reshape(128, ORD_DEV, 128)


def solution(mesh):
    split = Mesh(mesh.devices.reshape(4, 2, 4, 4, 2), ALL)
    placed = P(("y", "x", "z"), ("row", "core"), None)
    return jax.shard_map(
        body,
        mesh=split,
        in_specs=(placed, placed, P(), P(), P()),
        out_specs=(placed, placed),
        check_vma=False,
    )
```

time: 89.2 us -> 82.6 us (0.926); the launches traced: 87.7 us -> 82.5 us
  blocking collectives: 26.7 us -> 55.4 us
  waiting for transfers between devices: 27.8 us -> 10.3 us
  starting transfers between devices: 18.7 us -> 5.53 us
  local copies, waits for them, and re-layouts: 2.2 us -> 0.67 us
  matrix products: 0.98 us -> 0 us
    all_to_all x2, blocking collectives: 26.7 us -> 55.4 us  [the longest x1 31.2 us: body(): got = lax.all_to_all(sent.reshape(256, 4, 128), ALL, 0, 0, tiled=True)]
    all_to_all x2 -> x0, waiting for transfers between devices: 27.8 us -> none  [the longest x1 19.3 us: body(): lax.all_to_all(modes.reshape(8, 32, 1536), 'order', 0, 0, tiled=True)]
    all_to_all x2 -> x0, starting transfers between devices: 18.7 us -> none  [the longest x1 9.51 us: body(): lax.all_to_all(modes.reshape(8, 32, 1536), 'order', 0, 0, tiled=True)]
    ppermute x0 -> x6, waiting for transfers between devices: none -> 10.3 us  [exchange(): lax.ppermute(blocks[k], ALL, quad_shift(direction * k))]
    ppermute x0 -> x6, starting transfers between devices: none -> 5.53 us  [exchange(): lax.ppermute(blocks[k], ALL, quad_shift(direction * k))]
    unnamed x20 -> x12, local copies, waits for them, and re-layouts: 1.89 us -> 0.67 us
    dot_general x1 -> x0, matrix products: 0.98 us -> none  [weights_by_circle(): w = jnp.dot(picked, chosen, precision=lax.Precision.HIGHEST)]
  transfers between devices with their start and end apart: 2 -> 6, of which waited for: 2 -> 5; matrix products, arithmetic and copies ran while one was open for 2% -> 0% of each run, Pallas kernels for 0% -> 0%
where the time goes in v2:
time: 82.6 us; the launch traced here: 82.5 us
  blocking collectives  55.4 us (67%)
  waiting for transfers between devices  10.3 us (12%)
  Pallas kernels  9.86 us (12%)
  starting transfers between devices  5.53 us (7%)
    all_to_all x1, blocking collectives, body(): got = lax.all_to_all(sent.reshape(256, 4, 128), ALL, 0, 0, tiled=True)  31.2 us
    all_to_all x1, blocking collectives, body(): home = lax.all_to_all(sums.reshape(256, 4, 128), ALL, 0, 0, tiled=True)  24.3 us
    ppermute x6, waiting for transfers between devices, exchange(): lax.ppermute(blocks[k], ALL, quad_shift(direction * k))  10.3 us
    pallas_call x5, Pallas kernels, call(): pl.pallas_call(kernel, name=name, out_shape=[jax.ShapeDtypeStruct(s, d) f...  9.86 us
    ppermute x6, starting transfers between devices, exchange(): lax.ppermute(blocks[k], ALL, quad_shift(direction * k))  5.53 us
  transfers between devices with their start and end apart: 6, of which 5 were waited for; matrix products, arithmetic and copies ran while one was open for 0% of the time, Pallas kernels for 0%

profile of v2, /device:TPU:1, one launch (start us, length us, event | category | flops | bytes accessed | tf_op | source)
XLA Modules:
  0.0 82.5 jit_solution(2609131454170683597)
XLA Ops:
  0.6 0.0 copy-start
  0.6 2.1 %pack.1 = (bf16[1024,128]{1,0:T(8,128)(2,1)S(1)}, bf16[2,64,256]{2,1,0:T(8,128)(2,1)S(1)}, f32[8,128]{1,0:T(8,128)S(1)}) custom-call(bf16[512,128]{1,0:T(8,128)(2,1)} %bitcast.14, bf16[512,128]{1,0:T(8,128)(2,1)} %bitcast.15, s32[32,128]{1,0:T(8,128)} %bitcast.16, f32[32,128]{1,0:T(8,128)} %bitcast.17, s32[32]{0:T(128)} %m_ref.3), custom_call_target="tpu_custom_call" | custom-call | tf_op jit(solution)/shard_map/pack/pallas_call | solution.py:365
  2.8 0.0 copy-start.1
  2.8 0.0 copy-start.3
  2.8 31.2 %all_to_all.10 = bf16[256,4,128]{2,1,0:T(4,128)(2,1)S(1)} all-to-all(bf16[256,4,128]{2,1,0:T(4,128)(2,1)S(1)} %bitcast.13), channel_id=1, replica_groups=mesh['row'=4,'core'=2,'y'=4,'x'=4,'z'=2] {'row','core','y','x','z'}, dimensions={0} | all-to-all | bytes 524288 | tf_op jit(solution)/shard_map/all_to_all | solution.py:409
  34.0 0.0 copy-start.5
  34.0 0.0 copy-done
  34.0 0.0 copy-done.1
  34.0 0.0 copy-done.3
  34.0 0.6 copy-done.5
  34.6 2.9 %synth.1 = (bf16[128,768]{1,0:T(8,128)(2,1)S(1)}, bf16[128,768]{1,0:T(8,128)(2,1)S(1)}, bf16[128,768]{1,0:T(8,128)(2,1)S(1)}, bf16[128,768]{1,0:T(8,128)(2,1)S(1)}) custom-call(s32[32]{0:T(128)S(1)} %copy-done.5, bf16[1024,128]{1,0:T(8,128)(2,1)S(1)} %bitcast.12, bf16[128,64]{1,0:T(8,128)(2,1)S(1)} %copy-done.3, f32[6,32,128]{2,1,0:T(8,128)S(1)} %copy-done.1, ...), custom_call_target="tpu_custom_call" | custom-call | tf_op jit(solution)/shard_map/synth/pallas_call | solution.py:365
  37.5 0.4 collective-permute-start
  37.9 1.7 %collective-permute-start.1 = (bf16[128,768]{1,0:T(8,128)(2,1)S(1)}, bf16[128,768]{1,0:T(8,128)(2,1)S(1)}, u32[]{:S(2)}, u32[]{:S(2)}) collective-permute-start(bf16[128,768]{1,0:T(8,128)(2,1)S(1)} %get-tuple-element.18), channel_id=1, source_target_pairs={{0,16},{1,17},{2,18},{3,19},{4,20},{5,21},{6,22},{7,23},{8,24},{9,... | collective-permute-start | bytes 589832 | tf_op jit(solution)/shard_map/ppermute | solution.py:38
  39.5 0.9 %collective-permute-start.2 = (bf16[128,768]{1,0:T(8,128)(2,1)S(1)}, bf16[128,768]{1,0:T(8,128)(2,1)S(1)}, u32[]{:S(2)}, u32[]{:S(2)}) collective-permute-start(bf16[128,768]{1,0:T(8,128)(2,1)S(1)} %get-tuple-element.19), channel_id=1, source_target_pairs={{0,24},{1,25},{2,26},{3,27},{4,28},{5,29},{6,30},{7,31},{8,0},{9,1... | collective-permute-start | bytes 589832 | tf_op jit(solution)/shard_map/ppermute | solution.py:38
  40.4 5.3 %collective-permute-done.refs_1_ = bf16[128,768]{1,0:T(8,128)(2,1)S(1)} collective-permute-done((bf16[128,768]{1,0:T(8,128)(2,1)S(1)}, bf16[128,768]{1,0:T(8,128)(2,1)S(1)}, u32[]{:S(2)}, u32[]{:S(2)}) %collective-permute-start) | collective-permute-done | bytes 196640 | tf_op jit(solution)/shard_map/ppermute | solution.py:38
  45.7 0.0 collective-permute-done.1.refs_2_
  45.7 0.6 collective-permute-done.2.refs_3_
  46.4 0.0 copy-start.2
  46.4 0.0 copy-start.4
  46.4 2.4 %pixel.1 = (bf16[128,256]{1,0:T(8,128)(2,1)S(1)}, bf16[128,256]{1,0:T(8,128)(2,1)S(1)}, bf16[128,256]{1,0:T(8,128)(2,1)S(1)}, bf16[128,256]{1,0:T(8,128)(2,1)S(1)}) custom-call(bf16[128,768]{1,0:T(8,128)(2,1)S(1)} %get-tuple-element.16.refs_0_, bf16[128,768]{1,0:T(8,128)(2,1)S(1)} %collective-permute-done.refs_1_, ...), custom_call_target="tpu_custom_call" | custom-call | tf_op jit(solution)/shard_map/pixel/pallas_call | solution.py:365
  48.7 2.0 %collective-permute-start.3 = (bf16[128,256]{1,0:T(8,128)(2,1)S(1)}, bf16[128,256]{1,0:T(8,128)(2,1)S(1)}, u32[]{:S(2)}, u32[]{:S(2)}) collective-permute-start(bf16[128,256]{1,0:T(8,128)(2,1)S(1)} %get-tuple-element.23), channel_id=1, source_target_pairs={{0,24},{1,25},{2,26},{3,27},{4,28},{5,29},{6,30},{7,31},{8,0},{9,1... | collective-permute-start | bytes 196616 | tf_op jit(solution)/shard_map/ppermute | solution.py:38
  50.7 0.0 collective-permute-start.4
  50.7 0.7 collective-permute-start.5
  51.4 0.7 collective-permute-done.3.refs_1_
  52.0 3.4 %collective-permute-done.4.refs_2_ = bf16[128,256]{1,0:T(8,128)(2,1)S(1)} collective-permute-done((bf16[128,256]{1,0:T(8,128)(2,1)S(1)}, bf16[128,256]{1,0:T(8,128)(2,1)S(1)}, u32[]{:S(2)}, u32[]{:S(2)}) %collective-permute-start.4) | collective-permute-done | bytes 65568 | tf_op jit(solution)/shard_map/ppermute | solution.py:38
  55.4 0.3 collective-permute-done.5.refs_3_
  55.7 0.0 copy-done.2
  55.7 0.0 copy-done.4
  55.7 1.5 %adjoint.1 = bf16[1024,128]{1,0:T(8,128)(2,1)S(1)} custom-call(s32[32]{0:T(128)S(1)} %copy-done.5, bf16[128,256]{1,0:T(8,128)(2,1)S(1)} %get-tuple-element.22.refs_0_, bf16[128,256]{1,0:T(8,128)(2,1)S(1)} %collective-permute-done.3.refs_1_, bf16[128,256]{1,0:T(8,128)(2,1)S(1)} %collective-permute-done.4.refs_2_, ...), custom_call_target="tpu_custom_call" | custom-call | tf_op jit(solution)/shard_map/adjoint/pallas_call | solution.py:365
  57.3 24.3 %all_to_all.11 = bf16[256,4,128]{2,1,0:T(4,128)(2,1)S(1)} all-to-all(bf16[256,4,128]{2,1,0:T(4,128)(2,1)S(1)} %bitcast.10), channel_id=1, replica_groups=mesh['row'=4,'core'=2,'y'=4,'x'=4,'z'=2] {'row','core','y','x','z'}, dimensions={0} | all-to-all | bytes 524288 | tf_op jit(solution)/shard_map/all_to_all | solution.py:431
  81.5 1.0 %unpack.1 = (bf16[512,128]{1,0:T(8,128)(2,1)}, bf16[512,128]{1,0:T(8,128)(2,1)}) custom-call(bf16[1024,128]{1,0:T(8,128)(2,1)S(1)} %bitcast.11), custom_call_target="tpu_custom_call" | custom-call | tf_op jit(solution)/shard_map/unpack/pallas_call | solution.py:365
Async XLA Ops:
  0.6 33.4 %copy-start = (bf16[3,256,256]{2,1,0:T(8,128)(2,1)S(1)}, bf16[3,256,256]{2,1,0:T(8,128)(2,1)}, u32[]{:S(2)}) copy-start(bf16[3,256,256]{2,1,0:T(8,128)(2,1)} %constant.12.clone.w2_ref) | copy-start | bytes 1179652
  2.8 31.2 %copy-start.1 = (f32[6,32,128]{2,1,0:T(8,128)S(1)}, f32[6,32,128]{2,1,0:T(8,128)}, u32[]{:S(2)}) copy-start(f32[6,32,128]{2,1,0:T(8,128)} %constant.11.clone.tw_ref.refs_4_) | copy-start | bytes 294916
  2.8 31.2 %copy-start.3 = (bf16[128,64]{1,0:T(8,128)(2,1)S(1)}, bf16[128,64]{1,0:T(8,128)(2,1)}, u32[]{:S(2)}) copy-start(bf16[128,64]{1,0:T(8,128)(2,1)} %constant.10.clone.w1_ref) | copy-start | bytes 49156
  34.0 0.7 copy-start.5
  37.5 8.2 %collective-permute-start = (bf16[128,768]{1,0:T(8,128)(2,1)S(1)}, bf16[128,768]{1,0:T(8,128)(2,1)S(1)}, u32[]{:S(2)}, u32[]{:S(2)}) collective-permute-start(bf16[128,768]{1,0:T(8,128)(2,1)S(1)} %get-tuple-element.17), channel_id=1, source_target_pairs={{0,8},{1,9},{2,10},{3,11},{4,12},{5,13},{6,14},{7,15},{8,16},{9,17... | collective-permute-start | bytes 589832 | tf_op jit(solution)/shard_map/ppermute | solution.py:38
  37.9 7.9 %collective-permute-start.1 = (bf16[128,768]{1,0:T(8,128)(2,1)S(1)}, bf16[128,768]{1,0:T(8,128)(2,1)S(1)}, u32[]{:S(2)}, u32[]{:S(2)}) collective-permute-start(bf16[128,768]{1,0:T(8,128)(2,1)S(1)} %get-tuple-element.18), channel_id=1, source_target_pairs={{0,16},{1,17},{2,18},{3,19},{4,20},{5,21},{6,22},{7,23},{8,24},{9,... | collective-permute-start | bytes 589832 | tf_op jit(solution)/shard_map/ppermute | solution.py:38
  39.5 6.8 %collective-permute-start.2 = (bf16[128,768]{1,0:T(8,128)(2,1)S(1)}, bf16[128,768]{1,0:T(8,128)(2,1)S(1)}, u32[]{:S(2)}, u32[]{:S(2)}) collective-permute-start(bf16[128,768]{1,0:T(8,128)(2,1)S(1)} %get-tuple-element.19), channel_id=1, source_target_pairs={{0,24},{1,25},{2,26},{3,27},{4,28},{5,29},{6,30},{7,31},{8,0},{9,1... | collective-permute-start | bytes 589832 | tf_op jit(solution)/shard_map/ppermute | solution.py:38
  46.4 9.4 %copy-start.2 = (bf16[256,512]{1,0:T(8,128)(2,1)S(1)}, bf16[256,512]{1,0:T(8,128)(2,1)}, u32[]{:S(2)}) copy-start(bf16[256,512]{1,0:T(8,128)(2,1)} %constant.13.clone.refs_5_) | copy-start | bytes 786436
  46.4 9.4 %copy-start.4 = (bf16[32,192]{1,0:T(8,128)(2,1)S(1)}, bf16[32,192]{1,0:T(8,128)(2,1)}, u32[]{:S(2)}) copy-start(bf16[32,192]{1,0:T(8,128)(2,1)} %constant.14.clone.refs_6_) | copy-start | bytes 36868
  48.7 3.3 %collective-permute-start.3 = (bf16[128,256]{1,0:T(8,128)(2,1)S(1)}, bf16[128,256]{1,0:T(8,128)(2,1)S(1)}, u32[]{:S(2)}, u32[]{:S(2)}) collective-permute-start(bf16[128,256]{1,0:T(8,128)(2,1)S(1)} %get-tuple-element.23), channel_id=1, source_target_pairs={{0,24},{1,25},{2,26},{3,27},{4,28},{5,29},{6,30},{7,31},{8,0},{9,1... | collective-permute-start | bytes 196616 | tf_op jit(solution)/shard_map/ppermute | solution.py:38
  50.7 4.7 %collective-permute-start.4 = (bf16[128,256]{1,0:T(8,128)(2,1)S(1)}, bf16[128,256]{1,0:T(8,128)(2,1)S(1)}, u32[]{:S(2)}, u32[]{:S(2)}) collective-permute-start(bf16[128,256]{1,0:T(8,128)(2,1)S(1)} %get-tuple-element.24), channel_id=1, source_target_pairs={{0,16},{1,17},{2,18},{3,19},{4,20},{5,21},{6,22},{7,23},{8,24},{9,... | collective-permute-start | bytes 196616 | tf_op jit(solution)/shard_map/ppermute | solution.py:38
  50.7 5.0 %collective-permute-start.5 = (bf16[128,256]{1,0:T(8,128)(2,1)S(1)}, bf16[128,256]{1,0:T(8,128)(2,1)S(1)}, u32[]{:S(2)}, u32[]{:S(2)}) collective-permute-start(bf16[128,256]{1,0:T(8,128)(2,1)S(1)} %get-tuple-element.25), channel_id=1, source_target_pairs={{0,8},{1,9},{2,10},{3,11},{4,12},{5,13},{6,14},{7,15},{8,16},{9,17... | collective-permute-start | bytes 196616 | tf_op jit(solution)/shard_map/ppermute | solution.py:38

commit v3 on v2

v3 whole, which is shorter than its diff:
```python
import math

import jax
import jax.numpy as jnp
import numpy as np
from jax import lax
from jax.experimental import pallas as pl
from jax.experimental.pallas import tpu as pltpu
from jax.sharding import Mesh
from jax.sharding import PartitionSpec as P

LMAX = 4096
ORD_DEV = 4
ORD_ROW = 16
SIMS = 64
LONGS = 256
SPINS = (2, -2, 0)
ALL = ("row", "core", "y", "x", "z")


CHIPS = ("row", "y", "x", "z")


def place():
    return jnp.right_shift(lax.axis_index("row"), 1), lax.axis_index("core")


def order_slot(o, core):
    return (o // ORD_DEV) * 2 * ORD_DEV + core * ORD_DEV + o % ORD_DEV


def swap_cores(x):
    return lax.ppermute(x, "core", [(0, 1), (1, 0)])


F32 = jnp.float32
BF16 = jnp.bfloat16


def split_hi_lo(values):
    values = values.astype(np.float32)
    hi = values.astype(jnp.bfloat16)
    lo = (values - hi.astype(np.float32)).astype(jnp.bfloat16)
    return hi, lo


def make_constants():
    a = np.arange(32)
    b = np.arange(128)
    c = np.arange(64)
    e = np.arange(32)
    amp = math.sqrt(2.0 / LMAX)
    first = np.pi * np.outer(2 * e + 1, a) / 64.0
    plain = np.concatenate([np.cos(first), np.sin(first)], axis=0)
    both = np.concatenate([plain, plain * (a / 32.0)[None, :]], axis=0)
    hi, lo = split_hi_lo(both)
    w1 = np.concatenate([hi, lo], axis=1).reshape(4, 2, 16, 64)
    w1 = w1.transpose(1, 0, 2, 3).reshape(2, 64, 64)
    twiddle, w2, wadj = [], [], []
    for s in SPINS:
        f = 2 * b + 1 + s
        t = np.pi * np.outer(2 * e + 1, f) / 16384.0
        twiddle += [amp * np.cos(t), amp * np.sin(t)]
        at_c = np.pi * np.outer(f, c) / 128.0
        at_n = np.pi * np.outer(f, c + 1) / 128.0
        full = np.concatenate(
            [
                np.concatenate([np.cos(at_c), np.cos(at_n)], axis=1),
                np.concatenate([-np.sin(at_c), np.sin(at_n)], axis=1),
            ],
            axis=0,
        )
        w2.append(np.concatenate(split_hi_lo(full), axis=1))
        if s:
            back = np.concatenate([full[:128].T, -full[128:].T], axis=1)
            wadj.append(np.concatenate(split_hi_lo(back), axis=0))
    last = np.stack([np.cos(first).T, -np.sin(first).T], axis=1).reshape(32, 2, 2, 16)
    hi, lo = split_hi_lo(last.transpose(2, 0, 1, 3).reshape(2, 32, 32))
    w3 = np.concatenate([hi, hi, lo], axis=2)
    return {
        "w1": w1,
        "tw": np.stack(twiddle).astype(np.float32),
        "w2": np.stack(w2),
        "wadj": np.concatenate(wadj, axis=1),
        "w3": w3,
    }


CONST = make_constants()


def order_phase(m):
    q = jnp.bitwise_and(m, 3)
    pc = jnp.where(q == 0, 1.0, jnp.where(q == 2, -1.0, 0.0)).astype(F32)
    ps = jnp.where(q == 1, 1.0, jnp.where(q == 3, -1.0, 0.0)).astype(F32)
    sign = jnp.where(jnp.bitwise_and(m, 1) == 0, 1.0, -1.0).astype(F32)
    return pc, ps, sign


def half_sign(width, value):
    lane = lax.broadcasted_iota(jnp.int32, (1, width), 1)
    return jnp.where(jnp.bitwise_and(lane, 127) < 64, jnp.float32(1.0), value)


def degree_index():
    return lax.broadcasted_iota(jnp.int32, (32, 128), 0) * 128 + lax.broadcasted_iota(
        jnp.int32, (32, 128), 1
    )


def fourier_tables(m_ref, core, f_ref, ft_ref):
    row = lax.broadcasted_iota(jnp.int32, (64, LONGS), 0)
    longitude = lax.broadcasted_iota(jnp.int32, (64, LONGS), 1)
    slot = jnp.right_shift(row, 1)
    m = jnp.zeros((64, LONGS), jnp.int32)
    for k in range(32):
        value = m_ref[order_slot(k % 16, core if k < 16 else 1 - core)]
        m = jnp.where(slot == k, value, m)
    quarter = jnp.bitwise_and(row, 1) * LMAX
    for parity in range(2):
        steps = jnp.bitwise_and(m * (2 * longitude + parity) + quarter, 4 * LMAX - 1)
        angles = steps.astype(F32) * (math.pi / (2 * LMAX))
        table = jnp.cos(angles) * (1.0 / math.sqrt(32))
        f_ref[parity] = table.astype(BF16)
        ft_ref[parity] = table.T.astype(BF16)


def weight_rows(row_pos, ci_ref, cw_ref, w_ref):
    e = lax.broadcasted_iota(jnp.int32, (16, 128), 0)
    ds = jnp.where(e < 8, row_pos * 8 + e, 71 - row_pos * 8 - e)
    cs = lax.broadcasted_iota(jnp.int32, (64, 128), 0)
    picked, chosen = [], []
    for k in range(32):
        circle = ci_ref[k : k + 1, :]
        low = jnp.bitwise_and(circle, 63)
        high = jnp.right_shift(circle, 6)
        chosen.append(jnp.where(high == cs, 1.0, 0.0).astype(BF16))
        w = jnp.where(low == ds, cw_ref[k : k + 1, :], 0.0)
        w_hi = w.astype(BF16)
        rest = w - w_hi.astype(F32)
        w_mid = rest.astype(BF16)
        w_lo = (rest - w_mid.astype(F32)).astype(BF16)
        picked.append(jnp.concatenate([w_hi, w_mid, w_lo], axis=0))
    w = lax.dot_general(
        jnp.concatenate(picked, axis=1),
        jnp.concatenate(chosen, axis=1),
        (((1,), (1,)), ((), ())),
        preferred_element_type=F32,
    )
    w = (w[32:] + w[16:32]) + w[:16]
    w_ref[...] = jnp.concatenate([w[:8], w[8:]], axis=1)


def table_kernel(m_ref, ci_ref, cw_ref, f_ref, ft_ref, w_ref):
    half, core = place()
    fourier_tables(m_ref, core, f_ref, ft_ref)
    weight_rows(2 * half + core, ci_ref, cw_ref, w_ref)


def pack_kernel(e_hbm, x_hbm, m_hbm, out_ref, m_ref, ex, src, dst, sems):
    copies = [
        pltpu.make_async_copy(e_hbm, ex.at[0], sems.at[0]),
        pltpu.make_async_copy(x_hbm, ex.at[1], sems.at[1]),
        pltpu.make_async_copy(m_hbm, m_ref, sems.at[2]),
    ]
    for copy in copies:
        copy.start()
    for field in range(2):
        copies[field].wait()
        src[field] = ex[field].astype(F32)
        for o in range(ORD_DEV):
            tile = src[field, pl.ds(o, 128, stride=ORD_DEV), :].T
            for ri in range(2):
                j = o * 4 + field * 2 + ri
                dst[pl.ds(j, 64, stride=16), :] = tile[ri * 64 : ri * 64 + 64, :]
    packed = dst[...].astype(BF16)
    out_ref[:1024] = packed
    out_ref[1024:] = packed
    copies[2].wait()


def unpack_kernel(in_ref, g_ref, c_ref, src, dst):
    src[...] = in_ref[:1024].astype(F32) + in_ref[1024:].astype(F32)
    for part, ref in enumerate((g_ref, c_ref)):
        for o in range(ORD_DEV):
            rows = []
            for ri in range(2):
                j = o * 4 + part * 2 + ri
                rows.append(src[pl.ds(j, 64, stride=16), :])
            dst[part, pl.ds(o, 128, stride=ORD_DEV), :] = jnp.concatenate(rows, axis=0).T
        ref[...] = dst[part].astype(BF16)


def synth_kernel(m_ref, x_ref, w1_ref, tw_ref, w2_ref, *refs):
    keep_ref, send_ref, xs, lhs_ref, os = refs
    half, core = place()
    mine = pl.ds(half * 16, 16)
    xs[...] = x_ref[...].astype(F32)
    degree = degree_index()
    lane = lax.broadcasted_iota(jnp.int32, (1, 128), 1)
    for o in range(ORD_ROW):
        m = m_ref[order_slot(o, core)]
        inside = degree >= m
        pc, ps, sign = order_phase(m)
        for field in range(2):
            tiles = []
            for ri in range(2):
                j = (o // 4) * 512 + (o % 4) * 4 + field * 2 + ri
                tile = xs[pl.ds(j, 32, stride=16), :]
                tiles.append(jnp.where(inside, tile, 0.0).astype(BF16))
            rhs = jnp.concatenate(tiles, axis=1)
            rhs = jnp.concatenate([rhs, rhs], axis=0)
            first = jnp.dot(w1_ref[half], rhs, preferred_element_type=F32)
            for k in (0, 1) if field == 0 else (2,):
                ar, ai = tw_ref[2 * k, mine, :], tw_ref[2 * k + 1, mine, :]
                tr = ar * pc + ai * ps
                ti = ai * pc - ar * ps
                slope = (2 * lane + 1 + SPINS[k]).astype(F32) * (1.0 / (2 * LMAX))
                for ri in range(2):
                    part = first[:, ri * 128 : (ri + 1) * 128]
                    sr, si = part[0:16], part[16:32]
                    vr = part[32:48] + slope * sr
                    vi = part[48:64] + slope * si
                    rows = (
                        (sr * tr - si * ti, sr * ti + si * tr),
                        (-(vr * ti + vi * tr), vr * tr - vi * ti),
                    )
                    for kind in range(2):
                        row = jnp.concatenate(rows[kind], axis=1)
                        hi = row.astype(BF16)
                        lo = (row - hi.astype(F32)).astype(BF16)
                        at = ((kind * ORD_ROW + o) * 2 + ri) * 16
                        lhs_ref[k, at : at + 16, :] = hi
                        lhs_ref[k, 1024 + at : 1024 + at + 16, :] = lo
    for k in range(3):
        y = jnp.dot(lhs_ref[k], w2_ref[k], preferred_element_type=F32)
        y = (y[1024:, :128] + y[:1024, 128:]) + y[:1024, :128]
        der_map, cos_map = ((0, 2), (1, 3), (4, 5))[k]
        for o in range(ORD_ROW):
            m = m_ref[order_slot(o, core)]
            pc, ps, sign = order_phase(m)
            factor = m.astype(F32) * (1.0 / LMAX)
            for ri in range(2):
                rows = pl.ds(o * 2 + ri, 16, stride=32)
                scale = -factor if ri == 0 else factor
                at = (o * 2 + 1 - ri) * 16
                os[cos_map, rows, :] = y[at : at + 16] * (half_sign(128, sign) * scale)
                at = ((ORD_ROW + o) * 2 + ri) * 16
                os[der_map, rows, :] = y[at : at + 16] * half_sign(128, -sign)
    for k in range(6):
        lanes = slice(k * 128, (k + 1) * 128)
        send_ref[:, lanes] = os[k, pl.ds((1 - core) * 256, 256), :].astype(BF16)
        keep_ref[:, lanes] = os[k, pl.ds(core * 256, 256), :].astype(BF16)


def pixel_kernel(*refs):
    x_refs, (f_ref, ft_ref, w_ref), out_refs = refs[:2], refs[2:5], refs[5:]
    low_in = lax.bitwise_and(lax.broadcasted_iota(jnp.int32, (1, 6 * 128), 1), 127) < 64
    low_out = lax.bitwise_and(lax.broadcasted_iota(jnp.int32, (1, 2 * 128), 1), 127) < 64

    def rows_of(i):
        chunks = [x_ref[i * 32 : i * 32 + 32, :] for x_ref in x_refs]
        return jnp.concatenate(chunks, axis=0).astype(F32)

    for pair in range(4):
        i0, i1 = 2 * pair, 2 * pair + 1
        x0, x1 = rows_of(i0), rows_of(i1)
        results = []
        for parity in range(2):
            if parity == 0:
                x = jnp.where(low_in, x0, x1)
            else:
                x = jnp.where(low_in, x1, x0)
            px = jnp.dot(ft_ref[parity], x.astype(BF16), preferred_element_type=F32)
            qt, ut, qp, up, dt, dp = (px[:, k * 128 : (k + 1) * 128] for k in range(6))
            deflected = jnp.concatenate([dt * qt + dp * qp, dt * ut + dp * up], axis=1)
            results.append(
                jnp.dot(f_ref[parity], deflected.astype(BF16), preferred_element_type=F32)
            )
        even, odd = results
        for i, g in ((i0, jnp.where(low_out, even, odd)), (i1, jnp.where(low_out, odd, even))):
            w = w_ref[i : i + 1, :]
            g = (g * jnp.concatenate([w, w], axis=1)).astype(BF16)
            for k in range(2):
                out_refs[k][i * 32 : i * 32 + 32, :] = g[k * 32 : k * 32 + 32]


def adjoint_kernel(m_ref, *refs):
    g_refs, (tw_ref, wadj_ref, w3_ref, out_ref, gs, os) = refs[:2], refs[2:]
    half, core = place()
    mine = pl.ds(half * 16, 16)
    for k in range(2):
        lanes = slice(k * 128, (k + 1) * 128)
        gs[k, pl.ds(core * 256, 256), :] = g_refs[0][:, lanes].astype(F32)
        gs[k, pl.ds((1 - core) * 256, 256), :] = g_refs[1][:, lanes].astype(F32)
    degree = degree_index()
    rows = []
    for o in range(ORD_ROW):
        pc, ps, sign = order_phase(m_ref[order_slot(o, core)])
        signs = half_sign(128, sign)
        for ri in range(2):
            rows += [gs[k, pl.ds(o * 2 + ri, 16, stride=32), :] * signs for k in range(2)]
    lhs = jnp.concatenate(rows, axis=0).astype(BF16)
    lhs = jnp.concatenate([lhs, lhs], axis=1)
    y = jnp.dot(lhs, wadj_ref[...], preferred_element_type=F32)
    for o in range(ORD_ROW):
        m = m_ref[order_slot(o, core)]
        inside = degree >= m
        pc, ps, sign = order_phase(m)
        turned = []
        for k in range(2):
            ar, ai = tw_ref[2 * k, mine, :], tw_ref[2 * k + 1, mine, :]
            turned.append((ar * pc + ai * ps, ai * pc - ar * ps))
        (pr, pi), (mr, mi) = turned
        for ri in range(2):
            at = (o * 2 + ri) * 32
            yq, yu = y[at : at + 16], y[at + 16 : at + 32]
            qr, qi, nr, ni = (yq[:, k * 128 : (k + 1) * 128] for k in range(4))
            ur, ui, vr, vi = (yu[:, k * 128 : (k + 1) * 128] for k in range(4))
            grad_re = pr * qr - pi * qi + mr * vr - mi * vi
            grad_im = pr * qi + pi * qr + mr * vi + mi * vr
            curl_re = pr * ur - pi * ui - mr * nr + mi * ni
            curl_im = pr * ui + pi * ur - mr * ni - mi * nr
            p = jnp.concatenate(
                [
                    jnp.concatenate([grad_re, curl_re], axis=1),
                    jnp.concatenate([grad_im, curl_im], axis=1),
                ],
                axis=0,
            )
            hi = p.astype(BF16)
            lo = (p - hi.astype(F32)).astype(BF16)
            rhs = jnp.concatenate([hi, lo, hi], axis=0)
            r = jnp.dot(w3_ref[half], rhs, preferred_element_type=F32)
            for part in range(2):
                value = jnp.where(inside, r[:, part * 128 : part * 128 + 128], 0.0)
                j = (o // 4) * 512 + (o % 4) * 4 + part * 2 + ri
                os[pl.ds(j, 32, stride=16), :] = value
    out_ref[...] = os[...].astype(BF16)


VMEM = pl.BlockSpec(memory_space=pltpu.VMEM)
SMEM = pl.BlockSpec(memory_space=pltpu.SMEM)
HBM = pl.BlockSpec(memory_space=pltpu.HBM)


def call(kernel, name, inputs, outs, scratch, spaces=None):
    specs = spaces or [SMEM if x.ndim == 1 else VMEM for x in inputs]
    single = len(outs) == 1
    out = pl.pallas_call(
        kernel,
        name=name,
        out_shape=[jax.ShapeDtypeStruct(s, d) for s, d in outs],
        in_specs=specs,
        out_specs=[SMEM if len(shape) == 1 else VMEM for shape, dtype in outs],
        scratch_shapes=scratch,
        compiler_params=pltpu.CompilerParams(vmem_limit_bytes=48 << 20),
    )(*inputs)
    return out[0] if single else out


def in_hbm(x):
    return pltpu.with_memory_space_constraint(x, pltpu.HBM)


def scratch(shape, dtype=F32):
    return pltpu.VMEM(shape, dtype)


def body(emode_coeffs, lensing_coeffs, order_values, circle_indices, circle_weights):
    const = {k: jnp.asarray(v) for k, v in CONST.items()}
    sent, orders = call(
        pack_kernel,
        "pack",
        [
            in_hbm(emode_coeffs.reshape(512, 128)),
            in_hbm(lensing_coeffs.reshape(512, 128)),
            in_hbm(order_values),
        ],
        [((2048, 128), BF16), ((32,), jnp.int32)],
        [
            scratch((2, 512, 128), BF16),
            scratch((2, 512, 128)),
            scratch((1024, 128)),
            pltpu.SemaphoreType.DMA((3,)),
        ],
        [HBM] * 3,
    )
    fourier, fourier_t, weights = call(
        table_kernel,
        "tables",
        [orders, circle_indices.reshape(32, 128), circle_weights.reshape(32, 128)],
        [((2, 64, LONGS), BF16), ((2, LONGS, 64), BF16), ((8, 128), F32)],
        [],
    )
    got = lax.all_to_all(sent.reshape(128, 16, 128), CHIPS, 0, 0, tiled=True)
    kept, passed = call(
        synth_kernel,
        "synth",
        [orders, got.reshape(2048, 128), const["w1"], const["tw"], const["w2"]],
        [((256, 768), BF16)] * 2,
        [scratch((2048, 128)), scratch((3, 2048, 256), BF16), scratch((6, 512, 128))],
    )
    held, handed = call(
        pixel_kernel,
        "pixel",
        [kept, swap_cores(passed), fourier, fourier_t, weights],
        [((256, 256), BF16)] * 2,
        [],
    )
    sums = call(
        adjoint_kernel,
        "adjoint",
        [orders, held, swap_cores(handed), const["tw"], const["wadj"], const["w3"]],
        [((2048, 128), BF16)],
        [scratch((2, 512, 128)), scratch((2048, 128))],
    )
    home = lax.all_to_all(sums.reshape(128, 16, 128), CHIPS, 0, 0, tiled=True)
    grad, curl = call(
        unpack_kernel,
        "unpack",
        [home.reshape(2048, 128)],
        [((512, 128), BF16), ((512, 128), BF16)],
        [scratch((1024, 128)), scratch((2, 512, 128))],
    )
    return grad.reshape(128, ORD_DEV, 128), curl.reshape(128, ORD_DEV, 128)


def solution(mesh):
    split = Mesh(mesh.devices.reshape(4, 2, 4, 4, 2), ALL)
    placed = P(("y", "x", "z"), ("row", "core"), None)
    return jax.shard_map(
        body,
        mesh=split,
        in_specs=(placed, placed, P(), P(), P()),
        out_specs=(placed, placed),
        check_vma=False,
    )
```

time: 82.6 us -> 77.9 us (0.943)
  waiting for transfers between devices: 10.3 us -> 1.02 us
  blocking collectives: 55.4 us -> 60.4 us
  Pallas kernels: 9.86 us -> 12.3 us
  starting transfers between devices: 5.53 us -> 3.17 us
    ppermute x6 -> x2, waiting for transfers between devices: 10.3 us -> 1.02 us  [swap_cores(): return lax.ppermute(x, 'core', [(0, 1), (1, 0)])]
    all_to_all x2, blocking collectives: 55.4 us -> 60.4 us  [the longest x1 35.1 us: body(): got = lax.all_to_all(sent.reshape(128, 16, 128), CHIPS, 0, 0, tiled=True)]
    pallas_call x5 -> x6, Pallas kernels: 9.86 us -> 12.3 us  [call(): pl.pallas_call(kernel, name=name, out_shape=[jax.ShapeDtypeStruct(s, d) f...]
    ppermute x6 -> x2, starting transfers between devices: 5.53 us -> 3.17 us  [swap_cores(): return lax.ppermute(x, 'core', [(0, 1), (1, 0)])]
  transfers between devices with their start and end apart: 6 -> 2, of which waited for: 5 -> 1; matrix products, arithmetic and copies ran while one was open for 0% -> 0% of each run, Pallas kernels for 0% -> 2%
where the time goes in v3:
time: 77.9 us; the launch traced here: 77.7 us
  blocking collectives  60.4 us (78%)
  Pallas kernels  12.3 us (16%)
  starting transfers between devices  3.17 us (4%)
  waiting for transfers between devices  1.02 us (1%)
    all_to_all x1, blocking collectives, body(): got = lax.all_to_all(sent.reshape(128, 16, 128), CHIPS, 0, 0, tiled=True)  35.1 us
    all_to_all x1, blocking collectives, body(): home = lax.all_to_all(sums.reshape(128, 16, 128), CHIPS, 0, 0, tiled=True)  25.2 us
    pallas_call x6, Pallas kernels, call(): pl.pallas_call(kernel, name=name, out_shape=[jax.ShapeDtypeStruct(s, d) f...  12.3 us
    ppermute x2, starting transfers between devices, swap_cores(): return lax.ppermute(x, 'core', [(0, 1), (1, 0)])  3.17 us
  transfers between devices with their start and end apart: 2, of which 1 were waited for; matrix products, arithmetic and copies ran while one was open for 0% of the time, Pallas kernels for 2%

profile of v3, /device:TPU:1, one launch (start us, length us, event | category | flops | bytes accessed | tf_op | source)
XLA Modules:
  0.0 77.7 jit_solution(6866106176571258796)
XLA Ops:
  0.6 1.9 %pack.1 = (bf16[2048,128]{1,0:T(8,128)(2,1)S(1)}, s32[32]{0:T(128)S(1)}) custom-call(bf16[512,128]{1,0:T(8,128)(2,1)} %bitcast.16, bf16[512,128]{1,0:T(8,128)(2,1)} %bitcast.17, s32[32]{0:T(128)} %m_hbm.1), custom_call_target="tpu_custom_call" | custom-call | tf_op jit(solution)/shard_map/pack/pallas_call | solution.py:350
  2.5 0.0 copy-start
  2.5 0.0 copy-start.1
  2.6 0.0 copy-start.3
  2.6 35.1 %all_to_all.10 = bf16[128,16,128]{2,1,0:T(8,128)(2,1)S(1)} all-to-all(bf16[128,16,128]{2,1,0:T(8,128)(2,1)S(1)} %bitcast.13), channel_id=1, replica_groups=mesh['row'=4,'core'=2,'y'=4,'x'=4,'z'=2] {'row','y','x','z'}, dimensions={0} | all-to-all | bytes 1048576 | tf_op jit(solution)/shard_map/all_to_all | solution.py:396
  37.7 0.0 copy-done
  37.7 0.0 copy-done.1
  37.7 0.0 copy-done.3
  37.7 0.0 copy-start.5
  37.7 0.0 copy-start.6
  37.7 3.9 %synth.1 = (bf16[256,768]{1,0:T(8,128)(2,1)S(1)}, bf16[256,768]{1,0:T(8,128)(2,1)S(1)}) custom-call(s32[32]{0:T(128)S(1)} %get-tuple-element.13.m_ref, bf16[2048,128]{1,0:T(8,128)(2,1)S(1)} %bitcast.10, bf16[2,64,64]{2,1,0:T(8,128)(2,1)S(1)} %copy-done.3, f32[6,32,128]{2,1,0:T(8,128)S(1)} %copy-done.1, bf16[3,256,256]{2,1,0:T(8,128)(2,1)S(1)} %copy-done), custom_call_target="tpu_custom_call" | custom-call | tf_op jit(solution)/shard_map/synth/pallas_call | solution.py:350
  41.6 2.8 %collective-permute-start = (bf16[256,768]{1,0:T(8,128)(2,1)S(1)}, bf16[256,768]{1,0:T(8,128)(2,1)S(1)}, u32[]{:S(2)}, u32[]{:S(2)}) collective-permute-start(bf16[256,768]{1,0:T(8,128)(2,1)S(1)} %get-tuple-element.16), channel_id=1, source_target_pairs={{0,32},{32,0},{1,33},{33,1},{2,34},{34,2},{3,35},{35,3},{4,36},{36... | collective-permute-start | bytes 1179656 | tf_op jit(solution)/shard_map/ppermute | solution.py:33
  44.4 0.0 copy-done.5
  44.4 0.0 copy-done.6
  44.4 1.4 %tables.1 = (bf16[2,64,256]{2,1,0:T(8,128)(2,1)S(1)}, bf16[2,256,64]{2,1,0:T(8,128)(2,1)S(1)}, f32[8,128]{1,0:T(8,128)S(1)}) custom-call(s32[32]{0:T(128)S(1)} %get-tuple-element.13.m_ref, s32[32,128]{1,0:T(8,128)S(1)} %bitcast.14, f32[32,128]{1,0:T(8,128)S(1)} %bitcast.15), custom_call_target="tpu_custom_call" | custom-call | tf_op jit(solution)/shard_map/tables/pallas_call | solution.py:350
  45.8 0.0 collective-permute-done.refs_1_
  45.8 0.0 copy-start.2
  45.8 0.0 copy-start.4
  45.8 2.4 %pixel.1 = (bf16[256,256]{1,0:T(8,128)(2,1)S(1)}, bf16[256,256]{1,0:T(8,128)(2,1)S(1)}) custom-call(bf16[256,768]{1,0:T(8,128)(2,1)S(1)} %get-tuple-element.15.refs_0_, bf16[256,768]{1,0:T(8,128)(2,1)S(1)} %collective-permute-done.refs_1_, bf16[2,64,256]{2,1,0:T(8,128)(2,1)S(1)} %get-tuple-element.17.refs_2_, ...), custom_call_target="tpu_custom_call" | custom-call | tf_op jit(solution)/shard_map/pixel/pallas_call | solution.py:350
  48.2 0.4 collective-permute-start.1
  48.6 1.0 %collective-permute-done.1.refs_1_ = bf16[256,256]{1,0:T(8,128)(2,1)S(1)} collective-permute-done((bf16[256,256]{1,0:T(8,128)(2,1)S(1)}, bf16[256,256]{1,0:T(8,128)(2,1)S(1)}, u32[]{:S(2)}, u32[]{:S(2)}) %collective-permute-start.1) | collective-permute-done | bytes 131104 | tf_op jit(solution)/shard_map/ppermute | solution.py:33
  49.6 0.0 copy-done.2
  49.7 0.0 copy-done.4
  49.7 1.8 %adjoint.1 = bf16[2048,128]{1,0:T(8,128)(2,1)S(1)} custom-call(s32[32]{0:T(128)S(1)} %get-tuple-element.13.m_ref, bf16[256,256]{1,0:T(8,128)(2,1)S(1)} %get-tuple-element.20.refs_0_, bf16[256,256]{1,0:T(8,128)(2,1)S(1)} %collective-permute-done.1.refs_1_, f32[6,32,128]{2,1,0:T(8,128)S(1)} %copy-done.1, bf16[256,512]{1,0:T(8,128)(2,1)S(1)} %copy-done.2, ...), custom_call_target="tpu_custom_call" | custom-call | tf_op jit(solution)/shard_map/adjoint/pallas_call | solution.py:350
  51.5 25.2 %all_to_all.11 = bf16[128,16,128]{2,1,0:T(8,128)(2,1)S(1)} all-to-all(bf16[128,16,128]{2,1,0:T(8,128)(2,1)S(1)} %bitcast.11), channel_id=1, replica_groups=mesh['row'=4,'core'=2,'y'=4,'x'=4,'z'=2] {'row','y','x','z'}, dimensions={0} | all-to-all | bytes 1048576 | tf_op jit(solution)/shard_map/all_to_all | solution.py:418
  76.7 1.0 %unpack.1 = (bf16[512,128]{1,0:T(8,128)(2,1)}, bf16[512,128]{1,0:T(8,128)(2,1)}) custom-call(bf16[2048,128]{1,0:T(8,128)(2,1)S(1)} %bitcast.12), custom_call_target="tpu_custom_call" | custom-call | tf_op jit(solution)/shard_map/unpack/pallas_call | solution.py:350
Async XLA Ops:
  2.5 35.2 %copy-start = (bf16[3,256,256]{2,1,0:T(8,128)(2,1)S(1)}, bf16[3,256,256]{2,1,0:T(8,128)(2,1)}, u32[]{:S(2)}) copy-start(bf16[3,256,256]{2,1,0:T(8,128)(2,1)} %constant.12.clone.w2_ref) | copy-start | bytes 1179652
  2.5 35.2 %copy-start.1 = (f32[6,32,128]{2,1,0:T(8,128)S(1)}, f32[6,32,128]{2,1,0:T(8,128)}, u32[]{:S(2)}) copy-start(f32[6,32,128]{2,1,0:T(8,128)} %constant.11.clone.tw_ref.refs_2_) | copy-start | bytes 294916
  2.6 35.2 %copy-start.3 = (bf16[2,64,64]{2,1,0:T(8,128)(2,1)S(1)}, bf16[2,64,64]{2,1,0:T(8,128)(2,1)}, u32[]{:S(2)}) copy-start(bf16[2,64,64]{2,1,0:T(8,128)(2,1)} %constant.10.clone.w1_ref) | copy-start | bytes 49156
  37.7 6.7 %copy-start.5 = (s32[4096]{0:T(1024)S(1)}, s32[4096]{0:T(1024)}, u32[]{:S(2)}) copy-start(s32[4096]{0:T(1024)} %param.13) | copy-start | bytes 49156
  37.7 6.7 %copy-start.6 = (f32[4096]{0:T(1024)S(1)}, f32[4096]{0:T(1024)}, u32[]{:S(2)}) copy-start(f32[4096]{0:T(1024)} %param.14) | copy-start | bytes 49156
  41.6 4.1 %collective-permute-start = (bf16[256,768]{1,0:T(8,128)(2,1)S(1)}, bf16[256,768]{1,0:T(8,128)(2,1)S(1)}, u32[]{:S(2)}, u32[]{:S(2)}) collective-permute-start(bf16[256,768]{1,0:T(8,128)(2,1)S(1)} %get-tuple-element.16), channel_id=1, source_target_pairs={{0,32},{32,0},{1,33},{33,1},{2,34},{34,2},{3,35},{35,3},{4,36},{36... | collective-permute-start | bytes 1179656 | tf_op jit(solution)/shard_map/ppermute | solution.py:33
  45.8 3.9 %copy-start.2 = (bf16[256,512]{1,0:T(8,128)(2,1)S(1)}, bf16[256,512]{1,0:T(8,128)(2,1)}, u32[]{:S(2)}) copy-start(bf16[256,512]{1,0:T(8,128)(2,1)} %constant.13.clone.refs_3_) | copy-start | bytes 786436
  45.8 3.9 %copy-start.4 = (bf16[2,32,96]{2,1,0:T(8,128)(2,1)S(1)}, bf16[2,32,96]{2,1,0:T(8,128)(2,1)}, u32[]{:S(2)}) copy-start(bf16[2,32,96]{2,1,0:T(8,128)(2,1)} %constant.14.clone.refs_4_) | copy-start | bytes 36868
  48.2 1.4 %collective-permute-start.1 = (bf16[256,256]{1,0:T(8,128)(2,1)S(1)}, bf16[256,256]{1,0:T(8,128)(2,1)S(1)}, u32[]{:S(2)}, u32[]{:S(2)}) collective-permute-start(bf16[256,256]{1,0:T(8,128)(2,1)S(1)} %get-tuple-element.21), channel_id=1, source_target_pairs={{0,32},{32,0},{1,33},{33,1},{2,34},{34,2},{3,35},{35,3},{4,36},{36... | collective-permute-start | bytes 393224 | tf_op jit(solution)/shard_map/ppermute | solution.py:33

commit v4 on v3

--- a/solution.py
+++ b/solution.py
@@ -18,11 +18,11 @@
 ALL = ("row", "core", "y", "x", "z")
 
 
-CHIPS = ("row", "y", "x", "z")
+CHIPS = ("z", "row", "y", "x")
 
 
 def place():
-    return jnp.right_shift(lax.axis_index("row"), 1), lax.axis_index("core")
+    return lax.axis_index("z"), lax.axis_index("core")
 
 
 def order_slot(o, core):
@@ -45,7 +45,7 @@
 
 
 def make_constants():
-    a = np.arange(32)
+    a = np.concatenate([np.arange(0, 32, 2), np.arange(1, 32, 2)])
     b = np.arange(128)
     c = np.arange(64)
     e = np.arange(32)
@@ -103,9 +103,14 @@
 
 
 def degree_index():
-    return lax.broadcasted_iota(jnp.int32, (32, 128), 0) * 128 + lax.broadcasted_iota(
-        jnp.int32, (32, 128), 1
-    )
+    row = lax.broadcasted_iota(jnp.int32, (32, 128), 0)
+    a = jnp.bitwise_and(row, 15) * 2 + jnp.right_shift(row, 4)
+    return a * 128 + lax.broadcasted_iota(jnp.int32, (32, 128), 1)
+
+
+def chip_rows(o, j):
+    at = (o // 4) * 256 + (o % 4) * 4 + j
+    return [pl.ds(z * 1024 + at, 16, stride=16) for z in range(2)]
 
 
 def fourier_tables(m_ref, core, f_ref, ft_ref):
@@ -205,8 +210,8 @@
         for field in range(2):
             tiles = []
             for ri in range(2):
-                j = (o // 4) * 512 + (o % 4) * 4 + field * 2 + ri
-                tile = xs[pl.ds(j, 32, stride=16), :]
+                rows = chip_rows(o, field * 2 + ri)
+                tile = jnp.concatenate([xs[at, :] for at in rows], axis=0)
                 tiles.append(jnp.where(inside, tile, 0.0).astype(BF16))
             rhs = jnp.concatenate(tiles, axis=1)
             rhs = jnp.concatenate([rhs, rhs], axis=0)
@@ -334,8 +339,8 @@
             r = jnp.dot(w3_ref[half], rhs, preferred_element_type=F32)
             for part in range(2):
                 value = jnp.where(inside, r[:, part * 128 : part * 128 + 128], 0.0)
-                j = (o // 4) * 512 + (o % 4) * 4 + part * 2 + ri
-                os[pl.ds(j, 32, stride=16), :] = value
+                for z, at in enumerate(chip_rows(o, part * 2 + ri)):
+                    os[at, :] = value[z * 16 : z * 16 + 16]
     out_ref[...] = os[...].astype(BF16)
 
 

time: 77.9 us -> 74.8 us (0.960); the launches traced: 77.7 us -> 73.3 us
  blocking collectives: 60.4 us -> 55.7 us
    all_to_all x1, blocking collectives: 35.1 us -> 31.7 us  [body(): got = lax.all_to_all(sent.reshape(128, 16, 128), CHIPS, 0, 0, tiled=True)]
    all_to_all x1, blocking collectives: 25.2 us -> 24 us  [body(): home = lax.all_to_all(sums.reshape(128, 16, 128), CHIPS, 0, 0, tiled=True)]
where the time goes in v4:
time: 74.8 us; the launch traced here: 73.3 us
  blocking collectives  55.7 us (74%)
  Pallas kernels  12.4 us (17%)
  starting transfers between devices  3.45 us (5%)
  waiting for transfers between devices  1.02 us (1%)
    all_to_all x1, blocking collectives, body(): got = lax.all_to_all(sent.reshape(128, 16, 128), CHIPS, 0, 0, tiled=True)  31.7 us
    all_to_all x1, blocking collectives, body(): home = lax.all_to_all(sums.reshape(128, 16, 128), CHIPS, 0, 0, tiled=True)  24 us
    pallas_call x6, Pallas kernels, call(): pl.pallas_call(kernel, name=name, out_shape=[jax.ShapeDtypeStruct(s, d) f...  12.4 us
    ppermute x2, starting transfers between devices, swap_cores(): return lax.ppermute(x, 'core', [(0, 1), (1, 0)])  3.45 us
  transfers between devices with their start and end apart: 2, of which 1 were waited for; matrix products, arithmetic and copies ran while one was open for 0% of the time, Pallas kernels for 2%

profile of v4, /device:TPU:1, one launch (start us, length us, event | category | flops | bytes accessed | tf_op | source)
XLA Modules:
  0.0 73.3 jit_solution(1108149117157577400)
XLA Ops:
  0.6 1.9 %pack.1 = (bf16[2048,128]{1,0:T(8,128)(2,1)S(1)}, s32[32]{0:T(128)S(1)}) custom-call(bf16[512,128]{1,0:T(8,128)(2,1)} %bitcast.16, bf16[512,128]{1,0:T(8,128)(2,1)} %bitcast.17, s32[32]{0:T(128)} %m_hbm.1), custom_call_target="tpu_custom_call" | custom-call | tf_op jit(solution)/shard_map/pack/pallas_call | solution.py:355
  2.5 0.0 copy-start
  2.5 0.0 copy-start.1
  2.6 0.0 copy-start.3
  2.6 31.7 %all_to_all.10 = bf16[128,16,128]{2,1,0:T(8,128)(2,1)S(1)} all-to-all(bf16[128,16,128]{2,1,0:T(8,128)(2,1)S(1)} %bitcast.13), channel_id=1, replica_groups=mesh['row'=4,'core'=2,'y'=4,'x'=4,'z'=2] {'z','row','y','x'}, dimensions={0} | all-to-all | bytes 1048576 | tf_op jit(solution)/shard_map/all_to_all | solution.py:401
  34.3 0.0 copy-done
  34.3 0.0 copy-done.1
  34.3 0.0 copy-done.3
  34.3 0.0 copy-start.5
  34.3 0.0 copy-start.6
  34.3 3.9 %synth.1 = (bf16[256,768]{1,0:T(8,128)(2,1)S(1)}, bf16[256,768]{1,0:T(8,128)(2,1)S(1)}) custom-call(s32[32]{0:T(128)S(1)} %get-tuple-element.13.m_ref, bf16[2048,128]{1,0:T(8,128)(2,1)S(1)} %bitcast.10, bf16[2,64,64]{2,1,0:T(8,128)(2,1)S(1)} %copy-done.3, f32[6,32,128]{2,1,0:T(8,128)S(1)} %copy-done.1, bf16[3,256,256]{2,1,0:T(8,128)(2,1)S(1)} %copy-done), custom_call_target="tpu_custom_call" | custom-call | tf_op jit(solution)/shard_map/synth/pallas_call | solution.py:355
  38.3 3.0 %collective-permute-start = (bf16[256,768]{1,0:T(8,128)(2,1)S(1)}, bf16[256,768]{1,0:T(8,128)(2,1)S(1)}, u32[]{:S(2)}, u32[]{:S(2)}) collective-permute-start(bf16[256,768]{1,0:T(8,128)(2,1)S(1)} %get-tuple-element.16), channel_id=1, source_target_pairs={{0,32},{32,0},{1,33},{33,1},{2,34},{34,2},{3,35},{35,3},{4,36},{36... | collective-permute-start | bytes 1179656 | tf_op jit(solution)/shard_map/ppermute | solution.py:33
  41.3 0.0 copy-done.5
  41.3 0.0 copy-done.6
  41.3 1.3 %tables.1 = (bf16[2,64,256]{2,1,0:T(8,128)(2,1)S(1)}, bf16[2,256,64]{2,1,0:T(8,128)(2,1)S(1)}, f32[8,128]{1,0:T(8,128)S(1)}) custom-call(s32[32]{0:T(128)S(1)} %get-tuple-element.13.m_ref, s32[32,128]{1,0:T(8,128)S(1)} %bitcast.14, f32[32,128]{1,0:T(8,128)S(1)} %bitcast.15), custom_call_target="tpu_custom_call" | custom-call | tf_op jit(solution)/shard_map/tables/pallas_call | solution.py:355
  42.7 0.0 collective-permute-done.refs_1_
  42.7 0.0 copy-start.2
  42.7 0.0 copy-start.4
  42.7 2.4 %pixel.1 = (bf16[256,256]{1,0:T(8,128)(2,1)S(1)}, bf16[256,256]{1,0:T(8,128)(2,1)S(1)}) custom-call(bf16[256,768]{1,0:T(8,128)(2,1)S(1)} %get-tuple-element.15.refs_0_, bf16[256,768]{1,0:T(8,128)(2,1)S(1)} %collective-permute-done.refs_1_, bf16[2,64,256]{2,1,0:T(8,128)(2,1)S(1)} %get-tuple-element.17.refs_2_, ...), custom_call_target="tpu_custom_call" | custom-call | tf_op jit(solution)/shard_map/pixel/pallas_call | solution.py:355
  45.1 0.4 collective-permute-start.1
  45.5 1.0 %collective-permute-done.1.refs_1_ = bf16[256,256]{1,0:T(8,128)(2,1)S(1)} collective-permute-done((bf16[256,256]{1,0:T(8,128)(2,1)S(1)}, bf16[256,256]{1,0:T(8,128)(2,1)S(1)}, u32[]{:S(2)}, u32[]{:S(2)}) %collective-permute-start.1) | collective-permute-done | bytes 131104 | tf_op jit(solution)/shard_map/ppermute | solution.py:33
  46.5 0.0 copy-done.2
  46.6 0.0 copy-done.4
  46.6 1.8 %adjoint.1 = bf16[2048,128]{1,0:T(8,128)(2,1)S(1)} custom-call(s32[32]{0:T(128)S(1)} %get-tuple-element.13.m_ref, bf16[256,256]{1,0:T(8,128)(2,1)S(1)} %get-tuple-element.20.refs_0_, bf16[256,256]{1,0:T(8,128)(2,1)S(1)} %collective-permute-done.1.refs_1_, f32[6,32,128]{2,1,0:T(8,128)S(1)} %copy-done.1, bf16[256,512]{1,0:T(8,128)(2,1)S(1)} %copy-done.2, ...), custom_call_target="tpu_custom_call" | custom-call | tf_op jit(solution)/shard_map/adjoint/pallas_call | solution.py:355
  48.4 24.0 %all_to_all.11 = bf16[128,16,128]{2,1,0:T(8,128)(2,1)S(1)} all-to-all(bf16[128,16,128]{2,1,0:T(8,128)(2,1)S(1)} %bitcast.11), channel_id=1, replica_groups=mesh['row'=4,'core'=2,'y'=4,'x'=4,'z'=2] {'z','row','y','x'}, dimensions={0} | all-to-all | bytes 1048576 | tf_op jit(solution)/shard_map/all_to_all | solution.py:423
  72.3 1.0 %unpack.1 = (bf16[512,128]{1,0:T(8,128)(2,1)}, bf16[512,128]{1,0:T(8,128)(2,1)}) custom-call(bf16[2048,128]{1,0:T(8,128)(2,1)S(1)} %bitcast.12), custom_call_target="tpu_custom_call" | custom-call | tf_op jit(solution)/shard_map/unpack/pallas_call | solution.py:355
Async XLA Ops:
  2.5 31.8 %copy-start = (bf16[3,256,256]{2,1,0:T(8,128)(2,1)S(1)}, bf16[3,256,256]{2,1,0:T(8,128)(2,1)}, u32[]{:S(2)}) copy-start(bf16[3,256,256]{2,1,0:T(8,128)(2,1)} %constant.12.clone.w2_ref) | copy-start | bytes 1179652
  2.5 31.8 %copy-start.1 = (f32[6,32,128]{2,1,0:T(8,128)S(1)}, f32[6,32,128]{2,1,0:T(8,128)}, u32[]{:S(2)}) copy-start(f32[6,32,128]{2,1,0:T(8,128)} %constant.11.clone.tw_ref.refs_2_) | copy-start | bytes 294916
  2.6 31.8 %copy-start.3 = (bf16[2,64,64]{2,1,0:T(8,128)(2,1)S(1)}, bf16[2,64,64]{2,1,0:T(8,128)(2,1)}, u32[]{:S(2)}) copy-start(bf16[2,64,64]{2,1,0:T(8,128)(2,1)} %constant.10.clone.w1_ref) | copy-start | bytes 49156
  34.3 7.0 %copy-start.5 = (s32[4096]{0:T(1024)S(1)}, s32[4096]{0:T(1024)}, u32[]{:S(2)}) copy-start(s32[4096]{0:T(1024)} %param.13) | copy-start | bytes 49156
  34.3 7.0 %copy-start.6 = (f32[4096]{0:T(1024)S(1)}, f32[4096]{0:T(1024)}, u32[]{:S(2)}) copy-start(f32[4096]{0:T(1024)} %param.14) | copy-start | bytes 49156
  38.3 4.4 %collective-permute-start = (bf16[256,768]{1,0:T(8,128)(2,1)S(1)}, bf16[256,768]{1,0:T(8,128)(2,1)S(1)}, u32[]{:S(2)}, u32[]{:S(2)}) collective-permute-start(bf16[256,768]{1,0:T(8,128)(2,1)S(1)} %get-tuple-element.16), channel_id=1, source_target_pairs={{0,32},{32,0},{1,33},{33,1},{2,34},{34,2},{3,35},{35,3},{4,36},{36... | collective-permute-start | bytes 1179656 | tf_op jit(solution)/shard_map/ppermute | solution.py:33
  42.7 3.9 %copy-start.2 = (bf16[256,512]{1,0:T(8,128)(2,1)S(1)}, bf16[256,512]{1,0:T(8,128)(2,1)}, u32[]{:S(2)}) copy-start(bf16[256,512]{1,0:T(8,128)(2,1)} %constant.13.clone.refs_3_) | copy-start | bytes 786436
  42.7 3.9 %copy-start.4 = (bf16[2,32,96]{2,1,0:T(8,128)(2,1)S(1)}, bf16[2,32,96]{2,1,0:T(8,128)(2,1)}, u32[]{:S(2)}) copy-start(bf16[2,32,96]{2,1,0:T(8,128)(2,1)} %constant.14.clone.refs_4_) | copy-start | bytes 36868
  45.1 1.4 %collective-permute-start.1 = (bf16[256,256]{1,0:T(8,128)(2,1)S(1)}, bf16[256,256]{1,0:T(8,128)(2,1)S(1)}, u32[]{:S(2)}, u32[]{:S(2)}) collective-permute-start(bf16[256,256]{1,0:T(8,128)(2,1)S(1)} %get-tuple-element.21), channel_id=1, source_target_pairs={{0,32},{32,0},{1,33},{33,1},{2,34},{34,2},{3,35},{35,3},{4,36},{36... | collective-permute-start | bytes 393224 | tf_op jit(solution)/shard_map/ppermute | solution.py:33

commit v5 on v4

--- a/solution.py
+++ b/solution.py
@@ -42,6 +42,10 @@
     hi = values.astype(jnp.bfloat16)
     lo = (values - hi.astype(np.float32)).astype(jnp.bfloat16)
     return hi, lo
+
+
+def blocks(matrices, n):
+    return np.stack([np.kron(np.eye(n, dtype=m.dtype), m) for m in matrices])
 
 
 def make_constants():
@@ -55,7 +59,7 @@
     both = np.concatenate([plain, plain * (a / 32.0)[None, :]], axis=0)
     hi, lo = split_hi_lo(both)
     w1 = np.concatenate([hi, lo], axis=1).reshape(4, 2, 16, 64)
-    w1 = w1.transpose(1, 0, 2, 3).reshape(2, 64, 64)
+    w1 = blocks(w1.transpose(1, 0, 2, 3).reshape(2, 64, 64), 4)
     twiddle, w2, wadj = [], [], []
     for s in SPINS:
         f = 2 * b + 1 + s
@@ -76,7 +80,7 @@
             wadj.append(np.concatenate(split_hi_lo(back), axis=0))
     last = np.stack([np.cos(first).T, -np.sin(first).T], axis=1).reshape(32, 2, 2, 16)
     hi, lo = split_hi_lo(last.transpose(2, 0, 1, 3).reshape(2, 32, 32))
-    w3 = np.concatenate([hi, hi, lo], axis=2)
+    w3 = blocks(np.concatenate([hi, hi, lo], axis=2), 2)
     return {
         "w1": w1,
         "tw": np.stack(twiddle).astype(np.float32),
@@ -197,61 +201,61 @@
 
 
 def synth_kernel(m_ref, x_ref, w1_ref, tw_ref, w2_ref, *refs):
-    keep_ref, send_ref, xs, lhs_ref, os = refs
+    keep_ref, send_ref, xs, os = refs
     half, core = place()
     mine = pl.ds(half * 16, 16)
     xs[...] = x_ref[...].astype(F32)
     degree = degree_index()
     lane = lax.broadcasted_iota(jnp.int32, (1, 128), 1)
-    for o in range(ORD_ROW):
-        m = m_ref[order_slot(o, core)]
-        inside = degree >= m
-        pc, ps, sign = order_phase(m)
+    for group in range(ORD_ROW // 4):
+        first = []
         for field in range(2):
             tiles = []
-            for ri in range(2):
-                rows = chip_rows(o, field * 2 + ri)
-                tile = jnp.concatenate([xs[at, :] for at in rows], axis=0)
-                tiles.append(jnp.where(inside, tile, 0.0).astype(BF16))
-            rhs = jnp.concatenate(tiles, axis=1)
-            rhs = jnp.concatenate([rhs, rhs], axis=0)
-            first = jnp.dot(w1_ref[half], rhs, preferred_element_type=F32)
-            for k in (0, 1) if field == 0 else (2,):
-                ar, ai = tw_ref[2 * k, mine, :], tw_ref[2 * k + 1, mine, :]
+            for o in range(group * 4, group * 4 + 4):
+                inside = degree >= m_ref[order_slot(o, core)]
+                pair = []
+                for ri in range(2):
+                    rows = chip_rows(o, field * 2 + ri)
+                    tile = jnp.concatenate([xs[at, :] for at in rows], axis=0)
+                    pair.append(jnp.where(inside, tile, 0.0).astype(BF16))
+                tiles += [jnp.concatenate(pair, axis=1)] * 2
+            rhs = jnp.concatenate(tiles, axis=0)
+            first.append(jnp.dot(w1_ref[half], rhs, preferred_element_type=F32))
+        phases = [order_phase(m_ref[order_slot(group * 4 + i, core)]) for i in range(4)]
+        for k in (2, 0, 1):
+            ar, ai = tw_ref[2 * k, mine, :], tw_ref[2 * k + 1, mine, :]
+            slope = (2 * lane + 1 + SPINS[k]).astype(F32) * (1.0 / (2 * LMAX))
+            rows = [[], []]
+            for i in range(4):
+                pc, ps, sign = phases[i]
                 tr = ar * pc + ai * ps
                 ti = ai * pc - ar * ps
-                slope = (2 * lane + 1 + SPINS[k]).astype(F32) * (1.0 / (2 * LMAX))
                 for ri in range(2):
-                    part = first[:, ri * 128 : (ri + 1) * 128]
+                    part = first[k // 2][i * 64 : i * 64 + 64, ri * 128 : (ri + 1) * 128]
                     sr, si = part[0:16], part[16:32]
                     vr = part[32:48] + slope * sr
                     vi = part[48:64] + slope * si
-                    rows = (
-                        (sr * tr - si * ti, sr * ti + si * tr),
-                        (-(vr * ti + vi * tr), vr * tr - vi * ti),
+                    rows[0].append(jnp.concatenate([sr * tr - si * ti, sr * ti + si * tr], axis=1))
+                    rows[1].append(
+                        jnp.concatenate([-(vr * ti + vi * tr), vr * tr - vi * ti], axis=1)
                     )
-                    for kind in range(2):
-                        row = jnp.concatenate(rows[kind], axis=1)
-                        hi = row.astype(BF16)
-                        lo = (row - hi.astype(F32)).astype(BF16)
-                        at = ((kind * ORD_ROW + o) * 2 + ri) * 16
-                        lhs_ref[k, at : at + 16, :] = hi
-                        lhs_ref[k, 1024 + at : 1024 + at + 16, :] = lo
-    for k in range(3):
-        y = jnp.dot(lhs_ref[k], w2_ref[k], preferred_element_type=F32)
-        y = (y[1024:, :128] + y[:1024, 128:]) + y[:1024, :128]
-        der_map, cos_map = ((0, 2), (1, 3), (4, 5))[k]
-        for o in range(ORD_ROW):
-            m = m_ref[order_slot(o, core)]
-            pc, ps, sign = order_phase(m)
-            factor = m.astype(F32) * (1.0 / LMAX)
-            for ri in range(2):
-                rows = pl.ds(o * 2 + ri, 16, stride=32)
-                scale = -factor if ri == 0 else factor
-                at = (o * 2 + 1 - ri) * 16
-                os[cos_map, rows, :] = y[at : at + 16] * (half_sign(128, sign) * scale)
-                at = ((ORD_ROW + o) * 2 + ri) * 16
-                os[der_map, rows, :] = y[at : at + 16] * half_sign(128, -sign)
+            row = jnp.concatenate(rows[0] + rows[1], axis=0)
+            hi = row.astype(BF16)
+            lo = (row - hi.astype(F32)).astype(BF16)
+            y = jnp.dot(jnp.concatenate([hi, lo], axis=0), w2_ref[k], preferred_element_type=F32)
+            y = (y[256:, :128] + y[:256, 128:]) + y[:256, :128]
+            der_map, cos_map = ((0, 2), (1, 3), (4, 5))[k]
+            for i in range(4):
+                o = group * 4 + i
+                sign = phases[i][2]
+                factor = m_ref[order_slot(o, core)].astype(F32) * (1.0 / LMAX)
+                for ri in range(2):
+                    at = pl.ds(o * 2 + ri, 16, stride=32)
+                    scale = -factor if ri == 0 else factor
+                    c = (i * 2 + 1 - ri) * 16
+                    d = 128 + (i * 2 + ri) * 16
+                    os[cos_map, at, :] = y[c : c + 16] * (half_sign(128, sign) * scale)
+                    os[der_map, at, :] = y[d : d + 16] * half_sign(128, -sign)
     for k in range(6):
         lanes = slice(k * 128, (k + 1) * 128)
         send_ref[:, lanes] = os[k, pl.ds((1 - core) * 256, 256), :].astype(BF16)
@@ -265,7 +269,7 @@
 
     def rows_of(i):
         chunks = [x_ref[i * 32 : i * 32 + 32, :] for x_ref in x_refs]
-        return jnp.concatenate(chunks, axis=0).astype(F32)
+        return jnp.concatenate(chunks, axis=0)
 
     for pair in range(4):
         i0, i1 = 2 * pair, 2 * pair + 1
@@ -276,7 +280,7 @@
                 x = jnp.where(low_in, x0, x1)
             else:
                 x = jnp.where(low_in, x1, x0)
-            px = jnp.dot(ft_ref[parity], x.astype(BF16), preferred_element_type=F32)
+            px = jnp.dot(ft_ref[parity], x, preferred_element_type=F32)
             qt, ut, qp, up, dt, dp = (px[:, k * 128 : (k + 1) * 128] for k in range(6))
             deflected = jnp.concatenate([dt * qt + dp * qp, dt * ut + dp * up], axis=1)
             results.append(
@@ -317,6 +321,7 @@
             ar, ai = tw_ref[2 * k, mine, :], tw_ref[2 * k + 1, mine, :]
             turned.append((ar * pc + ai * ps, ai * pc - ar * ps))
         (pr, pi), (mr, mi) = turned
+        columns = []
         for ri in range(2):
             at = (o * 2 + ri) * 32
             yq, yu = y[at : at + 16], y[at + 16 : at + 32]
@@ -335,10 +340,13 @@
             )
             hi = p.astype(BF16)
             lo = (p - hi.astype(F32)).astype(BF16)
-            rhs = jnp.concatenate([hi, lo, hi], axis=0)
-            r = jnp.dot(w3_ref[half], rhs, preferred_element_type=F32)
+            columns += [hi, lo, hi]
+        rhs = jnp.concatenate(columns, axis=0)
+        r = jnp.dot(w3_ref[half], rhs, preferred_element_type=F32)
+        for ri in range(2):
             for part in range(2):
-                value = jnp.where(inside, r[:, part * 128 : part * 128 + 128], 0.0)
+                value = r[ri * 32 : ri * 32 + 32, part * 128 : part * 128 + 128]
+                value = jnp.where(inside, value, 0.0)
                 for z, at in enumerate(chip_rows(o, part * 2 + ri)):
                     os[at, :] = value[z * 16 : z * 16 + 16]
     out_ref[...] = os[...].astype(BF16)
@@ -357,7 +365,7 @@
         name=name,
         out_shape=[jax.ShapeDtypeStruct(s, d) for s, d in outs],
         in_specs=specs,
-        out_specs=[SMEM if len(shape) == 1 else VMEM for shape, dtype in outs],
+        out_specs=[VMEM for o in outs],
         scratch_shapes=scratch,
         compiler_params=pltpu.CompilerParams(vmem_limit_bytes=48 << 20),
     )(*inputs)
@@ -404,7 +412,7 @@
         "synth",
         [orders, got.reshape(2048, 128), const["w1"], const["tw"], const["w2"]],
         [((256, 768), BF16)] * 2,
-        [scratch((2048, 128)), scratch((3, 2048, 256), BF16), scratch((6, 512, 128))],
+        [scratch((2048, 128)), scratch((6, 512, 128))],
     )
     held, handed = call(
         pixel_kernel,

time: 74.8 us -> 74 us (0.989)
  Pallas kernels: 12.4 us -> 11.6 us
    pallas_call x6, Pallas kernels: 12.4 us -> 11.6 us  [call(): pl.pallas_call(kernel, name=name, out_shape=[jax.ShapeDtypeStruct(s, d) f...]
where the time goes in v5:
time: 74 us; the launch traced here: 72.5 us
  blocking collectives  55.7 us (75%)
  Pallas kernels  11.6 us (16%)
  starting transfers between devices  3.46 us (5%)
  waiting for transfers between devices  1.02 us (1%)
  between operations  0.74 us (1%)
    all_to_all x1, blocking collectives, body(): got = lax.all_to_all(sent.reshape(128, 16, 128), CHIPS, 0, 0, tiled=True)  31.7 us
    all_to_all x1, blocking collectives, body(): home = lax.all_to_all(sums.reshape(128, 16, 128), CHIPS, 0, 0, tiled=True)  24 us
    pallas_call x6, Pallas kernels, call(): pl.pallas_call(kernel, name=name, out_shape=[jax.ShapeDtypeStruct(s, d) f...  11.6 us
    ppermute x2, starting transfers between devices, swap_cores(): return lax.ppermute(x, 'core', [(0, 1), (1, 0)])  3.46 us
  transfers between devices with their start and end apart: 2, of which 1 were waited for; matrix products, arithmetic and copies ran while one was open for 0% of the time, Pallas kernels for 2%

profile of v5, /device:TPU:1, one launch (start us, length us, event | category | flops | bytes accessed | tf_op | source)
XLA Modules:
  0.0 72.5 jit_solution(18083715912286004040)
XLA Ops:
  0.6 1.3 %pack.1 = (bf16[2048,128]{1,0:T(8,128)(2,1)S(1)}, s32[32]{0:T(128)S(1)}) custom-call(bf16[512,128]{1,0:T(8,128)(2,1)} %bitcast.16, bf16[512,128]{1,0:T(8,128)(2,1)} %bitcast.17, s32[32]{0:T(128)} %m_hbm.1), custom_call_target="tpu_custom_call" | custom-call | tf_op jit(solution)/shard_map/pack/pallas_call | solution.py:363
  1.9 0.0 copy-start
  1.9 0.0 copy-start.1
  2.0 0.0 copy-start.3
  2.0 31.7 %all_to_all.10 = bf16[128,16,128]{2,1,0:T(8,128)(2,1)S(1)} all-to-all(bf16[128,16,128]{2,1,0:T(8,128)(2,1)S(1)} %bitcast.13), channel_id=1, replica_groups=mesh['row'=4,'core'=2,'y'=4,'x'=4,'z'=2] {'z','row','y','x'}, dimensions={0} | all-to-all | bytes 1048576 | tf_op jit(solution)/shard_map/all_to_all | solution.py:409
  33.7 0.0 copy-done
  33.7 0.0 copy-done.1
  33.7 0.0 copy-done.3
  33.7 0.0 copy-start.5
  33.7 0.0 copy-start.6
  33.7 3.7 %synth.1 = (bf16[256,768]{1,0:T(8,128)(2,1)S(1)}, bf16[256,768]{1,0:T(8,128)(2,1)S(1)}) custom-call(s32[32]{0:T(128)S(1)} %get-tuple-element.13.m_ref, bf16[2048,128]{1,0:T(8,128)(2,1)S(1)} %bitcast.10, bf16[2,256,256]{2,1,0:T(8,128)(2,1)S(1)} %copy-done.3, f32[6,32,128]{2,1,0:T(8,128)S(1)} %copy-done, bf16[3,256,256]{2,1,0:T(8,128)(2,1)S(1)} %copy-done.1), custom_call_target="tpu_custom_call" | custom-call | tf_op jit(solution)/shard_map/synth/pallas_call | solution.py:363
  37.5 3.0 %collective-permute-start = (bf16[256,768]{1,0:T(8,128)(2,1)S(1)}, bf16[256,768]{1,0:T(8,128)(2,1)S(1)}, u32[]{:S(2)}, u32[]{:S(2)}) collective-permute-start(bf16[256,768]{1,0:T(8,128)(2,1)S(1)} %get-tuple-element.16), channel_id=1, source_target_pairs={{0,32},{32,0},{1,33},{33,1},{2,34},{34,2},{3,35},{35,3},{4,36},{36... | collective-permute-start | bytes 1179656 | tf_op jit(solution)/shard_map/ppermute | solution.py:33
  40.5 0.0 copy-done.5
  40.5 0.0 copy-done.6
  40.5 1.3 %tables.1 = (bf16[2,64,256]{2,1,0:T(8,128)(2,1)S(1)}, bf16[2,256,64]{2,1,0:T(8,128)(2,1)S(1)}, f32[8,128]{1,0:T(8,128)S(1)}) custom-call(s32[32]{0:T(128)S(1)} %get-tuple-element.13.m_ref, s32[32,128]{1,0:T(8,128)S(1)} %bitcast.14, f32[32,128]{1,0:T(8,128)S(1)} %bitcast.15), custom_call_target="tpu_custom_call" | custom-call | tf_op jit(solution)/shard_map/tables/pallas_call | solution.py:363
  41.9 0.0 collective-permute-done.refs_1_
  41.9 0.0 copy-start.2
  41.9 0.0 copy-start.4
  41.9 2.4 %pixel.1 = (bf16[256,256]{1,0:T(8,128)(2,1)S(1)}, bf16[256,256]{1,0:T(8,128)(2,1)S(1)}) custom-call(bf16[256,768]{1,0:T(8,128)(2,1)S(1)} %get-tuple-element.15.refs_0_, bf16[256,768]{1,0:T(8,128)(2,1)S(1)} %collective-permute-done.refs_1_, bf16[2,64,256]{2,1,0:T(8,128)(2,1)S(1)} %get-tuple-element.17.refs_2_, ...), custom_call_target="tpu_custom_call" | custom-call | tf_op jit(solution)/shard_map/pixel/pallas_call | solution.py:363
  44.3 0.4 collective-permute-start.1
  44.8 1.0 %collective-permute-done.1.refs_1_ = bf16[256,256]{1,0:T(8,128)(2,1)S(1)} collective-permute-done((bf16[256,256]{1,0:T(8,128)(2,1)S(1)}, bf16[256,256]{1,0:T(8,128)(2,1)S(1)}, u32[]{:S(2)}, u32[]{:S(2)}) %collective-permute-start.1) | collective-permute-done | bytes 131104 | tf_op jit(solution)/shard_map/ppermute | solution.py:33
  45.8 0.0 copy-done.2
  45.8 0.0 copy-done.4
  45.8 1.8 %adjoint.1 = bf16[2048,128]{1,0:T(8,128)(2,1)S(1)} custom-call(s32[32]{0:T(128)S(1)} %get-tuple-element.13.m_ref, bf16[256,256]{1,0:T(8,128)(2,1)S(1)} %get-tuple-element.20.refs_0_, bf16[256,256]{1,0:T(8,128)(2,1)S(1)} %collective-permute-done.1.refs_1_, f32[6,32,128]{2,1,0:T(8,128)S(1)} %copy-done, bf16[256,512]{1,0:T(8,128)(2,1)S(1)} %copy-done.2, ...), custom_call_target="tpu_custom_call" | custom-call | tf_op jit(solution)/shard_map/adjoint/pallas_call | solution.py:363
  47.6 24.0 %all_to_all.11 = bf16[128,16,128]{2,1,0:T(8,128)(2,1)S(1)} all-to-all(bf16[128,16,128]{2,1,0:T(8,128)(2,1)S(1)} %bitcast.11), channel_id=1, replica_groups=mesh['row'=4,'core'=2,'y'=4,'x'=4,'z'=2] {'z','row','y','x'}, dimensions={0} | all-to-all | bytes 1048576 | tf_op jit(solution)/shard_map/all_to_all | solution.py:431
  71.6 1.0 %unpack.1 = (bf16[512,128]{1,0:T(8,128)(2,1)}, bf16[512,128]{1,0:T(8,128)(2,1)}) custom-call(bf16[2048,128]{1,0:T(8,128)(2,1)S(1)} %bitcast.12), custom_call_target="tpu_custom_call" | custom-call | tf_op jit(solution)/shard_map/unpack/pallas_call | solution.py:363
Async XLA Ops:
  1.9 31.8 %copy-start = (f32[6,32,128]{2,1,0:T(8,128)S(1)}, f32[6,32,128]{2,1,0:T(8,128)}, u32[]{:S(2)}) copy-start(f32[6,32,128]{2,1,0:T(8,128)} %constant.11.clone.tw_ref.refs_2_) | copy-start | bytes 294916
  1.9 31.8 %copy-start.1 = (bf16[3,256,256]{2,1,0:T(8,128)(2,1)S(1)}, bf16[3,256,256]{2,1,0:T(8,128)(2,1)}, u32[]{:S(2)}) copy-start(bf16[3,256,256]{2,1,0:T(8,128)(2,1)} %constant.12.clone.w2_ref) | copy-start | bytes 1179652
  2.0 31.8 %copy-start.3 = (bf16[2,256,256]{2,1,0:T(8,128)(2,1)S(1)}, bf16[2,256,256]{2,1,0:T(8,128)(2,1)}, u32[]{:S(2)}) copy-start(bf16[2,256,256]{2,1,0:T(8,128)(2,1)} %constant.10.clone.w1_ref) | copy-start | bytes 786436
  33.7 6.8 %copy-start.5 = (s32[4096]{0:T(1024)S(1)}, s32[4096]{0:T(1024)}, u32[]{:S(2)}) copy-start(s32[4096]{0:T(1024)} %param.13) | copy-start | bytes 49156
  33.7 6.8 %copy-start.6 = (f32[4096]{0:T(1024)S(1)}, f32[4096]{0:T(1024)}, u32[]{:S(2)}) copy-start(f32[4096]{0:T(1024)} %param.14) | copy-start | bytes 49156
  37.5 4.4 %collective-permute-start = (bf16[256,768]{1,0:T(8,128)(2,1)S(1)}, bf16[256,768]{1,0:T(8,128)(2,1)S(1)}, u32[]{:S(2)}, u32[]{:S(2)}) collective-permute-start(bf16[256,768]{1,0:T(8,128)(2,1)S(1)} %get-tuple-element.16), channel_id=1, source_target_pairs={{0,32},{32,0},{1,33},{33,1},{2,34},{34,2},{3,35},{35,3},{4,36},{36... | collective-permute-start | bytes 1179656 | tf_op jit(solution)/shard_map/ppermute | solution.py:33
  41.9 3.9 %copy-start.2 = (bf16[256,512]{1,0:T(8,128)(2,1)S(1)}, bf16[256,512]{1,0:T(8,128)(2,1)}, u32[]{:S(2)}) copy-start(bf16[256,512]{1,0:T(8,128)(2,1)} %constant.13.clone.refs_3_) | copy-start | bytes 786436
  41.9 3.9 %copy-start.4 = (bf16[2,64,192]{2,1,0:T(8,128)(2,1)S(1)}, bf16[2,64,192]{2,1,0:T(8,128)(2,1)}, u32[]{:S(2)}) copy-start(bf16[2,64,192]{2,1,0:T(8,128)(2,1)} %constant.14.clone.refs_4_) | copy-start | bytes 147460
  44.3 1.4 %collective-permute-start.1 = (bf16[256,256]{1,0:T(8,128)(2,1)S(1)}, bf16[256,256]{1,0:T(8,128)(2,1)S(1)}, u32[]{:S(2)}, u32[]{:S(2)}) collective-permute-start(bf16[256,256]{1,0:T(8,128)(2,1)S(1)} %get-tuple-element.21), channel_id=1, source_target_pairs={{0,32},{32,0},{1,33},{33,1},{2,34},{34,2},{3,35},{35,3},{4,36},{36... | collective-permute-start | bytes 393224 | tf_op jit(solution)/shard_map/ppermute | solution.py:33

commit v6 on v5

--- a/solution.py
+++ b/solution.py
@@ -280,12 +280,15 @@
                 x = jnp.where(low_in, x0, x1)
             else:
                 x = jnp.where(low_in, x1, x0)
-            px = jnp.dot(ft_ref[parity], x, preferred_element_type=F32)
-            qt, ut, qp, up, dt, dp = (px[:, k * 128 : (k + 1) * 128] for k in range(6))
-            deflected = jnp.concatenate([dt * qt + dp * qp, dt * ut + dp * up], axis=1)
-            results.append(
-                jnp.dot(f_ref[parity], deflected.astype(BF16), preferred_element_type=F32)
-            )
+            parts = []
+            for at in range(0, LONGS, 64):
+                ft = ft_ref[parity, at : at + 64, :]
+                px = jnp.dot(ft, x, preferred_element_type=F32)
+                qt, ut, qp, up, dt, dp = (px[:, k * 128 : (k + 1) * 128] for k in range(6))
+                part = jnp.concatenate([dt * qt + dp * qp, dt * ut + dp * up], axis=1)
+                parts.append(part.astype(BF16))
+            deflected = jnp.concatenate(parts, axis=0)
+            results.append(jnp.dot(f_ref[parity], deflected, preferred_element_type=F32))
         even, odd = results
         for i, g in ((i0, jnp.where(low_out, even, odd)), (i1, jnp.where(low_out, odd, even))):
             w = w_ref[i : i + 1, :]

time: 74 us -> 73.5 us (level)
  no operation moved by 1% of the time
where the time goes in v6:
time: 73.5 us; the launch traced here: 72.1 us
  blocking collectives  55.7 us (76%)
  Pallas kernels  11.1 us (15%)
  starting transfers between devices  3.47 us (5%)
  waiting for transfers between devices  1.01 us (1%)
  between operations  0.74 us (1%)
    all_to_all x1, blocking collectives, body(): got = lax.all_to_all(sent.reshape(128, 16, 128), CHIPS, 0, 0, tiled=True)  31.7 us
    all_to_all x1, blocking collectives, body(): home = lax.all_to_all(sums.reshape(128, 16, 128), CHIPS, 0, 0, tiled=True)  24 us
    pallas_call x6, Pallas kernels, call(): pl.pallas_call(kernel, name=name, out_shape=[jax.ShapeDtypeStruct(s, d) f...  11.1 us
    ppermute x2, starting transfers between devices, swap_cores(): return lax.ppermute(x, 'core', [(0, 1), (1, 0)])  3.47 us
  transfers between devices with their start and end apart: 2, of which 1 were waited for; matrix products, arithmetic and copies ran while one was open for 0% of the time, Pallas kernels for 2%

profile of v6, /device:TPU:1, one launch (start us, length us, event | category | flops | bytes accessed | tf_op | source)
XLA Modules:
  0.0 72.1 jit_solution(11621672957263147943)
XLA Ops:
  0.6 1.3 %pack.1 = (bf16[2048,128]{1,0:T(8,128)(2,1)S(1)}, s32[32]{0:T(128)S(1)}) custom-call(bf16[512,128]{1,0:T(8,128)(2,1)} %bitcast.16, bf16[512,128]{1,0:T(8,128)(2,1)} %bitcast.17, s32[32]{0:T(128)} %m_hbm.1), custom_call_target="tpu_custom_call" | custom-call | tf_op jit(solution)/shard_map/pack/pallas_call | solution.py:366
  1.9 0.0 copy-start
  1.9 0.0 copy-start.1
  2.0 0.0 copy-start.3
  2.0 31.7 %all_to_all.10 = bf16[128,16,128]{2,1,0:T(8,128)(2,1)S(1)} all-to-all(bf16[128,16,128]{2,1,0:T(8,128)(2,1)S(1)} %bitcast.13), channel_id=1, replica_groups=mesh['row'=4,'core'=2,'y'=4,'x'=4,'z'=2] {'z','row','y','x'}, dimensions={0} | all-to-all | bytes 1048576 | tf_op jit(solution)/shard_map/all_to_all | solution.py:412
  33.7 0.0 copy-done
  33.7 0.0 copy-done.1
  33.7 0.0 copy-done.3
  33.7 0.0 copy-start.5
  33.7 0.0 copy-start.6
  33.7 3.7 %synth.1 = (bf16[256,768]{1,0:T(8,128)(2,1)S(1)}, bf16[256,768]{1,0:T(8,128)(2,1)S(1)}) custom-call(s32[32]{0:T(128)S(1)} %get-tuple-element.13.m_ref, bf16[2048,128]{1,0:T(8,128)(2,1)S(1)} %bitcast.10, bf16[2,256,256]{2,1,0:T(8,128)(2,1)S(1)} %copy-done.3, f32[6,32,128]{2,1,0:T(8,128)S(1)} %copy-done, bf16[3,256,256]{2,1,0:T(8,128)(2,1)S(1)} %copy-done.1), custom_call_target="tpu_custom_call" | custom-call | tf_op jit(solution)/shard_map/synth/pallas_call | solution.py:366
  37.5 3.0 %collective-permute-start = (bf16[256,768]{1,0:T(8,128)(2,1)S(1)}, bf16[256,768]{1,0:T(8,128)(2,1)S(1)}, u32[]{:S(2)}, u32[]{:S(2)}) collective-permute-start(bf16[256,768]{1,0:T(8,128)(2,1)S(1)} %get-tuple-element.16), channel_id=1, source_target_pairs={{0,32},{32,0},{1,33},{33,1},{2,34},{34,2},{3,35},{35,3},{4,36},{36... | collective-permute-start | bytes 1179656 | tf_op jit(solution)/shard_map/ppermute | solution.py:33
  40.5 0.0 copy-done.5
  40.5 0.0 copy-done.6
  40.5 1.3 %tables.1 = (bf16[2,64,256]{2,1,0:T(8,128)(2,1)S(1)}, bf16[2,256,64]{2,1,0:T(8,128)(2,1)S(1)}, f32[8,128]{1,0:T(8,128)S(1)}) custom-call(s32[32]{0:T(128)S(1)} %get-tuple-element.13.m_ref, s32[32,128]{1,0:T(8,128)S(1)} %bitcast.14, f32[32,128]{1,0:T(8,128)S(1)} %bitcast.15), custom_call_target="tpu_custom_call" | custom-call | tf_op jit(solution)/shard_map/tables/pallas_call | solution.py:366
  41.9 0.0 collective-permute-done.refs_1_
  41.9 0.0 copy-start.2
  41.9 0.0 copy-start.4
  41.9 2.0 %pixel.1 = (bf16[256,256]{1,0:T(8,128)(2,1)S(1)}, bf16[256,256]{1,0:T(8,128)(2,1)S(1)}) custom-call(bf16[256,768]{1,0:T(8,128)(2,1)S(1)} %get-tuple-element.15.refs_0_, bf16[256,768]{1,0:T(8,128)(2,1)S(1)} %collective-permute-done.refs_1_, bf16[2,64,256]{2,1,0:T(8,128)(2,1)S(1)} %get-tuple-element.17.refs_2_, ...), custom_call_target="tpu_custom_call" | custom-call | tf_op jit(solution)/shard_map/pixel/pallas_call | solution.py:366
  43.9 0.4 collective-permute-start.1
  44.3 1.0 %collective-permute-done.1.refs_1_ = bf16[256,256]{1,0:T(8,128)(2,1)S(1)} collective-permute-done((bf16[256,256]{1,0:T(8,128)(2,1)S(1)}, bf16[256,256]{1,0:T(8,128)(2,1)S(1)}, u32[]{:S(2)}, u32[]{:S(2)}) %collective-permute-start.1) | collective-permute-done | bytes 131104 | tf_op jit(solution)/shard_map/ppermute | solution.py:33
  45.3 0.0 copy-done.2
  45.3 0.0 copy-done.4
  45.3 1.8 %adjoint.1 = bf16[2048,128]{1,0:T(8,128)(2,1)S(1)} custom-call(s32[32]{0:T(128)S(1)} %get-tuple-element.13.m_ref, bf16[256,256]{1,0:T(8,128)(2,1)S(1)} %get-tuple-element.20.refs_0_, bf16[256,256]{1,0:T(8,128)(2,1)S(1)} %collective-permute-done.1.refs_1_, f32[6,32,128]{2,1,0:T(8,128)S(1)} %copy-done, bf16[256,512]{1,0:T(8,128)(2,1)S(1)} %copy-done.2, ...), custom_call_target="tpu_custom_call" | custom-call | tf_op jit(solution)/shard_map/adjoint/pallas_call | solution.py:366
  47.1 24.0 %all_to_all.11 = bf16[128,16,128]{2,1,0:T(8,128)(2,1)S(1)} all-to-all(bf16[128,16,128]{2,1,0:T(8,128)(2,1)S(1)} %bitcast.11), channel_id=1, replica_groups=mesh['row'=4,'core'=2,'y'=4,'x'=4,'z'=2] {'z','row','y','x'}, dimensions={0} | all-to-all | bytes 1048576 | tf_op jit(solution)/shard_map/all_to_all | solution.py:434
  71.1 1.0 %unpack.1 = (bf16[512,128]{1,0:T(8,128)(2,1)}, bf16[512,128]{1,0:T(8,128)(2,1)}) custom-call(bf16[2048,128]{1,0:T(8,128)(2,1)S(1)} %bitcast.12), custom_call_target="tpu_custom_call" | custom-call | tf_op jit(solution)/shard_map/unpack/pallas_call | solution.py:366
Async XLA Ops:
  1.9 31.8 %copy-start = (f32[6,32,128]{2,1,0:T(8,128)S(1)}, f32[6,32,128]{2,1,0:T(8,128)}, u32[]{:S(2)}) copy-start(f32[6,32,128]{2,1,0:T(8,128)} %constant.11.clone.tw_ref.refs_2_) | copy-start | bytes 294916
  1.9 31.8 %copy-start.1 = (bf16[3,256,256]{2,1,0:T(8,128)(2,1)S(1)}, bf16[3,256,256]{2,1,0:T(8,128)(2,1)}, u32[]{:S(2)}) copy-start(bf16[3,256,256]{2,1,0:T(8,128)(2,1)} %constant.12.clone.w2_ref) | copy-start | bytes 1179652
  2.0 31.8 %copy-start.3 = (bf16[2,256,256]{2,1,0:T(8,128)(2,1)S(1)}, bf16[2,256,256]{2,1,0:T(8,128)(2,1)}, u32[]{:S(2)}) copy-start(bf16[2,256,256]{2,1,0:T(8,128)(2,1)} %constant.10.clone.w1_ref) | copy-start | bytes 786436
  33.7 6.8 %copy-start.5 = (s32[4096]{0:T(1024)S(1)}, s32[4096]{0:T(1024)}, u32[]{:S(2)}) copy-start(s32[4096]{0:T(1024)} %param.13) | copy-start | bytes 49156
  33.7 6.8 %copy-start.6 = (f32[4096]{0:T(1024)S(1)}, f32[4096]{0:T(1024)}, u32[]{:S(2)}) copy-start(f32[4096]{0:T(1024)} %param.14) | copy-start | bytes 49156
  37.5 4.4 %collective-permute-start = (bf16[256,768]{1,0:T(8,128)(2,1)S(1)}, bf16[256,768]{1,0:T(8,128)(2,1)S(1)}, u32[]{:S(2)}, u32[]{:S(2)}) collective-permute-start(bf16[256,768]{1,0:T(8,128)(2,1)S(1)} %get-tuple-element.16), channel_id=1, source_target_pairs={{0,32},{32,0},{1,33},{33,1},{2,34},{34,2},{3,35},{35,3},{4,36},{36... | collective-permute-start | bytes 1179656 | tf_op jit(solution)/shard_map/ppermute | solution.py:33
  41.9 3.4 %copy-start.2 = (bf16[256,512]{1,0:T(8,128)(2,1)S(1)}, bf16[256,512]{1,0:T(8,128)(2,1)}, u32[]{:S(2)}) copy-start(bf16[256,512]{1,0:T(8,128)(2,1)} %constant.13.clone.refs_3_) | copy-start | bytes 786436
  41.9 3.4 %copy-start.4 = (bf16[2,64,192]{2,1,0:T(8,128)(2,1)S(1)}, bf16[2,64,192]{2,1,0:T(8,128)(2,1)}, u32[]{:S(2)}) copy-start(bf16[2,64,192]{2,1,0:T(8,128)(2,1)} %constant.14.clone.refs_4_) | copy-start | bytes 147460
  43.9 1.4 %collective-permute-start.1 = (bf16[256,256]{1,0:T(8,128)(2,1)S(1)}, bf16[256,256]{1,0:T(8,128)(2,1)S(1)}, u32[]{:S(2)}, u32[]{:S(2)}) collective-permute-start(bf16[256,256]{1,0:T(8,128)(2,1)S(1)} %get-tuple-element.21), channel_id=1, source_target_pairs={{0,32},{32,0},{1,33},{33,1},{2,34},{34,2},{3,35},{35,3},{4,36},{36... | collective-permute-start | bytes 393224 | tf_op jit(solution)/shard_map/ppermute | solution.py:33

commit v7 on v6

--- a/solution.py
+++ b/solution.py
@@ -239,23 +239,28 @@
                     rows[1].append(
                         jnp.concatenate([-(vr * ti + vi * tr), vr * tr - vi * ti], axis=1)
                     )
-            row = jnp.concatenate(rows[0] + rows[1], axis=0)
-            hi = row.astype(BF16)
-            lo = (row - hi.astype(F32)).astype(BF16)
-            y = jnp.dot(jnp.concatenate([hi, lo], axis=0), w2_ref[k], preferred_element_type=F32)
-            y = (y[256:, :128] + y[:256, 128:]) + y[:256, :128]
             der_map, cos_map = ((0, 2), (1, 3), (4, 5))[k]
-            for i in range(4):
-                o = group * 4 + i
-                sign = phases[i][2]
-                factor = m_ref[order_slot(o, core)].astype(F32) * (1.0 / LMAX)
-                for ri in range(2):
-                    at = pl.ds(o * 2 + ri, 16, stride=32)
-                    scale = -factor if ri == 0 else factor
-                    c = (i * 2 + 1 - ri) * 16
-                    d = 128 + (i * 2 + ri) * 16
-                    os[cos_map, at, :] = y[c : c + 16] * (half_sign(128, sign) * scale)
-                    os[der_map, at, :] = y[d : d + 16] * half_sign(128, -sign)
+            for kind in range(2):
+                row = jnp.concatenate(rows[kind], axis=0)
+                hi = row.astype(BF16)
+                lo = (row - hi.astype(F32)).astype(BF16)
+                y = jnp.dot(
+                    jnp.concatenate([hi, lo], axis=0), w2_ref[k], preferred_element_type=F32
+                )
+                y = (y[128:, :128] + y[:128, 128:]) + y[:128, :128]
+                for i in range(4):
+                    o = group * 4 + i
+                    sign = phases[i][2]
+                    factor = m_ref[order_slot(o, core)].astype(F32) * (1.0 / LMAX)
+                    for ri in range(2):
+                        at = pl.ds(o * 2 + ri, 16, stride=32)
+                        if kind == 0:
+                            scale = -factor if ri == 0 else factor
+                            c = (i * 2 + 1 - ri) * 16
+                            os[cos_map, at, :] = y[c : c + 16] * (half_sign(128, sign) * scale)
+                        else:
+                            d = (i * 2 + ri) * 16
+                            os[der_map, at, :] = y[d : d + 16] * half_sign(128, -sign)
     for k in range(6):
         lanes = slice(k * 128, (k + 1) * 128)
         send_ref[:, lanes] = os[k, pl.ds((1 - core) * 256, 256), :].astype(BF16)

time: 73.5 us -> 73.5 us (level)
  no operation moved by 1% of the time
where the time goes in v7:
time: 73.5 us; the launch traced here: 72.1 us
  blocking collectives  55.7 us (76%)
  Pallas kernels  11.1 us (15%)
  starting transfers between devices  3.45 us (5%)
  waiting for transfers between devices  1.03 us (1%)
  between operations  0.74 us (1%)
    all_to_all x1, blocking collectives, body(): got = lax.all_to_all(sent.reshape(128, 16, 128), CHIPS, 0, 0, tiled=True)  31.7 us
    all_to_all x1, blocking collectives, body(): home = lax.all_to_all(sums.reshape(128, 16, 128), CHIPS, 0, 0, tiled=True)  24 us
    pallas_call x6, Pallas kernels, call(): pl.pallas_call(kernel, name=name, out_shape=[jax.ShapeDtypeStruct(s, d) f...  11.1 us
    ppermute x2, starting transfers between devices, swap_cores(): return lax.ppermute(x, 'core', [(0, 1), (1, 0)])  3.45 us
  transfers between devices with their start and end apart: 2, of which 1 were waited for; matrix products, arithmetic and copies ran while one was open for 0% of the time, Pallas kernels for 2%

profile of v7, /device:TPU:1, one launch (start us, length us, event | category | flops | bytes accessed | tf_op | source)
XLA Modules:
  0.0 72.1 jit_solution(12592759804346201890)
XLA Ops:
  0.6 1.3 %pack.1 = (bf16[2048,128]{1,0:T(8,128)(2,1)S(1)}, s32[32]{0:T(128)S(1)}) custom-call(bf16[512,128]{1,0:T(8,128)(2,1)} %bitcast.16, bf16[512,128]{1,0:T(8,128)(2,1)} %bitcast.17, s32[32]{0:T(128)} %m_hbm.1), custom_call_target="tpu_custom_call" | custom-call | tf_op jit(solution)/shard_map/pack/pallas_call | solution.py:371
  1.9 0.0 copy-start
  1.9 0.0 copy-start.1
  2.0 0.0 copy-start.3
  2.0 31.7 %all_to_all.10 = bf16[128,16,128]{2,1,0:T(8,128)(2,1)S(1)} all-to-all(bf16[128,16,128]{2,1,0:T(8,128)(2,1)S(1)} %bitcast.13), channel_id=1, replica_groups=mesh['row'=4,'core'=2,'y'=4,'x'=4,'z'=2] {'z','row','y','x'}, dimensions={0} | all-to-all | bytes 1048576 | tf_op jit(solution)/shard_map/all_to_all | solution.py:417
  33.7 0.0 copy-done
  33.7 0.0 copy-done.1
  33.7 0.0 copy-done.3
  33.7 0.0 copy-start.5
  33.7 0.0 copy-start.6
  33.7 3.7 %synth.1 = (bf16[256,768]{1,0:T(8,128)(2,1)S(1)}, bf16[256,768]{1,0:T(8,128)(2,1)S(1)}) custom-call(s32[32]{0:T(128)S(1)} %get-tuple-element.13.m_ref, bf16[2048,128]{1,0:T(8,128)(2,1)S(1)} %bitcast.10, bf16[2,256,256]{2,1,0:T(8,128)(2,1)S(1)} %copy-done.3, f32[6,32,128]{2,1,0:T(8,128)S(1)} %copy-done, bf16[3,256,256]{2,1,0:T(8,128)(2,1)S(1)} %copy-done.1), custom_call_target="tpu_custom_call" | custom-call | tf_op jit(solution)/shard_map/synth/pallas_call | solution.py:371
  37.5 3.0 %collective-permute-start = (bf16[256,768]{1,0:T(8,128)(2,1)S(1)}, bf16[256,768]{1,0:T(8,128)(2,1)S(1)}, u32[]{:S(2)}, u32[]{:S(2)}) collective-permute-start(bf16[256,768]{1,0:T(8,128)(2,1)S(1)} %get-tuple-element.16), channel_id=1, source_target_pairs={{0,32},{32,0},{1,33},{33,1},{2,34},{34,2},{3,35},{35,3},{4,36},{36... | collective-permute-start | bytes 1179656 | tf_op jit(solution)/shard_map/ppermute | solution.py:33
  40.5 0.0 copy-done.5
  40.5 0.0 copy-done.6
  40.5 1.4 %tables.1 = (bf16[2,64,256]{2,1,0:T(8,128)(2,1)S(1)}, bf16[2,256,64]{2,1,0:T(8,128)(2,1)S(1)}, f32[8,128]{1,0:T(8,128)S(1)}) custom-call(s32[32]{0:T(128)S(1)} %get-tuple-element.13.m_ref, s32[32,128]{1,0:T(8,128)S(1)} %bitcast.14, f32[32,128]{1,0:T(8,128)S(1)} %bitcast.15), custom_call_target="tpu_custom_call" | custom-call | tf_op jit(solution)/shard_map/tables/pallas_call | solution.py:371
  41.9 0.0 collective-permute-done.refs_1_
  41.9 0.0 copy-start.2
  41.9 0.0 copy-start.4
  41.9 2.0 %pixel.1 = (bf16[256,256]{1,0:T(8,128)(2,1)S(1)}, bf16[256,256]{1,0:T(8,128)(2,1)S(1)}) custom-call(bf16[256,768]{1,0:T(8,128)(2,1)S(1)} %get-tuple-element.15.refs_0_, bf16[256,768]{1,0:T(8,128)(2,1)S(1)} %collective-permute-done.refs_1_, bf16[2,64,256]{2,1,0:T(8,128)(2,1)S(1)} %get-tuple-element.17.refs_2_, ...), custom_call_target="tpu_custom_call" | custom-call | tf_op jit(solution)/shard_map/pixel/pallas_call | solution.py:371
  43.9 0.4 collective-permute-start.1
  44.3 1.0 %collective-permute-done.1.refs_1_ = bf16[256,256]{1,0:T(8,128)(2,1)S(1)} collective-permute-done((bf16[256,256]{1,0:T(8,128)(2,1)S(1)}, bf16[256,256]{1,0:T(8,128)(2,1)S(1)}, u32[]{:S(2)}, u32[]{:S(2)}) %collective-permute-start.1) | collective-permute-done | bytes 131104 | tf_op jit(solution)/shard_map/ppermute | solution.py:33
  45.3 0.0 copy-done.2
  45.3 0.0 copy-done.4
  45.3 1.8 %adjoint.1 = bf16[2048,128]{1,0:T(8,128)(2,1)S(1)} custom-call(s32[32]{0:T(128)S(1)} %get-tuple-element.13.m_ref, bf16[256,256]{1,0:T(8,128)(2,1)S(1)} %get-tuple-element.20.refs_0_, bf16[256,256]{1,0:T(8,128)(2,1)S(1)} %collective-permute-done.1.refs_1_, f32[6,32,128]{2,1,0:T(8,128)S(1)} %copy-done, bf16[256,512]{1,0:T(8,128)(2,1)S(1)} %copy-done.2, ...), custom_call_target="tpu_custom_call" | custom-call | tf_op jit(solution)/shard_map/adjoint/pallas_call | solution.py:371
  47.1 24.0 %all_to_all.11 = bf16[128,16,128]{2,1,0:T(8,128)(2,1)S(1)} all-to-all(bf16[128,16,128]{2,1,0:T(8,128)(2,1)S(1)} %bitcast.11), channel_id=1, replica_groups=mesh['row'=4,'core'=2,'y'=4,'x'=4,'z'=2] {'z','row','y','x'}, dimensions={0} | all-to-all | bytes 1048576 | tf_op jit(solution)/shard_map/all_to_all | solution.py:439
  71.1 1.0 %unpack.1 = (bf16[512,128]{1,0:T(8,128)(2,1)}, bf16[512,128]{1,0:T(8,128)(2,1)}) custom-call(bf16[2048,128]{1,0:T(8,128)(2,1)S(1)} %bitcast.12), custom_call_target="tpu_custom_call" | custom-call | tf_op jit(solution)/shard_map/unpack/pallas_call | solution.py:371
Async XLA Ops:
  1.9 31.8 %copy-start = (f32[6,32,128]{2,1,0:T(8,128)S(1)}, f32[6,32,128]{2,1,0:T(8,128)}, u32[]{:S(2)}) copy-start(f32[6,32,128]{2,1,0:T(8,128)} %constant.11.clone.tw_ref.refs_2_) | copy-start | bytes 294916
  1.9 31.8 %copy-start.1 = (bf16[3,256,256]{2,1,0:T(8,128)(2,1)S(1)}, bf16[3,256,256]{2,1,0:T(8,128)(2,1)}, u32[]{:S(2)}) copy-start(bf16[3,256,256]{2,1,0:T(8,128)(2,1)} %constant.12.clone.w2_ref) | copy-start | bytes 1179652
  2.0 31.8 %copy-start.3 = (bf16[2,256,256]{2,1,0:T(8,128)(2,1)S(1)}, bf16[2,256,256]{2,1,0:T(8,128)(2,1)}, u32[]{:S(2)}) copy-start(bf16[2,256,256]{2,1,0:T(8,128)(2,1)} %constant.10.clone.w1_ref) | copy-start | bytes 786436
  33.7 6.8 %copy-start.5 = (s32[4096]{0:T(1024)S(1)}, s32[4096]{0:T(1024)}, u32[]{:S(2)}) copy-start(s32[4096]{0:T(1024)} %param.13) | copy-start | bytes 49156
  33.7 6.8 %copy-start.6 = (f32[4096]{0:T(1024)S(1)}, f32[4096]{0:T(1024)}, u32[]{:S(2)}) copy-start(f32[4096]{0:T(1024)} %param.14) | copy-start | bytes 49156
  37.5 4.4 %collective-permute-start = (bf16[256,768]{1,0:T(8,128)(2,1)S(1)}, bf16[256,768]{1,0:T(8,128)(2,1)S(1)}, u32[]{:S(2)}, u32[]{:S(2)}) collective-permute-start(bf16[256,768]{1,0:T(8,128)(2,1)S(1)} %get-tuple-element.16), channel_id=1, source_target_pairs={{0,32},{32,0},{1,33},{33,1},{2,34},{34,2},{3,35},{35,3},{4,36},{36... | collective-permute-start | bytes 1179656 | tf_op jit(solution)/shard_map/ppermute | solution.py:33
  41.9 3.4 %copy-start.2 = (bf16[256,512]{1,0:T(8,128)(2,1)S(1)}, bf16[256,512]{1,0:T(8,128)(2,1)}, u32[]{:S(2)}) copy-start(bf16[256,512]{1,0:T(8,128)(2,1)} %constant.13.clone.refs_3_) | copy-start | bytes 786436
  41.9 3.4 %copy-start.4 = (bf16[2,64,192]{2,1,0:T(8,128)(2,1)S(1)}, bf16[2,64,192]{2,1,0:T(8,128)(2,1)}, u32[]{:S(2)}) copy-start(bf16[2,64,192]{2,1,0:T(8,128)(2,1)} %constant.14.clone.refs_4_) | copy-start | bytes 147460
  43.9 1.4 %collective-permute-start.1 = (bf16[256,256]{1,0:T(8,128)(2,1)S(1)}, bf16[256,256]{1,0:T(8,128)(2,1)S(1)}, u32[]{:S(2)}, u32[]{:S(2)}) collective-permute-start(bf16[256,256]{1,0:T(8,128)(2,1)S(1)} %get-tuple-element.21), channel_id=1, source_target_pairs={{0,32},{32,0},{1,33},{33,1},{2,34},{34,2},{3,35},{35,3},{4,36},{36... | collective-permute-start | bytes 393224 | tf_op jit(solution)/shard_map/ppermute | solution.py:33

commit v8 on v7

--- a/solution.py
+++ b/solution.py
@@ -188,16 +188,21 @@
     copies[2].wait()
 
 
-def unpack_kernel(in_ref, g_ref, c_ref, src, dst):
+def unpack_kernel(in_ref, g_hbm, c_hbm, src, dst, out, sems):
     src[...] = in_ref[:1024].astype(F32) + in_ref[1024:].astype(F32)
-    for part, ref in enumerate((g_ref, c_ref)):
+    copies = []
+    for part, hbm in enumerate((g_hbm, c_hbm)):
         for o in range(ORD_DEV):
             rows = []
             for ri in range(2):
                 j = o * 4 + part * 2 + ri
                 rows.append(src[pl.ds(j, 64, stride=16), :])
             dst[part, pl.ds(o, 128, stride=ORD_DEV), :] = jnp.concatenate(rows, axis=0).T
-        ref[...] = dst[part].astype(BF16)
+        out[part] = dst[part].astype(BF16)
+        copies.append(pltpu.make_async_copy(out.at[part], hbm, sems.at[part]))
+        copies[part].start()
+    for copy in copies:
+        copy.wait()
 
 
 def synth_kernel(m_ref, x_ref, w1_ref, tw_ref, w2_ref, *refs):
@@ -365,7 +370,7 @@
 HBM = pl.BlockSpec(memory_space=pltpu.HBM)
 
 
-def call(kernel, name, inputs, outs, scratch, spaces=None):
+def call(kernel, name, inputs, outs, scratch, spaces=None, to=None):
     specs = spaces or [SMEM if x.ndim == 1 else VMEM for x in inputs]
     single = len(outs) == 1
     out = pl.pallas_call(
@@ -373,7 +378,7 @@
         name=name,
         out_shape=[jax.ShapeDtypeStruct(s, d) for s, d in outs],
         in_specs=specs,
-        out_specs=[VMEM for o in outs],
+        out_specs=[to or VMEM for o in outs],
         scratch_shapes=scratch,
         compiler_params=pltpu.CompilerParams(vmem_limit_bytes=48 << 20),
     )(*inputs)
@@ -442,7 +447,13 @@
         "unpack",
         [home.reshape(2048, 128)],
         [((512, 128), BF16), ((512, 128), BF16)],
-        [scratch((1024, 128)), scratch((2, 512, 128))],
+        [
+            scratch((1024, 128)),
+            scratch((2, 512, 128)),
+            scratch((2, 512, 128), BF16),
+            pltpu.SemaphoreType.DMA((2,)),
+        ],
+        to=HBM,
     )
     return grad.reshape(128, ORD_DEV, 128), curl.reshape(128, ORD_DEV, 128)
 

time: 73.5 us -> 73.5 us (level)
  no operation moved by 1% of the time
where the time goes in v8:
time: 73.5 us; the launch traced here: 72.1 us
  blocking collectives  55.7 us (76%)
  Pallas kernels  11.1 us (15%)
  starting transfers between devices  3.45 us (5%)
  waiting for transfers between devices  1.03 us (1%)
  between operations  0.74 us (1%)
    all_to_all x1, blocking collectives, body(): got = lax.all_to_all(sent.reshape(128, 16, 128), CHIPS, 0, 0, tiled=True)  31.7 us
    all_to_all x1, blocking collectives, body(): home = lax.all_to_all(sums.reshape(128, 16, 128), CHIPS, 0, 0, tiled=True)  24 us
    pallas_call x6, Pallas kernels, call(): pl.pallas_call(kernel, name=name, out_shape=[jax.ShapeDtypeStruct(s, d) f...  11.1 us
    ppermute x2, starting transfers between devices, swap_cores(): return lax.ppermute(x, 'core', [(0, 1), (1, 0)])  3.45 us
  transfers between devices with their start and end apart: 2, of which 1 were waited for; matrix products, arithmetic and copies ran while one was open for 0% of the time, Pallas kernels for 2%

profile of v8, /device:TPU:1, one launch (start us, length us, event | category | flops | bytes accessed | tf_op | source)
XLA Modules:
  0.0 72.1 jit_solution(1506424677610477777)
XLA Ops:
  0.6 1.3 %pack.1 = (bf16[2048,128]{1,0:T(8,128)(2,1)S(1)}, s32[32]{0:T(128)S(1)}) custom-call(bf16[512,128]{1,0:T(8,128)(2,1)} %bitcast.16, bf16[512,128]{1,0:T(8,128)(2,1)} %bitcast.17, s32[32]{0:T(128)} %m_hbm.1), custom_call_target="tpu_custom_call" | custom-call | tf_op jit(solution)/shard_map/pack/pallas_call | solution.py:376
  1.9 0.0 copy-start
  1.9 0.0 copy-start.1
  2.0 0.0 copy-start.3
  2.0 31.7 %all_to_all.10 = bf16[128,16,128]{2,1,0:T(8,128)(2,1)S(1)} all-to-all(bf16[128,16,128]{2,1,0:T(8,128)(2,1)S(1)} %bitcast.13), channel_id=1, replica_groups=mesh['row'=4,'core'=2,'y'=4,'x'=4,'z'=2] {'z','row','y','x'}, dimensions={0} | all-to-all | bytes 1048576 | tf_op jit(solution)/shard_map/all_to_all | solution.py:422
  33.7 0.0 copy-done
  33.7 0.0 copy-done.1
  33.7 0.0 copy-done.3
  33.7 0.0 copy-start.5
  33.7 0.0 copy-start.6
  33.7 3.7 %synth.1 = (bf16[256,768]{1,0:T(8,128)(2,1)S(1)}, bf16[256,768]{1,0:T(8,128)(2,1)S(1)}) custom-call(s32[32]{0:T(128)S(1)} %get-tuple-element.13.m_ref, bf16[2048,128]{1,0:T(8,128)(2,1)S(1)} %bitcast.10, bf16[2,256,256]{2,1,0:T(8,128)(2,1)S(1)} %copy-done.3, f32[6,32,128]{2,1,0:T(8,128)S(1)} %copy-done, bf16[3,256,256]{2,1,0:T(8,128)(2,1)S(1)} %copy-done.1), custom_call_target="tpu_custom_call" | custom-call | tf_op jit(solution)/shard_map/synth/pallas_call | solution.py:376
  37.5 3.0 %collective-permute-start = (bf16[256,768]{1,0:T(8,128)(2,1)S(1)}, bf16[256,768]{1,0:T(8,128)(2,1)S(1)}, u32[]{:S(2)}, u32[]{:S(2)}) collective-permute-start(bf16[256,768]{1,0:T(8,128)(2,1)S(1)} %get-tuple-element.16), channel_id=1, source_target_pairs={{0,32},{32,0},{1,33},{33,1},{2,34},{34,2},{3,35},{35,3},{4,36},{36... | collective-permute-start | bytes 1179656 | tf_op jit(solution)/shard_map/ppermute | solution.py:33
  40.5 0.0 copy-done.5
  40.5 0.0 copy-done.6
  40.5 1.4 %tables.1 = (bf16[2,64,256]{2,1,0:T(8,128)(2,1)S(1)}, bf16[2,256,64]{2,1,0:T(8,128)(2,1)S(1)}, f32[8,128]{1,0:T(8,128)S(1)}) custom-call(s32[32]{0:T(128)S(1)} %get-tuple-element.13.m_ref, s32[32,128]{1,0:T(8,128)S(1)} %bitcast.14, f32[32,128]{1,0:T(8,128)S(1)} %bitcast.15), custom_call_target="tpu_custom_call" | custom-call | tf_op jit(solution)/shard_map/tables/pallas_call | solution.py:376
  41.9 0.0 collective-permute-done.refs_1_
  41.9 0.0 copy-start.2
  41.9 0.0 copy-start.4
  41.9 2.0 %pixel.1 = (bf16[256,256]{1,0:T(8,128)(2,1)S(1)}, bf16[256,256]{1,0:T(8,128)(2,1)S(1)}) custom-call(bf16[256,768]{1,0:T(8,128)(2,1)S(1)} %get-tuple-element.15.refs_0_, bf16[256,768]{1,0:T(8,128)(2,1)S(1)} %collective-permute-done.refs_1_, bf16[2,64,256]{2,1,0:T(8,128)(2,1)S(1)} %get-tuple-element.17.refs_2_, ...), custom_call_target="tpu_custom_call" | custom-call | tf_op jit(solution)/shard_map/pixel/pallas_call | solution.py:376
  43.9 0.4 collective-permute-start.1
  44.3 1.0 %collective-permute-done.1.refs_1_ = bf16[256,256]{1,0:T(8,128)(2,1)S(1)} collective-permute-done((bf16[256,256]{1,0:T(8,128)(2,1)S(1)}, bf16[256,256]{1,0:T(8,128)(2,1)S(1)}, u32[]{:S(2)}, u32[]{:S(2)}) %collective-permute-start.1) | collective-permute-done | bytes 131104 | tf_op jit(solution)/shard_map/ppermute | solution.py:33
  45.3 0.0 copy-done.2
  45.3 0.0 copy-done.4
  45.3 1.8 %adjoint.1 = bf16[2048,128]{1,0:T(8,128)(2,1)S(1)} custom-call(s32[32]{0:T(128)S(1)} %get-tuple-element.13.m_ref, bf16[256,256]{1,0:T(8,128)(2,1)S(1)} %get-tuple-element.20.refs_0_, bf16[256,256]{1,0:T(8,128)(2,1)S(1)} %collective-permute-done.1.refs_1_, f32[6,32,128]{2,1,0:T(8,128)S(1)} %copy-done, bf16[256,512]{1,0:T(8,128)(2,1)S(1)} %copy-done.2, ...), custom_call_target="tpu_custom_call" | custom-call | tf_op jit(solution)/shard_map/adjoint/pallas_call | solution.py:376
  47.1 24.0 %all_to_all.11 = bf16[128,16,128]{2,1,0:T(8,128)(2,1)S(1)} all-to-all(bf16[128,16,128]{2,1,0:T(8,128)(2,1)S(1)} %bitcast.11), channel_id=1, replica_groups=mesh['row'=4,'core'=2,'y'=4,'x'=4,'z'=2] {'z','row','y','x'}, dimensions={0} | all-to-all | bytes 1048576 | tf_op jit(solution)/shard_map/all_to_all | solution.py:444
  71.1 1.0 %unpack.1 = (bf16[512,128]{1,0:T(8,128)(2,1)}, bf16[512,128]{1,0:T(8,128)(2,1)}) custom-call(bf16[2048,128]{1,0:T(8,128)(2,1)S(1)} %bitcast.12), custom_call_target="tpu_custom_call" | custom-call | tf_op jit(solution)/shard_map/unpack/pallas_call | solution.py:376
Async XLA Ops:
  1.9 31.8 %copy-start = (f32[6,32,128]{2,1,0:T(8,128)S(1)}, f32[6,32,128]{2,1,0:T(8,128)}, u32[]{:S(2)}) copy-start(f32[6,32,128]{2,1,0:T(8,128)} %constant.11.clone.tw_ref.refs_2_) | copy-start | bytes 294916
  1.9 31.8 %copy-start.1 = (bf16[3,256,256]{2,1,0:T(8,128)(2,1)S(1)}, bf16[3,256,256]{2,1,0:T(8,128)(2,1)}, u32[]{:S(2)}) copy-start(bf16[3,256,256]{2,1,0:T(8,128)(2,1)} %constant.12.clone.w2_ref) | copy-start | bytes 1179652
  2.0 31.8 %copy-start.3 = (bf16[2,256,256]{2,1,0:T(8,128)(2,1)S(1)}, bf16[2,256,256]{2,1,0:T(8,128)(2,1)}, u32[]{:S(2)}) copy-start(bf16[2,256,256]{2,1,0:T(8,128)(2,1)} %constant.10.clone.w1_ref) | copy-start | bytes 786436
  33.7 6.8 %copy-start.5 = (s32[4096]{0:T(1024)S(1)}, s32[4096]{0:T(1024)}, u32[]{:S(2)}) copy-start(s32[4096]{0:T(1024)} %param.13) | copy-start | bytes 49156
  33.7 6.8 %copy-start.6 = (f32[4096]{0:T(1024)S(1)}, f32[4096]{0:T(1024)}, u32[]{:S(2)}) copy-start(f32[4096]{0:T(1024)} %param.14) | copy-start | bytes 49156
  37.5 4.4 %collective-permute-start = (bf16[256,768]{1,0:T(8,128)(2,1)S(1)}, bf16[256,768]{1,0:T(8,128)(2,1)S(1)}, u32[]{:S(2)}, u32[]{:S(2)}) collective-permute-start(bf16[256,768]{1,0:T(8,128)(2,1)S(1)} %get-tuple-element.16), channel_id=1, source_target_pairs={{0,32},{32,0},{1,33},{33,1},{2,34},{34,2},{3,35},{35,3},{4,36},{36... | collective-permute-start | bytes 1179656 | tf_op jit(solution)/shard_map/ppermute | solution.py:33
  41.9 3.4 %copy-start.2 = (bf16[256,512]{1,0:T(8,128)(2,1)S(1)}, bf16[256,512]{1,0:T(8,128)(2,1)}, u32[]{:S(2)}) copy-start(bf16[256,512]{1,0:T(8,128)(2,1)} %constant.13.clone.refs_3_) | copy-start | bytes 786436
  41.9 3.4 %copy-start.4 = (bf16[2,64,192]{2,1,0:T(8,128)(2,1)S(1)}, bf16[2,64,192]{2,1,0:T(8,128)(2,1)}, u32[]{:S(2)}) copy-start(bf16[2,64,192]{2,1,0:T(8,128)(2,1)} %constant.14.clone.refs_4_) | copy-start | bytes 147460
  43.9 1.4 %collective-permute-start.1 = (bf16[256,256]{1,0:T(8,128)(2,1)S(1)}, bf16[256,256]{1,0:T(8,128)(2,1)S(1)}, u32[]{:S(2)}, u32[]{:S(2)}) collective-permute-start(bf16[256,256]{1,0:T(8,128)(2,1)S(1)} %get-tuple-element.21), channel_id=1, source_target_pairs={{0,32},{32,0},{1,33},{33,1},{2,34},{34,2},{3,35},{35,3},{4,36},{36... | collective-permute-start | bytes 393224 | tf_op jit(solution)/shard_map/ppermute | solution.py:33
